TPU v7x, 256 devices: a whole 4x4x8 slice. The times are simulated.
256 devices in a mesh: elem: 8 (over z), tm: 32 (over y, x, core).
Axes of the slice: x: 4, y: 4, z: 8, core: 2. Of those that a mesh axis runs over, the one named last changes fastest.
Arguments:
- samples: bfloat16 [24576, 2048], P('tm', 'elem'), may hold values from -160 to 160
- taps_weight: bfloat16 [16, 2048, 512], P(None, 'elem'), may hold values from -0.046875 to 0.046875
- retain: float32 [24576], P('tm')
Outputs:
- whitened: float32 [512, 24576], P('elem', 'tm')
All inputs are finite; a program needn't handle non-finite values.
Results may differ from a plain program's by a relative error of at most 0.0003.
Values may be sent and summed in bfloat16 or wider, within the bound.
No kernel may reach another device: no remote copies, remote signals or barrier semaphores. Data moves between devices by JAX's collectives and lax.ppermute only.
A program may use at most 192 MiB of HBM per device.

v0:
```python
import jax
import jax.numpy as jnp
from jax import lax
from jax.sharding import PartitionSpec as P

loading_level = 0.1


def shifted(array, axis, by):
    size = lax.axis_size(axis)
    pairs = [(i, i + by) for i in range(size) if 0 <= i + by < size]
    return lax.ppermute(array, axis, pairs)


def entering(value, axis, join, neutral):
    count, mine = (lax.axis_size(axis), lax.axis_index(axis))
    pieces = jax.tree.map(lambda part: lax.all_gather(part, axis), value)
    so_far = jax.tree.map(
        lambda part, zero: jnp.full_like(part, 0) + jnp.asarray(zero, part.dtype), value, neutral
    )

    def hop(position, so_far):
        longer = join(so_far, jax.tree.map(lambda part: part[position], pieces))
        return jax.tree.map(lambda new, old: jnp.where(position < mine, new, old), longer, so_far)

    return lax.fori_loop(0, count - 1, hop, so_far)


def combine_estimates(earlier, later):
    return (
        earlier[0] * later[2] + later[0],
        earlier[1] * later[2] + later[1],
        earlier[2] * later[2],
    )


def weighted_gram(beam_rows, row_weight):
    return jnp.dot((beam_rows * row_weight[:, None]).T, beam_rows, precision=lax.Precision.HIGHEST)


def local(samples, taps_weight, retain):
    row_count = samples.shape[0]
    elem_width = samples.shape[1]
    tap_count = taps_weight.shape[0]
    beam_count = taps_weight.shape[2]
    sample_history = shifted(samples[row_count - (tap_count - 1) :], "tm", 1)
    extended = jnp.concatenate([sample_history, samples], 0)
    windowed = jnp.concatenate(
        [
            extended[
                tap_count - 1 - filter_tap_index : tap_count - 1 - filter_tap_index + row_count
            ]
            for filter_tap_index in range(tap_count)
        ],
        1,
    )
    filters = taps_weight.reshape(tap_count * elem_width, beam_count)
    log_retain = jnp.log(retain)
    log_total = jnp.sum(log_retain)
    row_weight = jnp.exp(log_total - jnp.cumsum(log_retain))
    factor = jnp.exp(log_total)
    mass_aggregate = jnp.sum(row_weight)
    groups = lax.axis_size("elem")
    cluster_entry = lax.axis_index("elem")
    columns = beam_count // groups
    unit_matrix = jnp.eye(beam_count, dtype=jnp.float32)
    beam_rows = lax.psum(jnp.dot(windowed, filters, preferred_element_type=jnp.float32), "elem")
    gram_block = weighted_gram(beam_rows, row_weight)
    empty = (jnp.zeros_like(gram_block), jnp.zeros((), jnp.float32), jnp.ones((), jnp.float32))
    prefix = entering((gram_block, mass_aggregate, factor), "tm", combine_estimates, empty)
    gram_sum, count_sum, unused = combine_estimates(prefix, (gram_block, mass_aggregate, factor))
    covariance_estimate = gram_sum / count_sum + loading_level * unit_matrix
    lower_factor = jnp.linalg.cholesky(covariance_estimate)
    inverse_lower = jax.scipy.linalg.solve_triangular(lower_factor, unit_matrix, lower=True)
    local_rows = lax.dynamic_slice_in_dim(inverse_lower, cluster_entry * columns, columns, 0)
    return lax.dot_general(
        local_rows, beam_rows, (((1,), (1,)), ((), ())), precision=lax.Precision.HIGHEST
    )


def solution(mesh):
    placed = (P("tm", "elem"), P(None, "elem", None), P("tm"))
    return jax.shard_map(
        local, mesh=mesh, in_specs=placed, out_specs=P("elem", "tm"), check_vma=False
    )
```

profile of v0, /device:TPU:2, one launch (start us, length us, event | category | flops | bytes accessed | tf_op | source)
XLA Modules:
  0.0 555.1 jit_solution(1617515024383423267)
XLA Ops:
  7.3 2.2 collective-permute-start
  10.5 2.0 collective-permute-done
  14.7 1.1 fusion.21
  19.1 1.1 fusion.29
  21.1 4.6 fusion.74
  26.8 1.3 fusion.67
  28.1 79.3 %all-reduce.6.cloned.1.call-done = f32[768,512]{1,0:T(8,128)} async-done(((f32[768,512]{1,0:T(8,128)}), f32[768,512]{1,0:T(8,128)}) %all-reduce.6.cloned.1.call-update) | async-done | bytes 1572880 | tf_op jit(solution)/shard_map/psum | solution.py:67
  107.5 5.8 %fusion.1 = f32[512,512]{1,0:T(8,128)} fusion(f32[768,512]{1,0:T(8,128)} %all-reduce.6.cloned.1.call-done, f32[768]{0:T(1024)S(1)} %get-tuple-element.205), kind=kOutput, calls=%fused_computation.4 | convolution fusion | flops 2416312320 | bytes 2624512 | tf_op jit(solution)/shard_map/dot_general | solution.py:38
  114.6 1.3 dynamic-update-slice.24
  116.6 59.3 %all-reduce.3 = (f32[32]{0:T(128)S(1)}, f32[32]{0:T(128)S(1)}) all-reduce(f32[32]{0:T(128)S(1)} %dynamic-update-slice.23, f32[32]{0:T(128)S(1)} %dynamic-update-slice.24), channel_id=1, replica_groups=mesh['elem'=8,'tm'=32] {'tm'}, use_global_device_ids=true, to_apply=%add.1 | all-reduce | flops 64 | bytes 512
  177.7 1.6 copy.16
  179.3 52.1 %all-gather.3.cloned.1.call-done = f32[16384,512]{1,0:T(8,128)} async-done(((f32[512,512]{1,0:T(8,128)}), f32[16384,512]{1,0:T(8,128)}) %all-gather.3.cloned.1.call-update) | async-done | bytes 33554448 | tf_op jit(solution)/shard_map/all_gather | solution.py:17
  231.4 161.5 %while.18 = (s32[]{:T(128)}, f32[512,512]{1,0:T(8,128)S(1)}, f32[]{:T(128)}, s32[]{:T(128)}, f32[32]{0:T(128)S(1)}, /*index=5*/f32[32,512,512]{2,1,0:T(8,128)}, f32[32]{0:T(128)S(1)}, s32[]{:T(128)}, s32[]{:T(128)}) while((s32[]{:T(128)}, f32[512,512]{1,0:T(8,128)S(1)}, f32[]{:T(128)}, s32[]{:T(128)}, f32[32]{0:T(128)S(1)}, ...), condition=%wide.region_6.7_spmd.clone, body=%wide.region_5.6_spmd.clone.sunk | while | flops 1048583 | bytes 3145910 | solution.py:26
  232.1 2.4 fusion.87
  237.3 2.4 fusion.87
  242.5 2.4 fusion.87
  247.7 2.4 fusion.87
  252.9 2.4 fusion.87
  258.1 2.4 fusion.87
  263.3 2.4 fusion.87
  268.5 2.4 fusion.87
  273.7 2.4 fusion.87
  278.9 2.4 fusion.87
  284.1 2.4 fusion.87
  289.2 2.4 fusion.87
  294.4 2.4 fusion.87
  299.6 2.4 fusion.87
  304.8 2.4 fusion.87
  310.0 2.4 fusion.87
  315.2 2.4 fusion.87
  320.4 2.4 fusion.87
  325.6 2.4 fusion.87
  330.8 2.4 fusion.87
  336.0 2.4 fusion.87
  341.2 2.4 fusion.87
  346.4 2.4 fusion.87
  351.6 2.4 fusion.87
  356.8 2.4 fusion.87
  362.0 2.4 fusion.87
  367.2 2.4 fusion.87
  372.4 2.4 fusion.87
  377.5 2.4 fusion.87
  382.7 2.4 fusion.87
  387.9 2.4 fusion.87
  394.7 11.7 %cholesky.103 = f32[128,128]{1,0:T(8,128)S(1)} custom-call(f32[128,128]{1,0:T(8,128)S(1)} %cholesky.263), custom_call_target="Cholesky" | custom-call | tf_op jit(solution)/shard_map/jit(cholesky)/cholesky | solution.py:73
  406.5 9.8 %custom-call.31 = f32[1,128,128]{1,2,0:T(8,128)S(1)} custom-call(f32[1,128,128]{2,1,0:T(8,128)S(1)} %get-tuple-element.203), custom_call_target="InvertDiagBlocksLowerTriangular" | custom-call | tf_op jit(solution)/shard_map/jit(cholesky)/cholesky | solution.py:73
  417.0 11.7 %cholesky.215 = f32[128,128]{1,0:T(8,128)S(1)} custom-call(f32[128,128]{1,0:T(8,128)S(1)} %cholesky.267), custom_call_target="Cholesky" | custom-call | tf_op jit(solution)/shard_map/jit(cholesky)/cholesky | solution.py:73
  429.1 10.0 %custom-call.32 = f32[1,128,128]{1,2,0:T(8,128)S(1)} custom-call(f32[1,128,128]{2,1,0:T(8,128)S(1)} %get-tuple-element.201), custom_call_target="InvertDiagBlocksLowerTriangular" | custom-call | tf_op jit(solution)/shard_map/jit(cholesky)/cholesky | solution.py:73
  439.5 1.6 convolution_subtract_fusion.4
  441.2 11.7 %cholesky.236 = f32[128,128]{1,0:T(8,128)S(1)} custom-call(f32[128,128]{1,0:T(8,128)S(1)} %cholesky.272), custom_call_target="Cholesky" | custom-call | tf_op jit(solution)/shard_map/jit(cholesky)/cholesky | solution.py:73
  453.0 9.8 %custom-call.33 = f32[1,128,128]{1,2,0:T(8,128)S(1)} custom-call(f32[1,128,128]{2,1,0:T(8,128)S(1)} %get-tuple-element.199), custom_call_target="InvertDiagBlocksLowerTriangular" | custom-call | tf_op jit(solution)/shard_map/jit(cholesky)/cholesky | solution.py:73
  463.1 1.3 convolution_subtract_fusion.5
  464.5 11.9 %cholesky.253 = f32[128,128]{1,0:T(8,128)S(1)} custom-call(f32[128,128]{1,0:T(8,128)S(1)} %convolution_subtract_fusion.5), custom_call_target="Cholesky" | custom-call | tf_op jit(solution)/shard_map/jit(cholesky)/cholesky | solution.py:73
  481.1 1.1 select_select_fusion
  482.3 14.9 %while.17 = (s32[]{:T(128)}, f32[512,512]{0,1:T(8,128)}, s32[4,2]{0,1:T(2,128)S(1)}, f32[4,128,128]{2,1,0:T(8,128)}, s32[]{:T(128)}) while((s32[]{:T(128)}, f32[512,512]{0,1:T(8,128)}, s32[4,2]{0,1:T(2,128)S(1)}, f32[4,128,128]{2,1,0:T(8,128)}, s32[]{:T(128)}) %tuple.57), condition=%wide.while_cond, body=%wide.while_body.sunk | while | flops 2 | bytes 393829 | solution.py:74
  482.9 2.3 dynamic-slice.9
  486.7 2.3 dynamic-slice.9
  490.4 2.3 dynamic-slice.9
  494.1 2.3 dynamic-slice.9
  497.1 40.1 %custom-call.34 = f32[4,128,128]{1,2,0:T(8,128)S(1)} custom-call(f32[4,128,128]{2,1,0:T(8,128)} %get-tuple-element.139), custom_call_target="InvertDiagBlocksLowerTriangular" | custom-call | tf_op jit(solution)/shard_map/jit(_solve_triangular)/triangular_solve | solution.py:74
  538.3 1.6 convolution_subtract_fusion.1
  540.3 2.0 convolution_subtract_fusion
  542.8 2.5 convolution_subtract_fusion.2
  545.7 2.2 fusion.53
  (156 shorter events, 66.8 us)
Async XLA Ops:
  6.5 13.7 %copy-start = (bf16[768,256]{1,0:T(8,128)(2,1)S(1)}, bf16[768,256]{1,0:T(8,128)(2,1)}, u32[]{:S(2)}) copy-start(bf16[768,256]{1,0:T(8,128)(2,1)} %param.5) | copy-start | bytes 1179652
  6.5 100.9 %all-reduce.6.cloned.1.call-start = ((), (), s32[]{:S(2)}) async-start(), calls=%async_computation | async-start | bytes 3145728 | tf_op jit(solution)/shard_map/psum | solution.py:67
  7.3 13.7 %copy-start.4 = (bf16[16,256,512]{2,1,0:T(8,128)(2,1)S(1)}, bf16[16,256,512]{2,1,0:T(8,128)(2,1)}, u32[]{:S(2)}) copy-start(bf16[16,256,512]{2,1,0:T(8,128)(2,1)} %param.6) | copy-start | bytes 12582916
  7.3 5.2 collective-permute-start
  21.0 4.7 copy-start.3
  25.6 88.4 %copy-start.5 = (u32[256]{0:T(256)S(1)}, u32[256]{0:T(256)}, u32[]{:S(2)}) copy-start(u32[256]{0:T(256)} %constant.208) | copy-start | bytes 3076
  25.6 205.8 %all-gather.3.cloned.1.call-start = ((), (), s32[]{:S(2)}) async-start(), calls=%async_computation.1 | async-start | bytes 34603008 | tf_op jit(solution)/shard_map/all_gather | solution.py:17
  394.7 34.4 %copy-start.2 = (f32[512,512]{1,0:T(8,128)}, f32[512,512]{1,0:T(8,128)S(1)}, u32[]{:S(2)}) copy-start(f32[512,512]{1,0:T(8,128)S(1)} %fusion.3) | copy-start | bytes 3145732
  439.2 106.6 %copy-start.1 = (f32[768,512]{1,0:T(8,128)S(1)}, f32[768,512]{1,0:T(8,128)}, u32[]{:S(2)}) copy-start(f32[768,512]{1,0:T(8,128)} %all-reduce.6.cloned.1.call-done) | copy-start | bytes 4718596
Sparse Core Ops, SparseCore 0:
  25.8 81.6 all-reduce.5
  113.4 117.9 all-gather.2
where the time goes:
time: 566 us; the launch traced here: 555 us
  other arithmetic  209 us (37%)
  waiting for transfers between devices  134 us (24%)
  local copies, waits for them, and re-layouts  63.6 us (11%)
  blocking collectives  59.3 us (10%)
  loops' own time  44.4 us (8%)
  matrix products  25.2 us (4%)
  between operations  18 us (3%)
    psum x1, waiting for transfers between devices, local(): lax.psum(jnp.dot(windowed, filters, preferred_element_type=jnp.float32),...  79.3 us
    another operation x14, other arithmetic, local(): lower_factor = jnp.linalg.cholesky(covariance_estimate)  78.8 us
    select_n x31, other arithmetic, hop(): jnp.where(position < mine, new, old)  75.8 us
    unnamed x1, blocking collectives  59.3 us
    all_gather x1, waiting for transfers between devices, entering(): pieces = jax.tree.map(lambda part: lax.all_gather(part, axis), value)  52.1 us
    another operation x1, loops' own time, entering(): return lax.fori_loop(0, count - 1, hop, so_far)  44.4 us
    dynamic_slice x62, local copies, waits for them, and re-layouts, hop(): longer = join(so_far, jax.tree.map(lambda part: part[position], pieces))  41.3 us
    another operation x3, other arithmetic, local(): jax.scipy.linalg.solve_triangular(lower_factor, unit_matrix, lower=True)  41.2 us
  transfers between devices with their start and end apart: 3, of which 3 were waited for; matrix products, arithmetic and copies ran while one was open for 2% of the time, Pallas kernels for 0%

commit v1 on v0

v1 whole, which is shorter than its diff:
```python
import jax
import jax.numpy as jnp
from jax import lax
from jax.experimental import pallas as pl
from jax.experimental.pallas import tpu as pltpu
from jax.sharding import PartitionSpec as P

loading_level = 0.1
HI = lax.Precision.HIGHEST
TILE = 128
VMEM = pl.BlockSpec(memory_space=pltpu.VMEM)
SMEM = pl.BlockSpec(memory_space=pltpu.SMEM)


def shifted(array, axis, by):
    size = lax.axis_size(axis)
    pairs = [(i, i + by) for i in range(size) if 0 <= i + by < size]
    return lax.ppermute(array, axis, pairs)


def fir_body(halo_ref, x_ref, w_ref, o_ref, ext_ref):
    taps, width, beams = w_ref.shape
    rows = x_ref.shape[0]
    lead = halo_ref.shape[0]
    ext_ref[:lead, :] = halo_ref[...].astype(jnp.float32)
    ext_ref[lead:, :] = x_ref[...].astype(jnp.float32)
    step = 256
    for m in range(0, rows, step):
        window = jnp.concatenate(
            [
                ext_ref[lead - k + m : lead - k + m + step, :].astype(jnp.bfloat16)
                for k in range(taps)
            ],
            1,
        )
        o_ref[m : m + step, :] = jnp.dot(
            window, w_ref[...].reshape(taps * width, beams), preferred_element_type=jnp.float32
        )


def fir(halo, samples, taps_weight):
    rows, width = samples.shape
    taps, _, beams = taps_weight.shape
    return pl.pallas_call(
        fir_body,
        out_shape=jax.ShapeDtypeStruct((rows, beams), jnp.float32),
        in_specs=[VMEM] * 3,
        out_specs=VMEM,
        scratch_shapes=[pltpu.VMEM((rows + halo.shape[0], width), jnp.float32)],
        compiler_params=pltpu.CompilerParams(vmem_limit_bytes=40 << 20),
        cost_estimate=pl.CostEstimate(
            flops=2 * rows * taps * width * beams, bytes_accessed=6 << 20, transcendentals=0
        ),
        name="fir",
    )(halo, samples, taps_weight)


def gram_body(b_ref, weight_ref, o_ref):
    beams = b_ref.shape[1]
    weighted = b_ref[...] * weight_ref[...]
    at = 0
    for r in range(0, beams, TILE):
        part = lax.dot_general(
            weighted[:, r : r + TILE],
            b_ref[:, r:],
            (((0,), (0,)), ((), ())),
            precision=HI,
            preferred_element_type=jnp.float32,
        )
        for c in range(0, beams - r, TILE):
            o_ref[at : at + TILE, :] = part[:, c : c + TILE]
            at += TILE


def packed_gram(beam_rows, weight):
    beams = beam_rows.shape[1]
    n = beams // TILE
    return pl.pallas_call(
        gram_body,
        out_shape=jax.ShapeDtypeStruct((n * (n + 1) // 2 * TILE, TILE), jnp.float32),
        in_specs=[VMEM] * 2,
        out_specs=VMEM,
        name="packed_gram",
    )(beam_rows, weight)


def share_body(stats_ref, p_ref, o_ref):
    groups, rows, _ = p_ref.shape
    ways = o_ref.shape[0]
    total = p_ref[0]
    for g in range(1, groups):
        total = total + p_ref[g]
    tiles = rows // ways
    for s in range(tiles):
        o_ref[:, s * TILE : (s + 1) * TILE] = total[s * ways : (s + 1) * ways, :]
    lane = lax.broadcasted_iota(jnp.int32, (ways, TILE), 1)
    o_ref[:, tiles * TILE :] = jnp.where(lane == 0, stats_ref[0], stats_ref[1])


def spread_share(parts, log_total, mass, ways):
    groups, rows, _ = parts.shape
    return pl.pallas_call(
        share_body,
        out_shape=jax.ShapeDtypeStruct((ways, (rows // ways + 1) * TILE), jnp.float32),
        in_specs=[SMEM, VMEM],
        out_specs=VMEM,
        name="spread_share",
    )(jnp.stack([log_total, mass]), parts)


def decay_body(r_ref, o_ref):
    n, wide = r_ref.shape
    stats = r_ref[:, wide - TILE :]
    logs = stats[:, 0:1]
    row = lax.broadcasted_iota(jnp.int32, (n, n), 0)
    col = lax.broadcasted_iota(jnp.int32, (n, n), 1)
    upto = jnp.where(col <= row, 1.0, 0.0)
    later = jnp.where(row > col, jnp.broadcast_to(logs, (n, n)), 0.0)
    span = jnp.dot(upto, later, precision=HI, preferred_element_type=jnp.float32)
    factor = jnp.where(col <= row, jnp.exp(jnp.where(col <= row, span, 0.0)), 0.0)
    count = jnp.dot(factor, stats, precision=HI, preferred_element_type=jnp.float32)[:, 1:2]
    gram = jnp.dot(
        factor, r_ref[:, : wide - TILE], precision=HI, preferred_element_type=jnp.float32
    )
    o_ref[...] = gram / count


def decayed(received):
    n, wide = received.shape
    return pl.pallas_call(
        decay_body,
        out_shape=jax.ShapeDtypeStruct((n, wide - TILE), jnp.float32),
        in_specs=[VMEM],
        out_specs=VMEM,
        name="decayed_sums",
    )(received)


def spread_row(x, r):
    return jnp.broadcast_to(x[r : r + 1, :], x.shape)


def spread_lane(x, at):
    return jnp.broadcast_to(x[:, at : at + 1], x.shape)


def factor_tile(rows):
    lane = lax.broadcasted_iota(jnp.int32, (8, TILE), 1)
    sub = lax.broadcasted_iota(jnp.int32, (8, TILE), 0)
    rows, out = (list(rows), [])
    for k in range(len(rows)):
        base = 8 * k
        cols = [spread_lane(rows[k], base + c) for c in range(8)]
        inside = (lane >= base) & (lane < base + 8)
        g = jnp.where(inside, jnp.where(lane - base == sub, 1.0, 0.0), rows[k])
        w = g
        pivots = jnp.ones((8, TILE), jnp.float32)
        inverses = pivots
        for c in range(8):
            pivot = spread_row(cols[c], c)
            inverse = 1.0 / pivot
            scaled = cols[c] * inverse
            other = jnp.where(sub == c, 0.0, scaled)
            below = jnp.where(sub > c, scaled, 0.0)
            for s in range(c + 1, 8):
                cols[s] = cols[s] - other * spread_row(cols[s], c)
            g = g - other * spread_row(g, c)
            w = w - below * spread_row(w, c)
            pivots = jnp.where(sub == c, pivot, pivots)
            inverses = jnp.where(sub == c, inverse, inverses)
        z = g * inverses
        out.append(jnp.where(lane < base + 8, w * lax.rsqrt(pivots), 0.0))
        if k + 1 < len(rows):
            z_rows = [spread_row(z, c) for c in range(8)]
            for i in range(k + 1, len(rows)):
                m = [spread_lane(rows[i], base + c) * z_rows[c] for c in range(8)]
                total = ((m[0] + m[1]) + (m[2] + m[3])) + ((m[4] + m[5]) + (m[6] + m[7]))
                rows[i] = jnp.where(inside, 0.0, rows[i]) - total
    return out


def factor_body(group_ref, p_ref, o_ref, s_ref, d_ref, l_ref):
    groups, ways, wide = p_ref.shape
    n = s_ref.shape[0]
    count = n // TILE
    blocks = [(r, c) for r in range(count) for c in range(r, count)]
    for g in range(groups):
        for s in range(wide // TILE):
            first = (g * (wide // TILE) + s) * ways
            r, c = blocks[first // TILE]
            top = r * TILE + first % TILE
            piece = p_ref[g, :, s * TILE : (s + 1) * TILE]
            if r == c:
                row = lax.broadcasted_iota(jnp.int32, piece.shape, 0) + first % TILE
                lane = lax.broadcasted_iota(jnp.int32, piece.shape, 1)
                piece = piece + jnp.where(row == lane, loading_level, 0.0)
            s_ref[top : top + ways, c * TILE : (c + 1) * TILE] = piece
    for r in range(count):
        for c in range(r):
            s_ref[r * TILE : (r + 1) * TILE, c * TILE : (c + 1) * TILE] = jnp.zeros(
                (TILE, TILE), jnp.float32
            )
    tile_of = lax.broadcasted_iota(jnp.int32, (TILE, n), 1) // TILE

    @pl.loop(0, count)
    def _(k):
        first = pl.multiple_of(k * TILE, TILE)
        d_ref[...] = s_ref[pl.ds(first, TILE), pl.ds(first, TILE)]
        rows = factor_tile([d_ref[i : i + 8, :] for i in range(0, TILE, 8)])
        for i in range(TILE // 8):
            d_ref[8 * i : 8 * i + 8, :] = rows[i]
        x = d_ref[...]
        y = jnp.dot(x, s_ref[pl.ds(first, TILE), :], precision=HI, preferred_element_type=jnp.float32)
        y = jnp.where(tile_of == k, jnp.concatenate([x] * count, 1), y)
        l_ref[pl.ds(first, TILE), :] = jnp.where(tile_of <= k, y, 0.0)
        for i in range(1, count):

            @pl.when(i > k)
            def _():
                change = lax.dot_general(
                    y[:, i * TILE : (i + 1) * TILE],
                    y,
                    (((0,), (0,)), ((), ())),
                    precision=HI,
                    preferred_element_type=jnp.float32,
                )
                old = s_ref[i * TILE : (i + 1) * TILE, :]
                s_ref[i * TILE : (i + 1) * TILE, :] = jnp.where(tile_of == k, 0.0, old) - change

    mine = o_ref.shape[0]
    o_ref[...] = l_ref[pl.ds(pl.multiple_of(group_ref[0] * mine, mine), mine), :]


def inverse_factor_rows(packed, group, groups):
    ways, wide = packed.shape[1:]
    tiles = packed.size // (TILE * TILE)
    count = next(c for c in range(1, tiles + 1) if c * (c + 1) // 2 == tiles)
    n = count * TILE
    return pl.pallas_call(
        factor_body,
        out_shape=jax.ShapeDtypeStruct((n // groups, n), jnp.float32),
        in_specs=[SMEM, VMEM],
        out_specs=VMEM,
        scratch_shapes=[
            pltpu.VMEM((n, n), jnp.float32),
            pltpu.VMEM((TILE, TILE), jnp.float32),
            pltpu.VMEM((n, n), jnp.float32),
        ],
        compiler_params=pltpu.CompilerParams(vmem_limit_bytes=32 << 20),
        cost_estimate=pl.CostEstimate(flops=12 * n**3, bytes_accessed=1 << 20, transcendentals=n),
        name="inverse_factor",
    )(group.reshape(1).astype(jnp.int32), packed)


def local(samples, taps_weight, retain):
    row_count = samples.shape[0]
    groups, blocks = (lax.axis_size("elem"), lax.axis_size("tm"))
    group = lax.axis_index("elem")
    share = row_count // groups
    with jax.named_scope("halo"):
        halo = shifted(samples[row_count - 16 :], "tm", 1)
    beams_part = fir(halo, samples, taps_weight)
    log_retain = jnp.log(retain)
    log_total = jnp.sum(log_retain)
    row_weight = jnp.exp(log_total - jnp.cumsum(log_retain))
    mass = jnp.sum(row_weight)
    my_weight = lax.dynamic_slice_in_dim(row_weight, group * share, share)[:, None]
    with jax.named_scope("beams_sum"):
        my_beams = lax.psum_scatter(beams_part, "elem", scatter_dimension=0, tiled=True)
    packed = packed_gram(my_beams, my_weight)
    with jax.named_scope("gram_sum"):
        parts = lax.all_to_all(
            packed.reshape(groups, packed.shape[0] // groups, TILE), "elem", 0, 0
        )
    with jax.named_scope("beams_gather"):
        my_beams, _ = lax.optimization_barrier((my_beams, parts[0, :8]))
        beam_rows = lax.all_gather(my_beams, "elem", tiled=True)
    spread = spread_share(parts, log_total, mass, blocks)
    with jax.named_scope("blocks_out"):
        received = lax.all_to_all(spread, "tm", 0, 0, tiled=True)
    estimate = decayed(received)
    with jax.named_scope("blocks_back"):
        returned = lax.all_to_all(estimate, "tm", 0, 0, tiled=True)
    with jax.named_scope("gram_gather"):
        packed_estimate = lax.all_gather(returned, "elem")
    inverse_rows = inverse_factor_rows(packed_estimate, group, groups)
    return lax.dot_general(
        inverse_rows, beam_rows, (((1,), (1,)), ((), ())), precision=HI
    )


def solution(mesh):
    placed = (P("tm", "elem"), P(None, "elem", None), P("tm"))
    return jax.shard_map(
        local, mesh=mesh, in_specs=placed, out_specs=P("elem", "tm"), check_vma=False
    )
```

time: 566 us -> 190 us (0.34); the launches traced: 555 us -> 189 us
  other arithmetic: 209 us -> 4.1 us
  waiting for transfers between devices: 134 us -> 69.1 us
  local copies, waits for them, and re-layouts: 63.6 us -> 8.38 us
  loops' own time: 44.4 us -> 0 us
  Pallas kernels: 0 us -> 33.8 us
  matrix products: 25.2 us -> 3.68 us
  blocking collectives: 59.3 us -> 50.5 us
    another operation x19 -> x3, other arithmetic: 120 us -> 2.12 us  [the longest x1 1.82 us: spread_share(): jnp.stack([log_total, mass])]
    psum x1 -> x0, waiting for transfers between devices: 79.3 us -> none  [local(): lax.psum(jnp.dot(windowed, filters, preferred_element_type=jnp.float32),...]
    select_n x31 -> x0, other arithmetic: 75.8 us -> none  [hop(): jnp.where(position < mine, new, old)]
    unnamed x1 -> x0, blocking collectives: 59.3 us -> none
    all_gather x1, waiting for transfers between devices: 52.1 us -> 0.02 us  [local(): beam_rows = lax.all_gather(my_beams, 'elem', tiled=True)]
    another operation x2 -> x0, loops' own time: 44.4 us -> none  [the longest x1 44.4 us: entering(): return lax.fori_loop(0, count - 1, hop, so_far)]
    reduce_scatter x0 -> x1, waiting for transfers between devices: none -> 43.4 us  [local(): lax.psum_scatter(beams_part, 'elem', scatter_dimension=0, tiled=True)]
    dynamic_slice x62 -> x0, local copies, waits for them, and re-layouts: 41.3 us -> none  [hop(): longer = join(so_far, jax.tree.map(lambda part: part[position], pieces))]
  transfers between devices with their start and end apart: 3 -> 4, of which waited for: 3 -> 3; matrix products, arithmetic and copies ran while one was open for 2% -> 4% of each run, Pallas kernels for 0% -> 15%
where the time goes in v1:
time: 190 us; the launch traced here: 189 us
  waiting for transfers between devices  69.1 us (36%)
  blocking collectives  50.5 us (27%)
  Pallas kernels  33.8 us (18%)
  between operations  13.5 us (7%)
  local copies, waits for them, and re-layouts  8.38 us (4%)
  starting transfers between devices  6.22 us (3%)
  other arithmetic  4.1 us (2%)
  matrix products  3.68 us (2%)
    reduce_scatter x1, waiting for transfers between devices, local(): lax.psum_scatter(beams_part, 'elem', scatter_dimension=0, tiled=True)  43.4 us
    all_gather x1, blocking collectives, local(): packed_estimate = lax.all_gather(returned, 'elem')  25.9 us
    pallas_call x1, Pallas kernels, inverse_factor_rows(): pl.pallas_call(factor_body, out_shape=jax.ShapeDtypeStruct((n // groups,...  22.8 us
    all_to_all x1, waiting for transfers between devices, local(): lax.all_to_all(packed.reshape(groups, packed.shape[0] // groups, TILE), '...  22.6 us
    all_to_all x1, blocking collectives, local(): received = lax.all_to_all(spread, 'tm', 0, 0, tiled=True)  13.6 us
    all_to_all x1, blocking collectives, local(): returned = lax.all_to_all(estimate, 'tm', 0, 0, tiled=True)  11 us
    unnamed x10, local copies, waits for them, and re-layouts  4.72 us
    pallas_call x1, Pallas kernels, fir(): pl.pallas_call(fir_body, out_shape=jax.ShapeDtypeStruct((rows, beams), jn...  4.58 us
  transfers between devices with their start and end apart: 4, of which 3 were waited for; matrix products, arithmetic and copies ran while one was open for 4% of the time, Pallas kernels for 15%

profile of v1, /device:TPU:2, one launch (start us, length us, event | category | flops | bytes accessed | tf_op | source)
XLA Modules:
  0.0 189.2 jit_solution(5370510965022583024)
XLA Ops:
  6.5 0.0 reduce-scatter.2.cloned.1.call-start
  6.5 0.7 slice.13
  7.2 1.9 %collective-permute-start = (bf16[16,256]{1,0:T(8,128)(2,1)S(1)}, bf16[16,256]{1,0:T(8,128)(2,1)S(1)}, u32[]{:S(2)}, u32[]{:S(2)}) collective-permute-start(bf16[16,256]{1,0:T(8,128)(2,1)S(1)} %slice.13), channel_id=1, source_target_pairs={{0,1},{1,2},{2,3},{3,4},{4,5},{5,6},{6,7},{7,8},{8,9},{9,10},{10,1... | collective-permute-start | bytes 24584 | tf_op jit(solution)/shard_map/halo/ppermute | solution.py:18
  9.2 3.0 %collective-permute-done.halo_ref = bf16[16,256]{1,0:T(8,128)(2,1)S(1)} collective-permute-done((bf16[16,256]{1,0:T(8,128)(2,1)S(1)}, bf16[16,256]{1,0:T(8,128)(2,1)S(1)}, u32[]{:S(2)}, u32[]{:S(2)}) %collective-permute-start) | collective-permute-done | bytes 8224 | tf_op jit(solution)/shard_map/halo/ppermute | solution.py:18
  12.2 0.0 copy-start
  12.2 1.0 copy-done
  13.2 0.0 copy-start.1
  13.2 2.2 %copy-done.1 = bf16[16,256,512]{2,1,0:T(8,128)(2,1)S(1)} copy-done((bf16[16,256,512]{2,1,0:T(8,128)(2,1)S(1)}, bf16[16,256,512]{2,1,0:T(8,128)(2,1)}, u32[]{:S(2)}) %copy-start.1) | copy-done | bytes 4194328
  15.4 4.6 %fir.1 = f32[768,512]{1,0:T(8,128)} custom-call(bf16[16,256]{1,0:T(8,128)(2,1)S(1)} %collective-permute-done.halo_ref, bf16[768,256]{1,0:T(8,128)(2,1)S(1)} %copy-done, bf16[16,256,512]{2,1,0:T(8,128)(2,1)S(1)} %copy-done.1), custom_call_target="tpu_custom_call" | custom-call | flops 3221225472 | bytes 6291456 | tf_op jit(solution)/shard_map/fir/pallas_call | solution.py:44
  20.0 0.0 copy-start.3
  20.0 0.0 reduce-scatter.2.cloned.1.call-update
  20.0 0.0 all-gather.3.cloned.1.call-start
  20.0 43.4 %reduce-scatter.2.cloned.1.call-done.b_ref = f32[96,512]{1,0:T(8,128)} async-done(((f32[768,512]{1,0:T(8,128)}), f32[96,512]{1,0:T(8,128)}) %reduce-scatter.2.cloned.1.call-update) | async-done | bytes 196624 | tf_op jit(solution)/shard_map/beams_sum/reduce_scatter | solution.py:269
  63.5 0.0 all-gather.3.cloned.1.call-update
  63.5 0.0 copy-done.3
  63.5 0.7 log_reduce_fusion
  64.2 0.3 reduce-window.9
  64.5 0.1 slice.11
  64.6 0.1 slice_reduce_fusion
  64.7 1.3 fusion
  66.0 0.1 dynamic-slice_bitcast_fusion
  66.1 0.7 copy.9.weight_ref
  66.8 2.6 %packed_gram.1 = f32[1280,128]{1,0:T(8,128)} custom-call(f32[96,512]{1,0:T(8,128)} %reduce-scatter.2.cloned.1.call-done.b_ref, f32[96,1]{1,0:T(8,128)} %copy.9.weight_ref), custom_call_target="tpu_custom_call" | custom-call | tf_op jit(solution)/shard_map/packed_gram/pallas_call | solution.py:78
  69.4 4.3 %all-to-all-start = ((f32[8,160,128]{2,1,0:T(8,128)}), f32[8,160,128]{2,1,0:T(8,128)S(1)}, u32[]{:S(2)}, u32[]{:S(2)}) async-start(f32[8,160,128]{2,1,0:T(8,128)} %bitcast.19), calls=%async_computation.1 | async-start | bytes 1310720 | tf_op jit(solution)/shard_map/gram_sum/all_to_all | solution.py:272
  73.6 1.8 pad_maximum_fusion.stats_ref
  75.5 22.6 %all-to-all-done.p_ref = f32[8,160,128]{2,1,0:T(8,128)S(1)} async-done(((f32[8,160,128]{2,1,0:T(8,128)}), f32[8,160,128]{2,1,0:T(8,128)S(1)}, u32[]{:S(2)}, u32[]{:S(2)}) %all-to-all-start) | async-done | bytes 655392 | tf_op jit(solution)/shard_map/gram_sum/all_to_all | solution.py:272
  98.0 0.0 copy-start.2
  98.0 0.8 copy-done.2
  98.9 1.8 spread_share.1
  100.7 1.0 copy.10
  101.7 13.6 %all_to_all.25 = f32[32,1,768]{2,1,0:T(1,128)S(1)} all-to-all(f32[32,1,768]{2,1,0:T(1,128)S(1)} %copy.10), channel_id=1, replica_groups=mesh['elem'=8,'tm'=32] {'tm'}, dimensions={0} | all-to-all | bytes 196608 | tf_op jit(solution)/shard_map/blocks_out/all_to_all | solution.py:280
  115.2 0.6 copy.15
  115.9 2.0 %decayed_sums.1 = f32[32,640]{1,0:T(8,128)} custom-call(f32[32,768]{1,0:T(8,128)} %bitcast.21), custom_call_target="tpu_custom_call" | custom-call | tf_op jit(solution)/shard_map/decayed_sums/pallas_call | solution.py:130
  117.9 1.0 copy.11
  118.9 11.0 %all_to_all.26 = f32[32,1,640]{2,1,0:T(1,128)S(1)} all-to-all(f32[32,1,640]{2,1,0:T(1,128)S(1)} %copy.11), channel_id=1, replica_groups=mesh['elem'=8,'tm'=32] {'tm'}, dimensions={0} | all-to-all | bytes 163840 | tf_op jit(solution)/shard_map/blocks_back/all_to_all | solution.py:283
  129.8 25.9 %all-gather = f32[256,1,640]{2,1,0:T(1,128)S(1)} all-gather(f32[32,1,640]{2,1,0:T(1,128)S(1)} %all_to_all.26), channel_id=2, replica_groups=mesh['elem'=8,'tm'=32] {'elem'}, dimensions={0}, use_global_device_ids=true | all-gather | bytes 737280 | tf_op jit(solution)/shard_map/gram_gather/all_gather | solution.py:285
  155.8 22.8 %inverse_factor.1 = f32[64,512]{1,0:T(8,128)S(1)} custom-call(s32[1]{0:T(128)} %bitcast.group_ref, f32[8,32,640]{2,1,0:T(8,128)S(1)} %bitcast.18), custom_call_target="tpu_custom_call" | custom-call | flops 1610612736 | bytes 1048576 | tf_op jit(solution)/shard_map/inverse_factor/pallas_call | solution.py:239
  178.6 0.0 all-gather.3.cloned.1.call-done
  178.7 3.7 %fusion.2 = f32[64,768]{1,0:T(8,128)} fusion(f32[64,512]{1,0:T(8,128)S(1)} %inverse_factor.1, f32[768,512]{1,0:T(8,128)} %all-gather.3.cloned.1.call-done), kind=kOutput, calls=%fused_computation.9 | convolution fusion | flops 301989888 | bytes 1900544 | tf_op jit(solution)/shard_map/dot_general | solution.py:287
  (2 shorter events, 0.1 us)
Async XLA Ops:
  6.5 56.9 %reduce-scatter.2.cloned.1.call-start = ((), (), s32[]{:S(2)}) async-start(), calls=%async_computation.4 | async-start | bytes 1769472 | tf_op jit(solution)/shard_map/beams_sum/reduce_scatter | solution.py:269
  7.2 5.0 %collective-permute-start = (bf16[16,256]{1,0:T(8,128)(2,1)S(1)}, bf16[16,256]{1,0:T(8,128)(2,1)S(1)}, u32[]{:S(2)}, u32[]{:S(2)}) collective-permute-start(bf16[16,256]{1,0:T(8,128)(2,1)S(1)} %slice.13), channel_id=1, source_target_pairs={{0,1},{1,2},{2,3},{3,4},{4,5},{5,6},{6,7},{7,8},{8,9},{9,10},{10,1... | collective-permute-start | bytes 24584 | tf_op jit(solution)/shard_map/halo/ppermute | solution.py:18
  12.2 1.0 copy-start
  13.2 2.2 %copy-start.1 = (bf16[16,256,512]{2,1,0:T(8,128)(2,1)S(1)}, bf16[16,256,512]{2,1,0:T(8,128)(2,1)}, u32[]{:S(2)}) copy-start(bf16[16,256,512]{2,1,0:T(8,128)(2,1)} %w_ref.1) | copy-start | bytes 12582916
  20.0 43.6 %copy-start.3 = (f32[768]{0:T(1024)S(1)}, f32[768]{0:T(1024)}, u32[]{:S(2)}) copy-start(f32[768]{0:T(1024)} %param.5) | copy-start | bytes 9220
  20.0 158.7 %all-gather.3.cloned.1.call-start = ((), (), s32[]{:S(2)}) async-start(), calls=%async_computation.5 | async-start | bytes 1769472 | tf_op jit(solution)/shard_map/beams_gather/all_gather | solution.py:277
  69.4 28.7 %all-to-all-start = ((f32[8,160,128]{2,1,0:T(8,128)}), f32[8,160,128]{2,1,0:T(8,128)S(1)}, u32[]{:S(2)}, u32[]{:S(2)}) async-start(f32[8,160,128]{2,1,0:T(8,128)} %bitcast.19), calls=%async_computation.1 | async-start | bytes 1310720 | tf_op jit(solution)/shard_map/gram_sum/all_to_all | solution.py:272
  98.0 0.8 copy-start.2
Sparse Core Ops, SparseCore 0:
  20.1 43.3 reduce-scatter.1
  65.3 44.2 all-gather.2

commit v2 on v1

v2 whole, which is shorter than its diff:
```python
import jax
import jax.numpy as jnp
from jax import lax
from jax.experimental import pallas as pl
from jax.experimental.pallas import tpu as pltpu
from jax.sharding import PartitionSpec as P

loading_level = 0.1
HI = lax.Precision.HIGHEST
TILE = 128
VMEM = pl.BlockSpec(memory_space=pltpu.VMEM)
SMEM = pl.BlockSpec(memory_space=pltpu.SMEM)


def shifted(array, axis, by):
    size = lax.axis_size(axis)
    pairs = [(i, i + by) for i in range(size) if 0 <= i + by < size]
    return lax.ppermute(array, axis, pairs)


LEAD = 16
SPLIT = 4


def fir_body(offsets, weights, group_ref, halo_ref, x_hbm, w_hbm, retain_ref, *refs):
    outs, (xb_ref, xe_ref, part_ref, wv_ref, x_sem, w_sem) = (refs[:-6], refs[-6:])
    taps, width, beams = w_hbm.shape
    rows = x_hbm.shape[0]
    groups = 8
    share = rows // groups
    each = taps // SPLIT
    copy_x = pltpu.make_async_copy(x_hbm, xb_ref, x_sem)
    copy_x.start()
    copies = []
    for q in range(SPLIT):
        span = pl.ds(q * each, each)
        copies.append(pltpu.make_async_copy(w_hbm.at[span], wv_ref.at[span], w_sem.at[q]))
        copies[-1].start()
    group = group_ref[0]
    if weights:
        weights_of(group, groups, retain_ref, outs[-2], outs[-1])
        outs = outs[:-2]
    xe_ref[:LEAD, :] = halo_ref[...].astype(jnp.float32)
    copy_x.wait()
    xe_ref[LEAD:, :] = xb_ref[...].astype(jnp.float32)
    tall = share + LEAD
    for i, by in enumerate(offsets):
        chunk = lax.rem(group + (by + groups), groups)
        part_ref[i * tall : (i + 1) * tall, :] = xe_ref[
            pl.ds(pl.multiple_of(chunk * share, 8), tall), :
        ]
    total = None
    for q in range(SPLIT):
        copies[q].wait()
        window = jnp.concatenate(
            [
                jnp.concatenate(
                    [
                        part_ref[i * tall + LEAD - k : (i + 1) * tall - k, :]
                        for i in range(len(offsets))
                    ],
                    0,
                ).astype(jnp.bfloat16)
                for k in range(q * each, (q + 1) * each)
            ],
            1,
        )
        product = jnp.dot(
            window,
            wv_ref[q * each : (q + 1) * each].reshape(each * width, beams),
            preferred_element_type=jnp.float32,
        )
        at = 0
        for o_ref in outs:
            tall_o = o_ref.shape[0]
            piece = product[at : at + tall_o]
            o_ref[...] = piece if q == 0 else o_ref[...] + piece
            at += tall_o


def weights_of(group, groups, retain_ref, weight_ref, stats_ref):
    rows = retain_ref.shape[1]
    share = rows // groups
    logs = jnp.log(retain_ref[...])
    lane = lax.broadcasted_iota(jnp.int32, (share, rows), 1)
    row = lax.broadcasted_iota(jnp.int32, (share, rows), 0)
    spread = jnp.broadcast_to(logs, (share, rows))

    def weight_at(first):
        later = jnp.where(lane > row + first, spread, 0.0)
        return jnp.exp(jnp.sum(later, axis=1, keepdims=True))

    mass = jnp.zeros((1, 1), jnp.float32)
    for g in range(groups):
        mass = mass + jnp.sum(weight_at(g * share), axis=0, keepdims=True)
    weight_ref[...] = jnp.broadcast_to(weight_at(group * share), weight_ref.shape)
    log_total = jnp.sum(logs, axis=1, keepdims=True)
    at = lax.broadcasted_iota(jnp.int32, stats_ref.shape, 1)
    stats_ref[...] = jnp.where(
        at == 0,
        jnp.broadcast_to(log_total, stats_ref.shape),
        jnp.broadcast_to(mass, stats_ref.shape),
    )


def fir(offsets, heights, weights, group, halo, samples, taps_weight, retain):
    rows, width = samples.shape
    taps, _, beams = taps_weight.shape
    share = rows // 8
    tall = share + LEAD
    shapes = [jax.ShapeDtypeStruct((h, beams), jnp.float32) for h in heights]
    if weights:
        shapes.append(jax.ShapeDtypeStruct((share, TILE), jnp.float32))
        shapes.append(jax.ShapeDtypeStruct((1, TILE), jnp.float32))
    any_space = pl.BlockSpec(memory_space=pltpu.HBM)
    return pl.pallas_call(
        lambda *refs: fir_body(offsets, weights, *refs),
        out_shape=shapes,
        in_specs=[SMEM, VMEM, any_space, any_space, VMEM],
        out_specs=[VMEM] * len(shapes),
        scratch_shapes=[
            pltpu.VMEM((rows, width), samples.dtype),
            pltpu.VMEM((rows + LEAD, width), jnp.float32),
            pltpu.VMEM((tall * len(offsets), width), jnp.float32),
            pltpu.VMEM(taps_weight.shape, taps_weight.dtype),
            pltpu.SemaphoreType.DMA,
            pltpu.SemaphoreType.DMA((SPLIT,)),
        ],
        compiler_params=pltpu.CompilerParams(vmem_limit_bytes=60 << 20),
        cost_estimate=pl.CostEstimate(
            flops=2 * share * len(offsets) * taps * width * beams,
            bytes_accessed=6 << 20,
            transcendentals=0,
        ),
        name="fir_rest" if weights else "fir_sent",
    )(group, halo, samples, taps_weight, retain)


def ring(array, by):
    size = lax.axis_size("elem")
    return lax.ppermute(array, "elem", [(i, (i + by) % size) for i in range(size)])


def relay_body(keep_ref, down_ref, up_ref, far_down_ref, far_up_ref, low_ref, high_ref):
    share = low_ref.shape[0]
    half = share // 2
    low = keep_ref[share : 2 * share, :] + down_ref[share:, :]
    low_ref[:half, :] = low[:half] + far_down_ref[...]
    low_ref[half:, :] = low[half:]
    high = keep_ref[2 * share :, :] + up_ref[share:, :]
    high_ref[:half, :] = high[:half]
    high_ref[half:, :] = high[half:] + far_up_ref[...]


def relay_sums(keep, down, up, far_down, far_up):
    shape = jax.ShapeDtypeStruct((keep.shape[0] // 3, keep.shape[1]), jnp.float32)
    return pl.pallas_call(
        relay_body,
        out_shape=(shape, shape),
        in_specs=[VMEM] * 5,
        out_specs=(VMEM, VMEM),
        compiler_params=pltpu.CompilerParams(vmem_limit_bytes=5 << 20),
        name="relay_sums",
    )(keep, down, up, far_down, far_up)


def gram_body(keep_ref, down_ref, up_ref, low_ref, high_ref, weight_ref, b_ref, o_ref):
    share, beams = b_ref.shape
    b_ref[...] = (
        (keep_ref[:share, :] + down_ref[:share, :])
        + (up_ref[:share, :] + low_ref[...])
        + high_ref[...]
    )
    weighted = b_ref[...] * jnp.concatenate([weight_ref[...]] * (beams // TILE), 1)
    at = 0
    for r in range(0, beams, TILE):
        part = lax.dot_general(
            weighted[:, r : r + TILE],
            b_ref[:, r:],
            (((0,), (0,)), ((), ())),
            precision=HI,
            preferred_element_type=jnp.float32,
        )
        for c in range(0, beams - r, TILE):
            o_ref[at : at + TILE, :] = part[:, c : c + TILE]
            at += TILE


def packed_gram(keep, down, up, low, high, weight):
    share, beams = low.shape
    n = beams // TILE
    return pl.pallas_call(
        gram_body,
        out_shape=(
            jax.ShapeDtypeStruct((share, beams), jnp.float32),
            jax.ShapeDtypeStruct((n * (n + 1) // 2 * TILE, TILE), jnp.float32),
        ),
        in_specs=[VMEM] * 6,
        out_specs=(VMEM, VMEM),
        compiler_params=pltpu.CompilerParams(vmem_limit_bytes=6 << 20),
        name="packed_gram",
    )(keep, down, up, low, high, weight)


def share_body(stats_ref, p_ref, o_ref):
    groups, rows, _ = p_ref.shape
    ways = o_ref.shape[0]
    total = p_ref[0]
    for g in range(1, groups):
        total = total + p_ref[g]
    tiles = rows // ways
    for s in range(tiles):
        o_ref[:, s, :] = total[s * ways : (s + 1) * ways, :]
    o_ref[:, tiles, :] = jnp.broadcast_to(stats_ref[...], (ways, TILE))


def spread_share(parts, stats, ways):
    groups, rows, _ = parts.shape
    return pl.pallas_call(
        share_body,
        out_shape=jax.ShapeDtypeStruct((ways, rows // ways + 1, TILE), jnp.float32),
        in_specs=[VMEM, VMEM],
        out_specs=VMEM,
        compiler_params=pltpu.CompilerParams(vmem_limit_bytes=4 << 20),
        name="spread_share",
    )(stats, parts)


def decay_body(r_ref, o_ref):
    n, tiles, _ = r_ref.shape
    tiles -= 1
    stats = r_ref[:, tiles, :]
    logs = stats[:, 0:1]
    row = lax.broadcasted_iota(jnp.int32, (n, n), 0)
    col = lax.broadcasted_iota(jnp.int32, (n, n), 1)
    upto = jnp.where(col <= row, 1.0, 0.0)
    later = jnp.where(row > col, jnp.broadcast_to(logs, (n, n)), 0.0)
    span = jnp.dot(upto, later, precision=HI, preferred_element_type=jnp.float32)
    factor = jnp.where(col <= row, jnp.exp(jnp.where(col <= row, span, 0.0)), 0.0)
    count = jnp.dot(factor, stats, precision=HI, preferred_element_type=jnp.float32)[:, 1:2]
    gram = jnp.dot(
        factor,
        jnp.concatenate([r_ref[:, s, :] for s in range(tiles)], 1),
        precision=HI,
        preferred_element_type=jnp.float32,
    )
    gram = gram / count
    for s in range(tiles):
        o_ref[:, s, :] = gram[:, s * TILE : (s + 1) * TILE]


def decayed(received):
    n, tiles, _ = received.shape
    return pl.pallas_call(
        decay_body,
        out_shape=jax.ShapeDtypeStruct((n, tiles - 1, TILE), jnp.float32),
        in_specs=[VMEM],
        out_specs=VMEM,
        compiler_params=pltpu.CompilerParams(vmem_limit_bytes=4 << 20),
        name="decayed_sums",
    )(received)


def replicate_body(r_ref, o_ref):
    ways, tiles, _ = r_ref.shape
    for s in range(tiles):
        piece = r_ref[:, s, :]
        for g in range(o_ref.shape[0]):
            o_ref[g, s * ways : (s + 1) * ways, :] = piece


def replicated(returned, groups):
    ways, tiles, _ = returned.shape
    return pl.pallas_call(
        replicate_body,
        out_shape=jax.ShapeDtypeStruct((groups, ways * tiles, TILE), jnp.float32),
        in_specs=[VMEM],
        out_specs=VMEM,
        compiler_params=pltpu.CompilerParams(vmem_limit_bytes=4 << 20),
        name="replicated",
    )(returned)


def spread_row(x, r):
    return jnp.broadcast_to(x[r : r + 1, :], x.shape)


def spread_lane(x, at):
    return jnp.broadcast_to(x[:, at : at + 1], x.shape)


def factor_tile(rows):
    lane = lax.broadcasted_iota(jnp.int32, (8, TILE), 1)
    sub = lax.broadcasted_iota(jnp.int32, (8, TILE), 0)
    rows, out = (list(rows), [])
    for k in range(len(rows)):
        base = 8 * k
        cols = [spread_lane(rows[k], base + c) for c in range(8)]
        inside = (lane >= base) & (lane < base + 8)
        g = jnp.where(inside, jnp.where(lane - base == sub, 1.0, 0.0), rows[k])
        w = g
        pivots = jnp.ones((8, TILE), jnp.float32)
        inverses = pivots
        for c in range(8):
            pivot = spread_row(cols[c], c)
            inverse = 1.0 / pivot
            scaled = cols[c] * inverse
            other = jnp.where(sub == c, 0.0, scaled)
            below = jnp.where(sub > c, scaled, 0.0)
            for s in range(c + 1, 8):
                cols[s] = cols[s] - other * spread_row(cols[s], c)
            g = g - other * spread_row(g, c)
            w = w - below * spread_row(w, c)
            pivots = jnp.where(sub == c, pivot, pivots)
            inverses = jnp.where(sub == c, inverse, inverses)
        z = g * inverses
        out.append(jnp.where(lane < base + 8, w * lax.rsqrt(pivots), 0.0))
        if k + 1 < len(rows):
            z_rows = [spread_row(z, c) for c in range(8)]
            for i in range(k + 1, len(rows)):
                m = [spread_lane(rows[i], base + c) * z_rows[c] for c in range(8)]
                total = ((m[0] + m[1]) + (m[2] + m[3])) + ((m[4] + m[5]) + (m[6] + m[7]))
                rows[i] = jnp.where(inside, 0.0, rows[i]) - total
    return out


def factor_body(p_ref, b_ref, o_ref, s_ref, d_ref, l_ref):
    groups, high, _ = p_ref.shape
    ways = 32
    tiles = high // ways
    n = s_ref.shape[0]
    count = n // TILE
    blocks = [(r, c) for r in range(count) for c in range(r, count)]
    for g in range(groups):
        for s in range(tiles):
            first = (g * tiles + s) * ways
            r, c = blocks[first // TILE]
            top = r * TILE + first % TILE
            piece = p_ref[g, s * ways : (s + 1) * ways, :]
            if r == c:
                row = lax.broadcasted_iota(jnp.int32, piece.shape, 0) + first % TILE
                lane = lax.broadcasted_iota(jnp.int32, piece.shape, 1)
                piece = piece + jnp.where(row == lane, loading_level, 0.0)
            s_ref[top : top + ways, c * TILE : (c + 1) * TILE] = piece
    for r in range(count):
        for c in range(r):
            s_ref[r * TILE : (r + 1) * TILE, c * TILE : (c + 1) * TILE] = jnp.zeros(
                (TILE, TILE), jnp.float32
            )
    tile_of = lax.broadcasted_iota(jnp.int32, (TILE, n), 1) // TILE

    @pl.loop(0, count)
    def _(k):
        first = pl.multiple_of(k * TILE, TILE)
        d_ref[...] = s_ref[pl.ds(first, TILE), pl.ds(first, TILE)]
        rows = factor_tile([d_ref[i : i + 8, :] for i in range(0, TILE, 8)])
        for i in range(TILE // 8):
            d_ref[8 * i : 8 * i + 8, :] = rows[i]
        x = d_ref[...]
        y = jnp.dot(x, s_ref[pl.ds(first, TILE), :], precision=HI, preferred_element_type=jnp.float32)
        y = jnp.where(tile_of == k, jnp.concatenate([x] * count, 1), y)
        l_ref[pl.ds(first, TILE), :] = jnp.where(tile_of <= k, y, 0.0)
        for i in range(1, count):

            @pl.when(i > k)
            def _():
                change = lax.dot_general(
                    y[:, i * TILE : (i + 1) * TILE],
                    y,
                    (((0,), (0,)), ((), ())),
                    precision=HI,
                    preferred_element_type=jnp.float32,
                )
                old = s_ref[i * TILE : (i + 1) * TILE, :]
                s_ref[i * TILE : (i + 1) * TILE, :] = jnp.where(tile_of == k, 0.0, old) - change

    o_ref[...] = lax.dot_general(
        l_ref[...],
        b_ref[...],
        (((1,), (1,)), ((), ())),
        precision=HI,
        preferred_element_type=jnp.float32,
    )


def whitened_share(packed, my_beams):
    share, n = my_beams.shape
    return pl.pallas_call(
        factor_body,
        out_shape=jax.ShapeDtypeStruct((n, share), jnp.float32),
        in_specs=[VMEM, VMEM],
        out_specs=VMEM,
        scratch_shapes=[
            pltpu.VMEM((n, n), jnp.float32),
            pltpu.VMEM((TILE, TILE), jnp.float32),
            pltpu.VMEM((n, n), jnp.float32),
        ],
        compiler_params=pltpu.CompilerParams(vmem_limit_bytes=8 << 20),
        cost_estimate=pl.CostEstimate(flops=12 * n**3, bytes_accessed=1 << 20, transcendentals=n),
        name="whitened_share",
    )(packed, my_beams)


def join_body(r_ref, o_ref):
    share = r_ref.shape[2]
    for g in range(r_ref.shape[0]):
        o_ref[:, g * share : (g + 1) * share] = r_ref[g]


def joined(received):
    groups, mine, share = received.shape
    return pl.pallas_call(
        join_body,
        out_shape=jax.ShapeDtypeStruct((mine, groups * share), jnp.float32),
        in_specs=[VMEM],
        out_specs=VMEM,
        compiler_params=pltpu.CompilerParams(vmem_limit_bytes=3 << 20),
        name="joined",
    )(received)


def local(samples, taps_weight, retain):
    row_count = samples.shape[0]
    groups, blocks = (lax.axis_size("elem"), lax.axis_size("tm"))
    group = lax.axis_index("elem").reshape(1).astype(jnp.int32)
    share = row_count // groups
    half = share // 2
    with jax.named_scope("halo"):
        halo = shifted(samples[row_count - LEAD :], "tm", 1)
    args = (group, halo, samples, taps_weight, retain.reshape(1, row_count))
    down, up, far_down, far_up = fir(
        (-1, -3, 1, 3, 4), (2 * share, 2 * share, half, half), False, *args
    )
    with jax.named_scope("beams_near"):
        down, up = (ring(down, -1), ring(up, 1))
        far_down, far_up = (ring(far_down, -2), ring(far_up, 2))
    keep, weight, stats = fir((0, -2, 2), (3 * share,), True, *args)
    low, high = relay_sums(keep, down, up, far_down, far_up)
    with jax.named_scope("beams_far"):
        low, high = (ring(low, -2), ring(high, 2))
    my_beams, packed = packed_gram(keep, down, up, low, high, weight)
    with jax.named_scope("gram_sum"):
        parts = lax.all_to_all(
            packed.reshape(groups, packed.shape[0] // groups, TILE), "elem", 0, 0
        )
    spread = spread_share(parts, stats, blocks)
    with jax.named_scope("blocks_out"):
        received = lax.all_to_all(spread, "tm", 0, 0, tiled=True)
    estimate = decayed(received)
    with jax.named_scope("blocks_back"):
        returned = lax.all_to_all(estimate, "tm", 0, 0, tiled=True)
    with jax.named_scope("gram_gather"):
        packed_estimate = lax.all_to_all(replicated(returned, groups), "elem", 0, 0)
    mine = whitened_share(packed_estimate, my_beams)
    with jax.named_scope("whitened_out"):
        pieces = lax.all_to_all(mine.reshape(groups, mine.shape[0] // groups, share), "elem", 0, 0)
    return joined(pieces)


def solution(mesh):
    placed = (P("tm", "elem"), P(None, "elem", None), P("tm"))
    return jax.shard_map(
        local, mesh=mesh, in_specs=placed, out_specs=P("elem", "tm"), check_vma=False
    )
```

time: 190 us -> 161 us (0.85)
  waiting for transfers between devices: 69.1 us -> 19.8 us
  blocking collectives: 50.5 us -> 83.3 us
  between operations: 13.5 us -> 0.09 us
  starting transfers between devices: 6.22 us -> 13.8 us
  other arithmetic: 4.1 us -> 0 us
  matrix products: 3.68 us -> 0 us
  Pallas kernels: 33.8 us -> 37.2 us
  local copies, waits for them, and re-layouts: 8.38 us -> 5.51 us
    all_to_all x0 -> x3, blocking collectives: none -> 59.1 us  [the longest x1 23.3 us: local(): packed_estimate = lax.all_to_all(replicated(returned, groups), 'elem', 0, 0)]
    reduce_scatter x1 -> x0, waiting for transfers between devices: 43.4 us -> none  [local(): lax.psum_scatter(beams_part, 'elem', scatter_dimension=0, tiled=True)]
    all_gather x1 -> x0, blocking collectives: 25.9 us -> none  [local(): packed_estimate = lax.all_gather(returned, 'elem')]
    all_to_all x1 -> x0, waiting for transfers between devices: 22.6 us -> none  [local(): lax.all_to_all(packed.reshape(groups, packed.shape[0] // groups, TILE), '...]
    ppermute x0 -> x6, waiting for transfers between devices: none -> 18 us  [ring(): lax.ppermute(array, 'elem', [(i, (i + by) % size) for i in range(size)])]
    ppermute x0 -> x6, starting transfers between devices: none -> 11.9 us  [ring(): lax.ppermute(array, 'elem', [(i, (i + by) % size) for i in range(size)])]
    all_to_all x1 -> x0, starting transfers between devices: 4.27 us -> none  [local(): lax.all_to_all(packed.reshape(groups, packed.shape[0] // groups, TILE), '...]
    dot_general x1 -> x0, matrix products: 3.68 us -> none  [local(): lax.dot_general(inverse_rows, beam_rows, (((1,), (1,)), ((), ())), precis...]
  transfers between devices with their start and end apart: 4 -> 7, of which waited for: 3 -> 6; matrix products, arithmetic and copies ran while one was open for 4% -> 1% of each run, Pallas kernels for 15% -> 3%
where the time goes in v2:
time: 161 us; the launch traced here: 160 us
  blocking collectives  83.3 us (52%)
  Pallas kernels  37.2 us (23%)
  waiting for transfers between devices  19.8 us (12%)
  starting transfers between devices  13.8 us (9%)
  local copies, waits for them, and re-layouts  5.51 us (3%)
    pallas_call x1, Pallas kernels, whitened_share(): pl.pallas_call(factor_body, out_shape=jax.ShapeDtypeStruct((n, share), jn...  23.8 us
    all_to_all x1, blocking collectives, local(): packed_estimate = lax.all_to_all(replicated(returned, groups), 'elem', 0, 0)  23.3 us
    all_to_all x1, blocking collectives, local(): lax.all_to_all(packed.reshape(groups, packed.shape[0] // groups, TILE), '...  21.2 us
    ppermute x6, waiting for transfers between devices, ring(): lax.ppermute(array, 'elem', [(i, (i + by) % size) for i in range(size)])  18 us
    all_to_all x1, blocking collectives, local(): lax.all_to_all(mine.reshape(groups, mine.shape[0] // groups, share), 'ele...  14.6 us
    all_to_all x1, blocking collectives, local(): received = lax.all_to_all(spread, 'tm', 0, 0, tiled=True)  12.9 us
    ppermute x6, starting transfers between devices, ring(): lax.ppermute(array, 'elem', [(i, (i + by) % size) for i in range(size)])  11.9 us
    all_to_all x1, blocking collectives, local(): returned = lax.all_to_all(estimate, 'tm', 0, 0, tiled=True)  11.3 us
  transfers between devices with their start and end apart: 7, of which 6 were waited for; matrix products, arithmetic and copies ran while one was open for 1% of the time, Pallas kernels for 3%

profile of v2, /device:TPU:2, one launch (start us, length us, event | category | flops | bytes accessed | tf_op | source)
XLA Modules:
  0.0 159.7 jit_solution(4795391114618674110)
XLA Ops:
  0.0 0.7 slice.3
  0.7 1.9 %collective-permute-start = (bf16[16,256]{1,0:T(8,128)(2,1)S(1)}, bf16[16,256]{1,0:T(8,128)(2,1)S(1)}, u32[]{:S(2)}, u32[]{:S(2)}) collective-permute-start(bf16[16,256]{1,0:T(8,128)(2,1)S(1)} %slice.3), channel_id=1, source_target_pairs={{0,1},{1,2},{2,3},{3,4},{4,5},{5,6},{6,7},{7,8},{8,9},{9,10},{10,1... | collective-permute-start | bytes 24584 | tf_op jit(solution)/shard_map/halo/ppermute | solution.py:18
  2.6 1.3 reshape.13.refs_4_
  3.9 1.8 %collective-permute-done.refs_1_ = bf16[16,256]{1,0:T(8,128)(2,1)S(1)} collective-permute-done((bf16[16,256]{1,0:T(8,128)(2,1)S(1)}, bf16[16,256]{1,0:T(8,128)(2,1)S(1)}, u32[]{:S(2)}, u32[]{:S(2)}) %collective-permute-start) | collective-permute-done | bytes 8224 | tf_op jit(solution)/shard_map/halo/ppermute | solution.py:18
  5.7 0.0 copy-start.4
  5.7 0.6 copy-done.4
  6.3 6.0 %fir_sent.1 = (f32[192,512]{1,0:T(8,128)}, f32[192,512]{1,0:T(8,128)}, f32[48,512]{1,0:T(8,128)}, f32[48,512]{1,0:T(8,128)}) custom-call(s32[1]{0:T(128)} %bitcast.refs_0_, bf16[16,256]{1,0:T(8,128)(2,1)} %copy-done.4, bf16[768,256]{1,0:T(8,128)(2,1)} %refs_2_.3, bf16[16,256,512]{2,1,0:T(8,128)(2,1)} %refs_3_.3, f32[1,768]{1,0:T(1,128)} %reshape.13.refs_4_), custom_call_target="tpu_custom_call" | custom-call | flops 2013265920 | bytes 6291456 | tf_op jit(solution)/shard_map/fir_sent/pallas_call | solution.py:116
  12.2 5.9 %collective-permute-start.1 = (f32[192,512]{1,0:T(8,128)}, f32[192,512]{1,0:T(8,128)S(1)}, u32[]{:S(2)}, u32[]{:S(2)}) collective-permute-start(f32[192,512]{1,0:T(8,128)} %get-tuple-element.18), channel_id=1, source_target_pairs={{0,224},{32,0},{64,32},{96,64},{128,96},{160,128},{192,160},{224,1... | collective-permute-start | bytes 1179656 | tf_op jit(solution)/shard_map/beams_near/ppermute | solution.py:141
  18.2 0.0 collective-permute-start.2
  18.2 2.5 %collective-permute-start.3 = (f32[48,512]{1,0:T(8,128)}, f32[48,512]{1,0:T(8,128)S(1)}, u32[]{:S(2)}, u32[]{:S(2)}) collective-permute-start(f32[48,512]{1,0:T(8,128)} %get-tuple-element.20), channel_id=1, source_target_pairs={{0,192},{32,224},{64,0},{96,32},{128,64},{160,96},{192,128},{224,1... | collective-permute-start | bytes 294920 | tf_op jit(solution)/shard_map/beams_near/ppermute | solution.py:141
  20.7 0.5 collective-permute-start.4
  21.1 5.1 %fir_rest.1 = (f32[288,512]{1,0:T(8,128)}, f32[96,128]{1,0:T(8,128)}, f32[1,128]{1,0:T(1,128)}) custom-call(s32[1]{0:T(128)} %bitcast.refs_0_, bf16[16,256]{1,0:T(8,128)(2,1)} %copy-done.4, bf16[768,256]{1,0:T(8,128)(2,1)} %refs_2_.3, bf16[16,256,512]{2,1,0:T(8,128)(2,1)} %refs_3_.3, f32[1,768]{1,0:T(1,128)} %reshape.13.refs_4_), custom_call_target="tpu_custom_call" | custom-call | flops 1207959552 | bytes 6291456 | tf_op jit(solution)/shard_map/fir_rest/pallas_call | solution.py:116
  26.2 0.0 copy-start.3
  26.3 4.8 %collective-permute-done.3.far_down_ref = f32[48,512]{1,0:T(8,128)S(1)} collective-permute-done((f32[48,512]{1,0:T(8,128)}, f32[48,512]{1,0:T(8,128)S(1)}, u32[]{:S(2)}, u32[]{:S(2)}) %collective-permute-start.3) | collective-permute-done | bytes 98336 | tf_op jit(solution)/shard_map/beams_near/ppermute | solution.py:141
  31.1 1.6 %collective-permute-done.4.far_up_ref = f32[48,512]{1,0:T(8,128)S(1)} collective-permute-done((f32[48,512]{1,0:T(8,128)}, f32[48,512]{1,0:T(8,128)S(1)}, u32[]{:S(2)}, u32[]{:S(2)}) %collective-permute-start.4) | collective-permute-done | bytes 98336 | tf_op jit(solution)/shard_map/beams_near/ppermute | solution.py:141
  32.7 0.0 collective-permute-done.1.down_ref
  32.7 0.6 collective-permute-done.2.up_ref
  33.4 0.0 copy-start
  33.4 1.1 copy-done
  34.4 0.1 relay_sums.1
  34.5 2.3 %collective-permute-start.5 = (f32[96,512]{1,0:T(8,128)S(1)}, f32[96,512]{1,0:T(8,128)S(1)}, u32[]{:S(2)}, u32[]{:S(2)}) collective-permute-start(f32[96,512]{1,0:T(8,128)S(1)} %get-tuple-element.22), channel_id=1, source_target_pairs={{0,192},{32,224},{64,0},{96,32},{128,64},{160,96},{192,128},{224,1... | collective-permute-start | bytes 589832 | tf_op jit(solution)/shard_map/beams_far/ppermute | solution.py:141
  36.8 0.7 collective-permute-start.6
  37.5 7.1 %collective-permute-done.5.low_ref = f32[96,512]{1,0:T(8,128)S(1)} collective-permute-done((f32[96,512]{1,0:T(8,128)S(1)}, f32[96,512]{1,0:T(8,128)S(1)}, u32[]{:S(2)}, u32[]{:S(2)}) %collective-permute-start.5) | collective-permute-done | bytes 196640 | tf_op jit(solution)/shard_map/beams_far/ppermute | solution.py:141
  44.6 3.8 %collective-permute-done.6.high_ref = f32[96,512]{1,0:T(8,128)S(1)} collective-permute-done((f32[96,512]{1,0:T(8,128)S(1)}, f32[96,512]{1,0:T(8,128)S(1)}, u32[]{:S(2)}, u32[]{:S(2)}) %collective-permute-start.6) | collective-permute-done | bytes 196640 | tf_op jit(solution)/shard_map/beams_far/ppermute | solution.py:141
  48.4 0.0 copy-start.1
  48.4 1.1 copy-done.1
  49.5 0.0 copy-start.2
  49.5 0.8 copy-done.2
  50.3 0.8 packed_gram.1
  51.0 21.2 %all_to_all.25.p_ref = f32[8,160,128]{2,1,0:T(8,128)S(1)} all-to-all(f32[8,160,128]{2,1,0:T(8,128)S(1)} %bitcast.3), channel_id=1, replica_groups=mesh['elem'=8,'tm'=32] {'elem'}, dimensions={0} | all-to-all | bytes 1310720 | tf_op jit(solution)/shard_map/gram_sum/all_to_all | solution.py:443
  72.3 0.0 copy-done.3
  72.3 0.1 spread_share.1
  72.3 12.9 %all_to_all.26.r_ref = f32[32,6,128]{2,1,0:T(8,128)S(1)} all-to-all(f32[32,6,128]{2,1,0:T(8,128)S(1)} %spread_share.1), channel_id=1, replica_groups=mesh['elem'=8,'tm'=32] {'tm'}, dimensions={0} | all-to-all | bytes 196608 | tf_op jit(solution)/shard_map/blocks_out/all_to_all | solution.py:448
  85.3 0.6 decayed_sums.1
  85.8 11.3 %all_to_all.27.r_ref = f32[32,5,128]{2,1,0:T(8,128)S(1)} all-to-all(f32[32,5,128]{2,1,0:T(8,128)S(1)} %decayed_sums.1), channel_id=1, replica_groups=mesh['elem'=8,'tm'=32] {'tm'}, dimensions={0} | all-to-all | bytes 163840 | tf_op jit(solution)/shard_map/blocks_back/all_to_all | solution.py:451
  97.1 0.1 replicated.1
  97.2 23.3 %all_to_all.28.p_ref = f32[8,160,128]{2,1,0:T(8,128)S(1)} all-to-all(f32[8,160,128]{2,1,0:T(8,128)S(1)} %replicated.1), channel_id=1, replica_groups=mesh['elem'=8,'tm'=32] {'elem'}, dimensions={0} | all-to-all | bytes 1310720 | tf_op jit(solution)/shard_map/gram_gather/all_to_all | solution.py:453
  120.4 23.8 %whitened_share.1 = f32[512,96]{1,0:T(8,128)S(1)} custom-call(f32[8,160,128]{2,1,0:T(8,128)S(1)} %all_to_all.28.p_ref, f32[96,512]{1,0:T(8,128)S(1)} %get-tuple-element.26.b_ref), custom_call_target="tpu_custom_call" | custom-call | flops 1610612736 | bytes 1048576 | tf_op jit(solution)/shard_map/whitened_share/pallas_call | solution.py:388
  144.3 14.6 %all_to_all.29.r_ref = f32[8,64,96]{2,1,0:T(8,128)S(1)} all-to-all(f32[8,64,96]{2,1,0:T(8,128)S(1)} %bitcast.4), channel_id=1, replica_groups=mesh['elem'=8,'tm'=32] {'elem'}, dimensions={0} | all-to-all | bytes 393216 | tf_op jit(solution)/shard_map/whitened_out/all_to_all | solution.py:456
  158.9 0.8 joined.1
Async XLA Ops:
  0.7 5.0 %collective-permute-start = (bf16[16,256]{1,0:T(8,128)(2,1)S(1)}, bf16[16,256]{1,0:T(8,128)(2,1)S(1)}, u32[]{:S(2)}, u32[]{:S(2)}) collective-permute-start(bf16[16,256]{1,0:T(8,128)(2,1)S(1)} %slice.3), channel_id=1, source_target_pairs={{0,1},{1,2},{2,3},{3,4},{4,5},{5,6},{6,7},{7,8},{8,9},{9,10},{10,1... | collective-permute-start | bytes 24584 | tf_op jit(solution)/shard_map/halo/ppermute | solution.py:18
  5.7 0.6 copy-start.4
  12.2 20.5 %collective-permute-start.1 = (f32[192,512]{1,0:T(8,128)}, f32[192,512]{1,0:T(8,128)S(1)}, u32[]{:S(2)}, u32[]{:S(2)}) collective-permute-start(f32[192,512]{1,0:T(8,128)} %get-tuple-element.18), channel_id=1, source_target_pairs={{0,224},{32,0},{64,32},{96,64},{128,96},{160,128},{192,160},{224,1... | collective-permute-start | bytes 1179656 | tf_op jit(solution)/shard_map/beams_near/ppermute | solution.py:141
  18.2 15.2 %collective-permute-start.2 = (f32[192,512]{1,0:T(8,128)}, f32[192,512]{1,0:T(8,128)S(1)}, u32[]{:S(2)}, u32[]{:S(2)}) collective-permute-start(f32[192,512]{1,0:T(8,128)} %get-tuple-element.19), channel_id=1, source_target_pairs={{0,32},{32,64},{64,96},{96,128},{128,160},{160,192},{192,224},{224... | collective-permute-start | bytes 1179656 | tf_op jit(solution)/shard_map/beams_near/ppermute | solution.py:141
  18.2 12.9 %collective-permute-start.3 = (f32[48,512]{1,0:T(8,128)}, f32[48,512]{1,0:T(8,128)S(1)}, u32[]{:S(2)}, u32[]{:S(2)}) collective-permute-start(f32[48,512]{1,0:T(8,128)} %get-tuple-element.20), channel_id=1, source_target_pairs={{0,192},{32,224},{64,0},{96,32},{128,64},{160,96},{192,128},{224,1... | collective-permute-start | bytes 294920 | tf_op jit(solution)/shard_map/beams_near/ppermute | solution.py:141
  20.7 12.1 %collective-permute-start.4 = (f32[48,512]{1,0:T(8,128)}, f32[48,512]{1,0:T(8,128)S(1)}, u32[]{:S(2)}, u32[]{:S(2)}) collective-permute-start(f32[48,512]{1,0:T(8,128)} %get-tuple-element.21), channel_id=1, source_target_pairs={{0,64},{32,96},{64,128},{96,160},{128,192},{160,224},{192,0},{224,... | collective-permute-start | bytes 294920 | tf_op jit(solution)/shard_map/beams_near/ppermute | solution.py:141
  26.2 46.0 %copy-start.3 = (f32[1,128]{1,0:T(1,128)S(1)}, f32[1,128]{1,0:T(1,128)}, u32[]{:S(2)}) copy-start(f32[1,128]{1,0:T(1,128)} %get-tuple-element.16.stats_ref) | copy-start | bytes 1540
  33.4 1.1 copy-start
  34.5 10.1 %collective-permute-start.5 = (f32[96,512]{1,0:T(8,128)S(1)}, f32[96,512]{1,0:T(8,128)S(1)}, u32[]{:S(2)}, u32[]{:S(2)}) collective-permute-start(f32[96,512]{1,0:T(8,128)S(1)} %get-tuple-element.22), channel_id=1, source_target_pairs={{0,192},{32,224},{64,0},{96,32},{128,64},{160,96},{192,128},{224,1... | collective-permute-start | bytes 589832 | tf_op jit(solution)/shard_map/beams_far/ppermute | solution.py:141
  36.8 11.6 %collective-permute-start.6 = (f32[96,512]{1,0:T(8,128)S(1)}, f32[96,512]{1,0:T(8,128)S(1)}, u32[]{:S(2)}, u32[]{:S(2)}) collective-permute-start(f32[96,512]{1,0:T(8,128)S(1)} %get-tuple-element.23), channel_id=1, source_target_pairs={{0,64},{32,96},{64,128},{96,160},{128,192},{160,224},{192,0},{224,... | collective-permute-start | bytes 589832 | tf_op jit(solution)/shard_map/beams_far/ppermute | solution.py:141
  48.4 1.1 copy-start.1
  49.5 0.8 copy-start.2

commit v3 on v2

--- a/solution.py
+++ b/solution.py
@@ -22,26 +22,34 @@
 SPLIT = 4
 
 
-def fir_body(offsets, weights, group_ref, halo_ref, x_hbm, w_hbm, retain_ref, *refs):
-    outs, (xb_ref, xe_ref, part_ref, wv_ref, x_sem, w_sem) = (refs[:-6], refs[-6:])
+def fir_body(offsets, weights, group_ref, halo_ref, x_hbm, w_hbm, *refs):
+    if weights:
+        retain_ref, refs = (refs[0], refs[1:])
+    held = 2 if weights else 6
+    outs, (xe_ref, part_ref, *own) = (refs[:-held], refs[-held:])
     taps, width, beams = w_hbm.shape
     rows = x_hbm.shape[0]
     groups = 8
     share = rows // groups
     each = taps // SPLIT
-    copy_x = pltpu.make_async_copy(x_hbm, xb_ref, x_sem)
-    copy_x.start()
     copies = []
-    for q in range(SPLIT):
-        span = pl.ds(q * each, each)
-        copies.append(pltpu.make_async_copy(w_hbm.at[span], wv_ref.at[span], w_sem.at[q]))
-        copies[-1].start()
+    if weights:
+        xb_ref, wv_ref = (x_hbm, w_hbm)
+    else:
+        xb_ref, wv_ref, x_sem, w_sem = own
+        copy_x = pltpu.make_async_copy(x_hbm, xb_ref, x_sem)
+        copy_x.start()
+        for q in range(SPLIT):
+            span = pl.ds(q * each, each)
+            copies.append(pltpu.make_async_copy(w_hbm.at[span], wv_ref.at[span], w_sem.at[q]))
+            copies[-1].start()
     group = group_ref[0]
     if weights:
         weights_of(group, groups, retain_ref, outs[-2], outs[-1])
         outs = outs[:-2]
     xe_ref[:LEAD, :] = halo_ref[...].astype(jnp.float32)
-    copy_x.wait()
+    if not weights:
+        copy_x.wait()
     xe_ref[LEAD:, :] = xb_ref[...].astype(jnp.float32)
     tall = share + LEAD
     for i, by in enumerate(offsets):
@@ -51,7 +59,8 @@
         ]
     total = None
     for q in range(SPLIT):
-        copies[q].wait()
+        if not weights:
+            copies[q].wait()
         window = jnp.concatenate(
             [
                 jnp.concatenate(
@@ -79,9 +88,9 @@
 
 
 def weights_of(group, groups, retain_ref, weight_ref, stats_ref):
-    rows = retain_ref.shape[1]
+    rows = retain_ref.shape[0]
     share = rows // groups
-    logs = jnp.log(retain_ref[...])
+    logs = jnp.log(retain_ref[...].reshape(1, rows))
     lane = lax.broadcasted_iota(jnp.int32, (share, rows), 1)
     row = lax.broadcasted_iota(jnp.int32, (share, rows), 0)
     spread = jnp.broadcast_to(logs, (share, rows))
@@ -112,28 +121,32 @@
     if weights:
         shapes.append(jax.ShapeDtypeStruct((share, TILE), jnp.float32))
         shapes.append(jax.ShapeDtypeStruct((1, TILE), jnp.float32))
-    any_space = pl.BlockSpec(memory_space=pltpu.HBM)
-    return pl.pallas_call(
-        lambda *refs: fir_body(offsets, weights, *refs),
-        out_shape=shapes,
-        in_specs=[SMEM, VMEM, any_space, any_space, VMEM],
-        out_specs=[VMEM] * len(shapes),
-        scratch_shapes=[
+    large = VMEM if weights else pl.BlockSpec(memory_space=pltpu.HBM)
+    scratch = [
+        pltpu.VMEM((rows + LEAD, width), jnp.float32),
+        pltpu.VMEM((tall * len(offsets), width), jnp.float32),
+    ]
+    if not weights:
+        scratch += [
             pltpu.VMEM((rows, width), samples.dtype),
-            pltpu.VMEM((rows + LEAD, width), jnp.float32),
-            pltpu.VMEM((tall * len(offsets), width), jnp.float32),
             pltpu.VMEM(taps_weight.shape, taps_weight.dtype),
             pltpu.SemaphoreType.DMA,
             pltpu.SemaphoreType.DMA((SPLIT,)),
-        ],
-        compiler_params=pltpu.CompilerParams(vmem_limit_bytes=60 << 20),
+        ]
+    return pl.pallas_call(
+        lambda *refs: fir_body(offsets, weights, *refs),
+        out_shape=shapes,
+        in_specs=[SMEM, VMEM, large, large] + [VMEM] * weights,
+        out_specs=[VMEM] * len(shapes),
+        scratch_shapes=scratch,
+        compiler_params=pltpu.CompilerParams(vmem_limit_bytes=(16 if weights else 60) << 20),
         cost_estimate=pl.CostEstimate(
             flops=2 * share * len(offsets) * taps * width * beams,
             bytes_accessed=6 << 20,
             transcendentals=0,
         ),
         name="fir_rest" if weights else "fir_sent",
-    )(group, halo, samples, taps_weight, retain)
+    )(group, halo, samples, taps_weight, *([retain] if weights else []))
 
 
 def ring(array, by):
@@ -292,10 +305,12 @@
 def factor_tile(rows):
     lane = lax.broadcasted_iota(jnp.int32, (8, TILE), 1)
     sub = lax.broadcasted_iota(jnp.int32, (8, TILE), 0)
-    rows, out = (list(rows), [])
-    for k in range(len(rows)):
+    rows, out, n = (list(rows), [], len(rows))
+    cols = [spread_lane(rows[0], c) for c in range(8)]
+    for k in range(n):
         base = 8 * k
-        cols = [spread_lane(rows[k], base + c) for c in range(8)]
+        last = k + 1 == n
+        after = [] if last else [spread_lane(rows[k], base + 8 + c) for c in range(8)]
         inside = (lane >= base) & (lane < base + 8)
         g = jnp.where(inside, jnp.where(lane - base == sub, 1.0, 0.0), rows[k])
         w = g
@@ -304,24 +319,37 @@
         for c in range(8):
             pivot = spread_row(cols[c], c)
             inverse = 1.0 / pivot
-            scaled = cols[c] * inverse
-            other = jnp.where(sub == c, 0.0, scaled)
-            below = jnp.where(sub > c, scaled, 0.0)
+            other = jnp.where(sub == c, 0.0, cols[c])
+            below = jnp.where(sub > c, cols[c], 0.0)
             for s in range(c + 1, 8):
-                cols[s] = cols[s] - other * spread_row(cols[s], c)
-            g = g - other * spread_row(g, c)
-            w = w - below * spread_row(w, c)
+                cols[s] = cols[s] - (other * spread_row(cols[s], c)) * inverse
+            scaled = other * inverse
+            g = g - scaled * spread_row(g, c)
+            w = w - (below * inverse) * spread_row(w, c)
+            after = [v - scaled * spread_row(v, c) for v in after]
             pivots = jnp.where(sub == c, pivot, pivots)
             inverses = jnp.where(sub == c, inverse, inverses)
         z = g * inverses
         out.append(jnp.where(lane < base + 8, w * lax.rsqrt(pivots), 0.0))
-        if k + 1 < len(rows):
-            z_rows = [spread_row(z, c) for c in range(8)]
-            for i in range(k + 1, len(rows)):
-                m = [spread_lane(rows[i], base + c) * z_rows[c] for c in range(8)]
-                total = ((m[0] + m[1]) + (m[2] + m[3])) + ((m[4] + m[5]) + (m[6] + m[7]))
-                rows[i] = jnp.where(inside, 0.0, rows[i]) - total
+        if last:
+            break
+        z_rows = [spread_row(z, c) for c in range(8)]
+        for i in range(k + 1, n):
+            factors = [spread_lane(rows[i], base + c) for c in range(8)]
+            if i == k + 1:
+                new = []
+                for s in range(8):
+                    v = after[s] * inverses
+                    m = [factors[c] * spread_row(v, c) for c in range(8)]
+                    new.append(spread_lane(rows[i], base + 8 + s) - sum_of(m))
+                cols = new
+            m = [factors[c] * z_rows[c] for c in range(8)]
+            rows[i] = jnp.where(inside, 0.0, rows[i]) - sum_of(m)
     return out
+
+
+def sum_of(m):
+    return ((m[0] + m[1]) + (m[2] + m[3])) + ((m[4] + m[5]) + (m[6] + m[7]))
 
 
 def factor_body(p_ref, b_ref, o_ref, s_ref, d_ref, l_ref):
@@ -427,7 +455,7 @@
     half = share // 2
     with jax.named_scope("halo"):
         halo = shifted(samples[row_count - LEAD :], "tm", 1)
-    args = (group, halo, samples, taps_weight, retain.reshape(1, row_count))
+    args = (group, halo, samples, taps_weight, retain)
     down, up, far_down, far_up = fir(
         (-1, -3, 1, 3, 4), (2 * share, 2 * share, half, half), False, *args
     )

time: 161 us -> 153 us (0.950)
  Pallas kernels: 37.2 us -> 28.6 us
    pallas_call x1, Pallas kernels: 23.8 us -> 18.8 us  [whitened_share(): pl.pallas_call(factor_body, out_shape=jax.ShapeDtypeStruct((n, share), jn...]
    pallas_call x2, Pallas kernels: 11.1 us -> 7.47 us  [fir(): pl.pallas_call(lambda *refs: fir_body(offsets, weights, *refs), out_shape...]
  transfers between devices with their start and end apart: 7 -> 7, of which waited for: 6 -> 6; matrix products, arithmetic and copies ran while one was open for 1% -> 0% of each run, Pallas kernels for 3% -> 1%
where the time goes in v3:
time: 153 us; the launch traced here: 152 us
  blocking collectives  84.7 us (55%)
  Pallas kernels  28.6 us (19%)
  waiting for transfers between devices  20.2 us (13%)
  starting transfers between devices  13.8 us (9%)
  local copies, waits for them, and re-layouts  4.25 us (3%)
    all_to_all x1, blocking collectives, local(): packed_estimate = lax.all_to_all(replicated(returned, groups), 'elem', 0, 0)  23.3 us
    all_to_all x1, blocking collectives, local(): lax.all_to_all(packed.reshape(groups, packed.shape[0] // groups, TILE), '...  21.9 us
    pallas_call x1, Pallas kernels, whitened_share(): pl.pallas_call(factor_body, out_shape=jax.ShapeDtypeStruct((n, share), jn...  18.8 us
    ppermute x6, waiting for transfers between devices, ring(): lax.ppermute(array, 'elem', [(i, (i + by) % size) for i in range(size)])  17.2 us
    all_to_all x1, blocking collectives, local(): lax.all_to_all(mine.reshape(groups, mine.shape[0] // groups, share), 'ele...  14.6 us
    all_to_all x1, blocking collectives, local(): received = lax.all_to_all(spread, 'tm', 0, 0, tiled=True)  13.7 us
    ppermute x6, starting transfers between devices, ring(): lax.ppermute(array, 'elem', [(i, (i + by) % size) for i in range(size)])  11.9 us
    all_to_all x1, blocking collectives, local(): returned = lax.all_to_all(estimate, 'tm', 0, 0, tiled=True)  11.3 us
  transfers between devices with their start and end apart: 7, of which 6 were waited for; matrix products, arithmetic and copies ran while one was open for 0% of the time, Pallas kernels for 1%

profile of v3, /device:TPU:2, one launch (start us, length us, event | category | flops | bytes accessed | tf_op | source)
XLA Modules:
  0.0 151.6 jit_solution(15719664738385247210)
XLA Ops:
  0.0 0.0 copy-start.1
  0.0 0.0 copy-start.4
  0.0 0.8 slice.3
  0.8 1.9 %collective-permute-start = (bf16[16,256]{1,0:T(8,128)(2,1)S(1)}, bf16[16,256]{1,0:T(8,128)(2,1)S(1)}, u32[]{:S(2)}, u32[]{:S(2)}) collective-permute-start(bf16[16,256]{1,0:T(8,128)(2,1)S(1)} %slice.3), channel_id=1, source_target_pairs={{0,1},{1,2},{2,3},{3,4},{4,5},{5,6},{6,7},{7,8},{8,9},{9,10},{10,1... | collective-permute-start | bytes 24584 | tf_op jit(solution)/shard_map/halo/ppermute | solution.py:18
  2.7 3.0 %collective-permute-done.refs_1_ = bf16[16,256]{1,0:T(8,128)(2,1)S(1)} collective-permute-done((bf16[16,256]{1,0:T(8,128)(2,1)S(1)}, bf16[16,256]{1,0:T(8,128)(2,1)S(1)}, u32[]{:S(2)}, u32[]{:S(2)}) %collective-permute-start) | collective-permute-done | bytes 8224 | tf_op jit(solution)/shard_map/halo/ppermute | solution.py:18
  5.7 0.0 copy-start.2
  5.7 0.6 copy-done.2
  6.3 6.0 %fir_sent.1 = (f32[192,512]{1,0:T(8,128)}, f32[192,512]{1,0:T(8,128)}, f32[48,512]{1,0:T(8,128)}, f32[48,512]{1,0:T(8,128)}) custom-call(s32[1]{0:T(128)} %bitcast.refs_0_, bf16[16,256]{1,0:T(8,128)(2,1)} %copy-done.2, bf16[768,256]{1,0:T(8,128)(2,1)} %refs_2_.3, bf16[16,256,512]{2,1,0:T(8,128)(2,1)} %refs_3_.3), custom_call_target="tpu_custom_call" | custom-call | flops 2013265920 | bytes 6291456 | tf_op jit(solution)/shard_map/fir_sent/pallas_call | solution.py:136
  12.3 5.9 %collective-permute-start.1 = (f32[192,512]{1,0:T(8,128)}, f32[192,512]{1,0:T(8,128)S(1)}, u32[]{:S(2)}, u32[]{:S(2)}) collective-permute-start(f32[192,512]{1,0:T(8,128)} %get-tuple-element.18), channel_id=1, source_target_pairs={{0,224},{32,0},{64,32},{96,64},{128,96},{160,128},{192,160},{224,1... | collective-permute-start | bytes 1179656 | tf_op jit(solution)/shard_map/beams_near/ppermute | solution.py:154
  18.3 0.0 collective-permute-start.2
  18.3 2.5 %collective-permute-start.3 = (f32[48,512]{1,0:T(8,128)}, f32[48,512]{1,0:T(8,128)S(1)}, u32[]{:S(2)}, u32[]{:S(2)}) collective-permute-start(f32[48,512]{1,0:T(8,128)} %get-tuple-element.20), channel_id=1, source_target_pairs={{0,192},{32,224},{64,0},{96,32},{128,64},{160,96},{192,128},{224,1... | collective-permute-start | bytes 294920 | tf_op jit(solution)/shard_map/beams_near/ppermute | solution.py:154
  20.7 0.5 collective-permute-start.4
  21.2 0.0 copy-done.1
  21.2 0.0 copy-done.4
  21.2 0.0 copy-start
  21.2 2.2 %copy-done = bf16[16,256,512]{2,1,0:T(8,128)(2,1)S(1)} copy-done((bf16[16,256,512]{2,1,0:T(8,128)(2,1)S(1)}, bf16[16,256,512]{2,1,0:T(8,128)(2,1)}, u32[]{:S(2)}) %copy-start) | copy-done | bytes 4194328
  23.4 0.0 copy-start.3
  23.4 0.7 copy-done.3
  24.1 1.5 fir_rest.1
  25.6 5.1 %collective-permute-done.3.far_down_ref = f32[48,512]{1,0:T(8,128)S(1)} collective-permute-done((f32[48,512]{1,0:T(8,128)}, f32[48,512]{1,0:T(8,128)S(1)}, u32[]{:S(2)}, u32[]{:S(2)}) %collective-permute-start.3) | collective-permute-done | bytes 98336 | tf_op jit(solution)/shard_map/beams_near/ppermute | solution.py:154
  30.6 2.0 %collective-permute-done.4.far_up_ref = f32[48,512]{1,0:T(8,128)S(1)} collective-permute-done((f32[48,512]{1,0:T(8,128)}, f32[48,512]{1,0:T(8,128)S(1)}, u32[]{:S(2)}, u32[]{:S(2)}) %collective-permute-start.4) | collective-permute-done | bytes 98336 | tf_op jit(solution)/shard_map/beams_near/ppermute | solution.py:154
  32.6 0.0 collective-permute-done.1.down_ref
  32.6 0.3 collective-permute-done.2.up_ref
  32.9 0.1 relay_sums.1
  33.0 2.3 %collective-permute-start.5 = (f32[96,512]{1,0:T(8,128)S(1)}, f32[96,512]{1,0:T(8,128)S(1)}, u32[]{:S(2)}, u32[]{:S(2)}) collective-permute-start(f32[96,512]{1,0:T(8,128)S(1)} %get-tuple-element.22), channel_id=1, source_target_pairs={{0,192},{32,224},{64,0},{96,32},{128,64},{160,96},{192,128},{224,1... | collective-permute-start | bytes 589832 | tf_op jit(solution)/shard_map/beams_far/ppermute | solution.py:154
  35.3 0.7 collective-permute-start.6
  36.0 5.9 %collective-permute-done.5.low_ref = f32[96,512]{1,0:T(8,128)S(1)} collective-permute-done((f32[96,512]{1,0:T(8,128)S(1)}, f32[96,512]{1,0:T(8,128)S(1)}, u32[]{:S(2)}, u32[]{:S(2)}) %collective-permute-start.5) | collective-permute-done | bytes 196640 | tf_op jit(solution)/shard_map/beams_far/ppermute | solution.py:154
  41.9 3.9 %collective-permute-done.6.high_ref = f32[96,512]{1,0:T(8,128)S(1)} collective-permute-done((f32[96,512]{1,0:T(8,128)S(1)}, f32[96,512]{1,0:T(8,128)S(1)}, u32[]{:S(2)}, u32[]{:S(2)}) %collective-permute-start.6) | collective-permute-done | bytes 196640 | tf_op jit(solution)/shard_map/beams_far/ppermute | solution.py:154
  45.8 0.8 packed_gram.1
  46.6 21.9 %all_to_all.25.p_ref = f32[8,160,128]{2,1,0:T(8,128)S(1)} all-to-all(f32[8,160,128]{2,1,0:T(8,128)S(1)} %bitcast.3), channel_id=1, replica_groups=mesh['elem'=8,'tm'=32] {'elem'}, dimensions={0} | all-to-all | bytes 1310720 | tf_op jit(solution)/shard_map/gram_sum/all_to_all | solution.py:471
  68.5 0.1 spread_share.1
  68.5 13.7 %all_to_all.26.r_ref = f32[32,6,128]{2,1,0:T(8,128)S(1)} all-to-all(f32[32,6,128]{2,1,0:T(8,128)S(1)} %spread_share.1), channel_id=1, replica_groups=mesh['elem'=8,'tm'=32] {'tm'}, dimensions={0} | all-to-all | bytes 196608 | tf_op jit(solution)/shard_map/blocks_out/all_to_all | solution.py:476
  82.2 0.5 decayed_sums.1
  82.8 11.3 %all_to_all.27.r_ref = f32[32,5,128]{2,1,0:T(8,128)S(1)} all-to-all(f32[32,5,128]{2,1,0:T(8,128)S(1)} %decayed_sums.1), channel_id=1, replica_groups=mesh['elem'=8,'tm'=32] {'tm'}, dimensions={0} | all-to-all | bytes 163840 | tf_op jit(solution)/shard_map/blocks_back/all_to_all | solution.py:479
  94.0 0.1 replicated.1
  94.1 23.3 %all_to_all.28.p_ref = f32[8,160,128]{2,1,0:T(8,128)S(1)} all-to-all(f32[8,160,128]{2,1,0:T(8,128)S(1)} %replicated.1), channel_id=1, replica_groups=mesh['elem'=8,'tm'=32] {'elem'}, dimensions={0} | all-to-all | bytes 1310720 | tf_op jit(solution)/shard_map/gram_gather/all_to_all | solution.py:481
  117.4 18.8 %whitened_share.1 = f32[512,96]{1,0:T(8,128)S(1)} custom-call(f32[8,160,128]{2,1,0:T(8,128)S(1)} %all_to_all.28.p_ref, f32[96,512]{1,0:T(8,128)S(1)} %get-tuple-element.26.b_ref), custom_call_target="tpu_custom_call" | custom-call | flops 1610612736 | bytes 1048576 | tf_op jit(solution)/shard_map/whitened_share/pallas_call | solution.py:416
  136.2 14.6 %all_to_all.29.r_ref = f32[8,64,96]{2,1,0:T(8,128)S(1)} all-to-all(f32[8,64,96]{2,1,0:T(8,128)S(1)} %bitcast.4), channel_id=1, replica_groups=mesh['elem'=8,'tm'=32] {'elem'}, dimensions={0} | all-to-all | bytes 393216 | tf_op jit(solution)/shard_map/whitened_out/all_to_all | solution.py:484
  150.8 0.8 joined.1
Async XLA Ops:
  0.0 21.2 %copy-start.1 = (bf16[768,256]{1,0:T(8,128)(2,1)S(1)}, bf16[768,256]{1,0:T(8,128)(2,1)}, u32[]{:S(2)}) copy-start(bf16[768,256]{1,0:T(8,128)(2,1)} %refs_2_.3) | copy-start | bytes 1179652
  0.0 21.2 %copy-start.4 = (f32[768]{0:T(1024)S(1)}, f32[768]{0:T(1024)}, u32[]{:S(2)}) copy-start(f32[768]{0:T(1024)} %refs_4_.1) | copy-start | bytes 9220
  0.8 5.0 %collective-permute-start = (bf16[16,256]{1,0:T(8,128)(2,1)S(1)}, bf16[16,256]{1,0:T(8,128)(2,1)S(1)}, u32[]{:S(2)}, u32[]{:S(2)}) collective-permute-start(bf16[16,256]{1,0:T(8,128)(2,1)S(1)} %slice.3), channel_id=1, source_target_pairs={{0,1},{1,2},{2,3},{3,4},{4,5},{5,6},{6,7},{7,8},{8,9},{9,10},{10,1... | collective-permute-start | bytes 24584 | tf_op jit(solution)/shard_map/halo/ppermute | solution.py:18
  5.7 0.6 copy-start.2
  12.3 20.3 %collective-permute-start.1 = (f32[192,512]{1,0:T(8,128)}, f32[192,512]{1,0:T(8,128)S(1)}, u32[]{:S(2)}, u32[]{:S(2)}) collective-permute-start(f32[192,512]{1,0:T(8,128)} %get-tuple-element.18), channel_id=1, source_target_pairs={{0,224},{32,0},{64,32},{96,64},{128,96},{160,128},{192,160},{224,1... | collective-permute-start | bytes 1179656 | tf_op jit(solution)/shard_map/beams_near/ppermute | solution.py:154
  18.3 14.7 %collective-permute-start.2 = (f32[192,512]{1,0:T(8,128)}, f32[192,512]{1,0:T(8,128)S(1)}, u32[]{:S(2)}, u32[]{:S(2)}) collective-permute-start(f32[192,512]{1,0:T(8,128)} %get-tuple-element.19), channel_id=1, source_target_pairs={{0,32},{32,64},{64,96},{96,128},{128,160},{160,192},{192,224},{224... | collective-permute-start | bytes 1179656 | tf_op jit(solution)/shard_map/beams_near/ppermute | solution.py:154
  18.3 12.4 %collective-permute-start.3 = (f32[48,512]{1,0:T(8,128)}, f32[48,512]{1,0:T(8,128)S(1)}, u32[]{:S(2)}, u32[]{:S(2)}) collective-permute-start(f32[48,512]{1,0:T(8,128)} %get-tuple-element.20), channel_id=1, source_target_pairs={{0,192},{32,224},{64,0},{96,32},{128,64},{160,96},{192,128},{224,1... | collective-permute-start | bytes 294920 | tf_op jit(solution)/shard_map/beams_near/ppermute | solution.py:154
  20.7 11.9 %collective-permute-start.4 = (f32[48,512]{1,0:T(8,128)}, f32[48,512]{1,0:T(8,128)S(1)}, u32[]{:S(2)}, u32[]{:S(2)}) collective-permute-start(f32[48,512]{1,0:T(8,128)} %get-tuple-element.21), channel_id=1, source_target_pairs={{0,64},{32,96},{64,128},{96,160},{128,192},{160,224},{192,0},{224,... | collective-permute-start | bytes 294920 | tf_op jit(solution)/shard_map/beams_near/ppermute | solution.py:154
  21.2 2.2 %copy-start = (bf16[16,256,512]{2,1,0:T(8,128)(2,1)S(1)}, bf16[16,256,512]{2,1,0:T(8,128)(2,1)}, u32[]{:S(2)}) copy-start(bf16[16,256,512]{2,1,0:T(8,128)(2,1)} %refs_3_.3) | copy-start | bytes 12582916
  23.4 0.7 copy-start.3
  33.0 8.9 %collective-permute-start.5 = (f32[96,512]{1,0:T(8,128)S(1)}, f32[96,512]{1,0:T(8,128)S(1)}, u32[]{:S(2)}, u32[]{:S(2)}) collective-permute-start(f32[96,512]{1,0:T(8,128)S(1)} %get-tuple-element.22), channel_id=1, source_target_pairs={{0,192},{32,224},{64,0},{96,32},{128,64},{160,96},{192,128},{224,1... | collective-permute-start | bytes 589832 | tf_op jit(solution)/shard_map/beams_far/ppermute | solution.py:154
  35.3 10.5 %collective-permute-start.6 = (f32[96,512]{1,0:T(8,128)S(1)}, f32[96,512]{1,0:T(8,128)S(1)}, u32[]{:S(2)}, u32[]{:S(2)}) collective-permute-start(f32[96,512]{1,0:T(8,128)S(1)} %get-tuple-element.23), channel_id=1, source_target_pairs={{0,64},{32,96},{64,128},{96,160},{128,192},{160,224},{192,0},{224,... | collective-permute-start | bytes 589832 | tf_op jit(solution)/shard_map/beams_far/ppermute | solution.py:154

commit v4 on v3

--- a/solution.py
+++ b/solution.py
@@ -215,7 +215,8 @@
     )(keep, down, up, low, high, weight)
 
 
-def share_body(stats_ref, p_ref, o_ref):
+def share_body(stats_ref, p_ref, b_ref, o_ref, c_ref):
+    c_ref[...] = b_ref[...]
     groups, rows, _ = p_ref.shape
     ways = o_ref.shape[0]
     total = p_ref[0]
@@ -227,19 +228,28 @@
     o_ref[:, tiles, :] = jnp.broadcast_to(stats_ref[...], (ways, TILE))
 
 
-def spread_share(parts, stats, ways):
+def spread_share(parts, stats, my_beams, ways):
     groups, rows, _ = parts.shape
     return pl.pallas_call(
         share_body,
-        out_shape=jax.ShapeDtypeStruct((ways, rows // ways + 1, TILE), jnp.float32),
-        in_specs=[VMEM, VMEM],
-        out_specs=VMEM,
+        out_shape=(
+            jax.ShapeDtypeStruct((ways, rows // ways + 1, TILE), jnp.float32),
+            jax.ShapeDtypeStruct(my_beams.shape, jnp.float32),
+        ),
+        in_specs=[VMEM] * 3,
+        out_specs=(VMEM, VMEM),
         compiler_params=pltpu.CompilerParams(vmem_limit_bytes=4 << 20),
         name="spread_share",
-    )(stats, parts)
-
-
-def decay_body(r_ref, o_ref):
+    )(stats, parts, my_beams)
+
+
+def decay_body(r_ref, from_below, from_below2, from_above, from_above2, o_ref, low_ref, high_ref):
+    share = from_below.shape[0]
+    half = share // 2
+    low_ref[:share, :] = from_above[...]
+    low_ref[share:, :] = from_above2[:half, :]
+    high_ref[:share, :] = from_below[...]
+    high_ref[share:, :] = from_below2[half:, :]
     n, tiles, _ = r_ref.shape
     tiles -= 1
     stats = r_ref[:, tiles, :]
@@ -262,19 +272,21 @@
         o_ref[:, s, :] = gram[:, s * TILE : (s + 1) * TILE]
 
 
-def decayed(received):
+def decayed(received, *near):
     n, tiles, _ = received.shape
+    share, beams = near[0].shape
+    packed = jax.ShapeDtypeStruct((share + share // 2, beams), jnp.float32)
     return pl.pallas_call(
         decay_body,
-        out_shape=jax.ShapeDtypeStruct((n, tiles - 1, TILE), jnp.float32),
-        in_specs=[VMEM],
-        out_specs=VMEM,
-        compiler_params=pltpu.CompilerParams(vmem_limit_bytes=4 << 20),
+        out_shape=(jax.ShapeDtypeStruct((n, tiles - 1, TILE), jnp.float32), packed, packed),
+        in_specs=[VMEM] * 5,
+        out_specs=(VMEM,) * 3,
+        compiler_params=pltpu.CompilerParams(vmem_limit_bytes=5 << 20),
         name="decayed_sums",
-    )(received)
-
-
-def replicate_body(r_ref, o_ref):
+    )(received, *near)
+
+
+def replicate_body(r_ref, low_ref, high_ref, o_ref):
     ways, tiles, _ = r_ref.shape
     for s in range(tiles):
         piece = r_ref[:, s, :]
@@ -282,16 +294,16 @@
             o_ref[g, s * ways : (s + 1) * ways, :] = piece
 
 
-def replicated(returned, groups):
+def replicated(returned, groups, low, high):
     ways, tiles, _ = returned.shape
     return pl.pallas_call(
         replicate_body,
         out_shape=jax.ShapeDtypeStruct((groups, ways * tiles, TILE), jnp.float32),
-        in_specs=[VMEM],
+        in_specs=[VMEM] * 3,
         out_specs=VMEM,
         compiler_params=pltpu.CompilerParams(vmem_limit_bytes=4 << 20),
         name="replicated",
-    )(returned)
+    )(returned, low, high)
 
 
 def spread_row(x, r):
@@ -305,7 +317,7 @@
 def factor_tile(rows):
     lane = lax.broadcasted_iota(jnp.int32, (8, TILE), 1)
     sub = lax.broadcasted_iota(jnp.int32, (8, TILE), 0)
-    rows, out, n = (list(rows), [], len(rows))
+    rows, out, done, n = (list(rows), [], [], len(rows))
     cols = [spread_lane(rows[0], c) for c in range(8)]
     for k in range(n):
         base = 8 * k
@@ -330,11 +342,31 @@
             pivots = jnp.where(sub == c, pivot, pivots)
             inverses = jnp.where(sub == c, inverse, inverses)
         z = g * inverses
-        out.append(jnp.where(lane < base + 8, w * lax.rsqrt(pivots), 0.0))
+        y = w * lax.rsqrt(pivots)
+        out.append(jnp.where(lane < base + 8, y, 0.0))
         if last:
             break
         z_rows = [spread_row(z, c) for c in range(8)]
-        for i in range(k + 1, n):
+        panel = (k // 8 + 1) * 8
+        far = k + 1 == panel
+        done.append((y, jnp.where((lane < base + 8) | (lane >= 8 * panel), y, 0.0)))
+        if far:
+            block = jnp.concatenate([d[0] for d in done[-8:]], 0)
+            right = jnp.concatenate([d[1] for d in done[-8:]], 0)
+            rest = jnp.concatenate(rows[panel:], 0)
+            change = lax.dot_general(
+                block[:, 8 * panel :],
+                right,
+                (((0,), (0,)), ((), ())),
+                precision=HI,
+                preferred_element_type=jnp.float32,
+            )
+            cut = (lax.broadcasted_iota(jnp.int32, change.shape, 1) // 64) == k // 8
+            rest = jnp.where(cut, 0.0, rest) - change
+            for i in range(panel, n):
+                rows[i] = rest[8 * (i - panel) : 8 * (i - panel) + 8, :]
+            cols = [spread_lane(rows[k + 1], base + 8 + c) for c in range(8)]
+        for i in range(k + 1, panel):
             factors = [spread_lane(rows[i], base + c) for c in range(8)]
             if i == k + 1:
                 new = []
@@ -352,7 +384,8 @@
     return ((m[0] + m[1]) + (m[2] + m[3])) + ((m[4] + m[5]) + (m[6] + m[7]))
 
 
-def factor_body(p_ref, b_ref, o_ref, s_ref, d_ref, l_ref):
+def factor_body(group_ref, p_ref, *refs):
+    *beam_refs, o_ref, s_ref, d_ref, l_ref, b_ref = refs
     groups, high, _ = p_ref.shape
     ways = 32
     tiles = high // ways
@@ -402,8 +435,10 @@
                 old = s_ref[i * TILE : (i + 1) * TILE, :]
                 s_ref[i * TILE : (i + 1) * TILE, :] = jnp.where(tile_of == k, 0.0, old) - change
 
+    place_beams(group_ref[0], groups, beam_refs, b_ref)
+    mine = o_ref.shape[0]
     o_ref[...] = lax.dot_general(
-        l_ref[...],
+        l_ref[pl.ds(pl.multiple_of(group_ref[0] * mine, 8), mine), :],
         b_ref[...],
         (((1,), (1,)), ((), ())),
         precision=HI,
@@ -411,40 +446,45 @@
     )
 
 
-def whitened_share(packed, my_beams):
-    share, n = my_beams.shape
+def place_beams(group, groups, beam_refs, b_ref):
+    own, below, below2, above, above2, low, high = beam_refs
+    share = own.shape[0]
+    half = share // 2
+
+    def put(by, at, values):
+        owner = lax.rem(group + (by + groups), groups)
+        first = pl.multiple_of(owner * share + at, 8)
+        b_ref[pl.ds(first, values.shape[0]), :] = values
+
+    put(0, 0, own[...])
+    put(1, 0, above[...])
+    put(2, 0, above2[...])
+    put(3, 0, low[:share, :])
+    put(4, 0, low[share:, :])
+    put(4, half, high[share:, :])
+    put(-3, 0, high[:share, :])
+    put(-2, 0, below2[...])
+    put(-1, 0, below[...])
+
+
+def whitened_rows(group, packed, *beams):
+    share, n = beams[0].shape
+    groups = packed.shape[0]
     return pl.pallas_call(
         factor_body,
-        out_shape=jax.ShapeDtypeStruct((n, share), jnp.float32),
-        in_specs=[VMEM, VMEM],
+        out_shape=jax.ShapeDtypeStruct((n // groups, groups * share), jnp.float32),
+        in_specs=[SMEM] + [VMEM] * 8,
         out_specs=VMEM,
         scratch_shapes=[
             pltpu.VMEM((n, n), jnp.float32),
             pltpu.VMEM((TILE, TILE), jnp.float32),
             pltpu.VMEM((n, n), jnp.float32),
+            pltpu.VMEM((groups * share, n), jnp.float32),
         ],
-        compiler_params=pltpu.CompilerParams(vmem_limit_bytes=8 << 20),
+        compiler_params=pltpu.CompilerParams(vmem_limit_bytes=14 << 20),
         cost_estimate=pl.CostEstimate(flops=12 * n**3, bytes_accessed=1 << 20, transcendentals=n),
-        name="whitened_share",
-    )(packed, my_beams)
-
-
-def join_body(r_ref, o_ref):
-    share = r_ref.shape[2]
-    for g in range(r_ref.shape[0]):
-        o_ref[:, g * share : (g + 1) * share] = r_ref[g]
-
-
-def joined(received):
-    groups, mine, share = received.shape
-    return pl.pallas_call(
-        join_body,
-        out_shape=jax.ShapeDtypeStruct((mine, groups * share), jnp.float32),
-        in_specs=[VMEM],
-        out_specs=VMEM,
-        compiler_params=pltpu.CompilerParams(vmem_limit_bytes=3 << 20),
-        name="joined",
-    )(received)
+        name="whitened_rows",
+    )(group, packed, *beams)
 
 
 def local(samples, taps_weight, retain):
@@ -471,18 +511,24 @@
         parts = lax.all_to_all(
             packed.reshape(groups, packed.shape[0] // groups, TILE), "elem", 0, 0
         )
-    spread = spread_share(parts, stats, blocks)
+    spread, own = spread_share(parts, stats, my_beams, blocks)
+    with jax.named_scope("beams_gather"):
+        below, above = (ring(own, 1), ring(own, -1))
+        below2, above2 = (ring(own, 2), ring(own, -2))
     with jax.named_scope("blocks_out"):
         received = lax.all_to_all(spread, "tm", 0, 0, tiled=True)
-    estimate = decayed(received)
+    estimate, low, high = decayed(received, below, below2, above, above2)
+    with jax.named_scope("beams_gather"):
+        low, high = (ring(low, -2), ring(high, 2))
     with jax.named_scope("blocks_back"):
         returned = lax.all_to_all(estimate, "tm", 0, 0, tiled=True)
     with jax.named_scope("gram_gather"):
-        packed_estimate = lax.all_to_all(replicated(returned, groups), "elem", 0, 0)
-    mine = whitened_share(packed_estimate, my_beams)
-    with jax.named_scope("whitened_out"):
-        pieces = lax.all_to_all(mine.reshape(groups, mine.shape[0] // groups, share), "elem", 0, 0)
-    return joined(pieces)
+        packed_estimate = lax.all_to_all(
+            replicated(returned, groups, low, high), "elem", 0, 0
+        )
+    return whitened_rows(
+        group, packed_estimate, own, below, below2, above, above2, low, high
+    )
 
 
 def solution(mesh):

time: 153 us -> 149 us (0.974)
  blocking collectives: 84.7 us -> 71.5 us
  starting transfers between devices: 13.8 us -> 21.8 us
  waiting for transfers between devices: 20.2 us -> 23.5 us
    all_to_all x2 -> x1, blocking collectives: 37.9 us -> 24 us  [local(): lax.all_to_all(replicated(returned, groups, low, high), 'elem', 0, 0)]
    ppermute x6 -> x12, starting transfers between devices: 11.9 us -> 19.9 us  [ring(): lax.ppermute(array, 'elem', [(i, (i + by) % size) for i in range(size)])]
    ppermute x6 -> x12, waiting for transfers between devices: 17.2 us -> 20.5 us  [ring(): lax.ppermute(array, 'elem', [(i, (i + by) % size) for i in range(size)])]
    pallas_call x4 -> x3, Pallas kernels: 20.2 us -> 19.3 us  [the longest x1 18.7 us: whitened_rows(): pl.pallas_call(factor_body, out_shape=jax.ShapeDtypeStruct((n // groups,...]
  transfers between devices with their start and end apart: 7 -> 13, of which waited for: 6 -> 8; matrix products, arithmetic and copies ran while one was open for 0% -> 0% of each run, Pallas kernels for 1% -> 1%
where the time goes in v4:
time: 149 us
  blocking collectives  71.5 us (48%)
  Pallas kernels  27.7 us (19%)
  waiting for transfers between devices  23.5 us (16%)
  starting transfers between devices  21.8 us (15%)
  local copies, waits for them, and re-layouts  4.25 us (3%)
    all_to_all x1, blocking collectives, local(): lax.all_to_all(replicated(returned, groups, low, high), 'elem', 0, 0)  24 us
    all_to_all x1, blocking collectives, local(): lax.all_to_all(packed.reshape(groups, packed.shape[0] // groups, TILE), '...  21.9 us
    ppermute x12, waiting for transfers between devices, ring(): lax.ppermute(array, 'elem', [(i, (i + by) % size) for i in range(size)])  20.5 us
    ppermute x12, starting transfers between devices, ring(): lax.ppermute(array, 'elem', [(i, (i + by) % size) for i in range(size)])  19.9 us
    pallas_call x1, Pallas kernels, whitened_rows(): pl.pallas_call(factor_body, out_shape=jax.ShapeDtypeStruct((n // groups,...  18.7 us
    all_to_all x1, blocking collectives, local(): received = lax.all_to_all(spread, 'tm', 0, 0, tiled=True)  13.6 us
    all_to_all x1, blocking collectives, local(): returned = lax.all_to_all(estimate, 'tm', 0, 0, tiled=True)  12.1 us
    pallas_call x2, Pallas kernels, fir(): pl.pallas_call(lambda *refs: fir_body(offsets, weights, *refs), out_shape...  7.46 us
  transfers between devices with their start and end apart: 13, of which 8 were waited for; matrix products, arithmetic and copies ran while one was open for 0% of the time, Pallas kernels for 1%

profile of v4, /device:TPU:2, one launch (start us, length us, event | category | flops | bytes accessed | tf_op | source)
XLA Modules:
  0.0 148.9 jit_solution(12045844216720958311)
XLA Ops:
  0.0 0.0 copy-start.1
  0.0 0.0 copy-start.4
  0.0 0.8 slice.3
  0.8 1.9 %collective-permute-start = (bf16[16,256]{1,0:T(8,128)(2,1)S(1)}, bf16[16,256]{1,0:T(8,128)(2,1)S(1)}, u32[]{:S(2)}, u32[]{:S(2)}) collective-permute-start(bf16[16,256]{1,0:T(8,128)(2,1)S(1)} %slice.3), channel_id=1, source_target_pairs={{0,1},{1,2},{2,3},{3,4},{4,5},{5,6},{6,7},{7,8},{8,9},{9,10},{10,1... | collective-permute-start | bytes 24584 | tf_op jit(solution)/shard_map/halo/ppermute | solution.py:18
  2.7 3.0 %collective-permute-done.refs_1_ = bf16[16,256]{1,0:T(8,128)(2,1)S(1)} collective-permute-done((bf16[16,256]{1,0:T(8,128)(2,1)S(1)}, bf16[16,256]{1,0:T(8,128)(2,1)S(1)}, u32[]{:S(2)}, u32[]{:S(2)}) %collective-permute-start) | collective-permute-done | bytes 8224 | tf_op jit(solution)/shard_map/halo/ppermute | solution.py:18
  5.7 0.0 copy-start.2
  5.7 0.6 copy-done.2
  6.3 6.0 %fir_sent.1 = (f32[192,512]{1,0:T(8,128)}, f32[192,512]{1,0:T(8,128)}, f32[48,512]{1,0:T(8,128)}, f32[48,512]{1,0:T(8,128)}) custom-call(s32[1]{0:T(128)} %bitcast.refs_0_.group_ref, bf16[16,256]{1,0:T(8,128)(2,1)} %copy-done.2, bf16[768,256]{1,0:T(8,128)(2,1)} %refs_2_.3, bf16[16,256,512]{2,1,0:T(8,128)(2,1)} %refs_3_.3), custom_call_target="tpu_custom_call" | custom-call | flops 2013265920 | bytes 6291456 | tf_op jit(solution)/shard_map/fir_sent/pallas_call | solution.py:136
  12.3 5.9 %collective-permute-start.1 = (f32[192,512]{1,0:T(8,128)}, f32[192,512]{1,0:T(8,128)S(1)}, u32[]{:S(2)}, u32[]{:S(2)}) collective-permute-start(f32[192,512]{1,0:T(8,128)} %get-tuple-element.23), channel_id=1, source_target_pairs={{0,224},{32,0},{64,32},{96,64},{128,96},{160,128},{192,160},{224,1... | collective-permute-start | bytes 1179656 | tf_op jit(solution)/shard_map/beams_near/ppermute | solution.py:154
  18.3 0.0 collective-permute-start.2
  18.3 2.5 %collective-permute-start.3 = (f32[48,512]{1,0:T(8,128)}, f32[48,512]{1,0:T(8,128)S(1)}, u32[]{:S(2)}, u32[]{:S(2)}) collective-permute-start(f32[48,512]{1,0:T(8,128)} %get-tuple-element.25), channel_id=1, source_target_pairs={{0,192},{32,224},{64,0},{96,32},{128,64},{160,96},{192,128},{224,1... | collective-permute-start | bytes 294920 | tf_op jit(solution)/shard_map/beams_near/ppermute | solution.py:154
  20.7 0.5 collective-permute-start.4
  21.2 0.0 copy-done.1
  21.2 0.0 copy-done.4
  21.2 0.0 copy-start
  21.2 2.2 %copy-done = bf16[16,256,512]{2,1,0:T(8,128)(2,1)S(1)} copy-done((bf16[16,256,512]{2,1,0:T(8,128)(2,1)S(1)}, bf16[16,256,512]{2,1,0:T(8,128)(2,1)}, u32[]{:S(2)}) %copy-start) | copy-done | bytes 4194328
  23.4 0.0 copy-start.3
  23.4 0.7 copy-done.3
  24.1 1.5 fir_rest.1
  25.6 5.1 %collective-permute-done.3.far_down_ref = f32[48,512]{1,0:T(8,128)S(1)} collective-permute-done((f32[48,512]{1,0:T(8,128)}, f32[48,512]{1,0:T(8,128)S(1)}, u32[]{:S(2)}, u32[]{:S(2)}) %collective-permute-start.3) | collective-permute-done | bytes 98336 | tf_op jit(solution)/shard_map/beams_near/ppermute | solution.py:154
  30.6 2.0 %collective-permute-done.4.far_up_ref = f32[48,512]{1,0:T(8,128)S(1)} collective-permute-done((f32[48,512]{1,0:T(8,128)}, f32[48,512]{1,0:T(8,128)S(1)}, u32[]{:S(2)}, u32[]{:S(2)}) %collective-permute-start.4) | collective-permute-done | bytes 98336 | tf_op jit(solution)/shard_map/beams_near/ppermute | solution.py:154
  32.6 0.0 collective-permute-done.1.down_ref
  32.6 0.3 collective-permute-done.2.up_ref
  32.9 0.1 relay_sums.1
  33.0 2.3 %collective-permute-start.5 = (f32[96,512]{1,0:T(8,128)S(1)}, f32[96,512]{1,0:T(8,128)S(1)}, u32[]{:S(2)}, u32[]{:S(2)}) collective-permute-start(f32[96,512]{1,0:T(8,128)S(1)} %get-tuple-element.27), channel_id=1, source_target_pairs={{0,192},{32,224},{64,0},{96,32},{128,64},{160,96},{192,128},{224,1... | collective-permute-start | bytes 589832 | tf_op jit(solution)/shard_map/beams_far/ppermute | solution.py:154
  35.3 0.7 collective-permute-start.6
  36.0 5.9 %collective-permute-done.5.low_ref = f32[96,512]{1,0:T(8,128)S(1)} collective-permute-done((f32[96,512]{1,0:T(8,128)S(1)}, f32[96,512]{1,0:T(8,128)S(1)}, u32[]{:S(2)}, u32[]{:S(2)}) %collective-permute-start.5) | collective-permute-done | bytes 196640 | tf_op jit(solution)/shard_map/beams_far/ppermute | solution.py:154
  41.9 3.9 %collective-permute-done.6.high_ref = f32[96,512]{1,0:T(8,128)S(1)} collective-permute-done((f32[96,512]{1,0:T(8,128)S(1)}, f32[96,512]{1,0:T(8,128)S(1)}, u32[]{:S(2)}, u32[]{:S(2)}) %collective-permute-start.6) | collective-permute-done | bytes 196640 | tf_op jit(solution)/shard_map/beams_far/ppermute | solution.py:154
  45.8 0.8 packed_gram.1
  46.6 21.9 %all_to_all.20.p_ref = f32[8,160,128]{2,1,0:T(8,128)S(1)} all-to-all(f32[8,160,128]{2,1,0:T(8,128)S(1)} %bitcast.2), channel_id=1, replica_groups=mesh['elem'=8,'tm'=32] {'elem'}, dimensions={0} | all-to-all | bytes 1310720 | tf_op jit(solution)/shard_map/gram_sum/all_to_all | solution.py:511
  68.5 0.1 spread_share.1
  68.5 0.4 collective-permute-start.10
  69.0 0.8 collective-permute-start.9
  69.7 1.8 %collective-permute-start.8 = (f32[96,512]{1,0:T(8,128)S(1)}, f32[96,512]{1,0:T(8,128)S(1)}, u32[]{:S(2)}, u32[]{:S(2)}) collective-permute-start(f32[96,512]{1,0:T(8,128)S(1)} %get-tuple-element.33.refs_0_), channel_id=1, source_target_pairs={{0,64},{32,96},{64,128},{96,160},{128,192},{160,224},{192,0},{224,... | collective-permute-start | bytes 589832 | tf_op jit(solution)/shard_map/beams_gather/ppermute | solution.py:154
  71.6 2.0 %collective-permute-start.7 = (f32[96,512]{1,0:T(8,128)S(1)}, f32[96,512]{1,0:T(8,128)S(1)}, u32[]{:S(2)}, u32[]{:S(2)}) collective-permute-start(f32[96,512]{1,0:T(8,128)S(1)} %get-tuple-element.33.refs_0_), channel_id=1, source_target_pairs={{0,32},{32,64},{64,96},{96,128},{128,160},{160,192},{192,224},{224... | collective-permute-start | bytes 589832 | tf_op jit(solution)/shard_map/beams_gather/ppermute | solution.py:154
  73.6 13.6 %all_to_all.21.r_ref = f32[32,6,128]{2,1,0:T(8,128)S(1)} all-to-all(f32[32,6,128]{2,1,0:T(8,128)S(1)} %get-tuple-element.32), channel_id=1, replica_groups=mesh['elem'=8,'tm'=32] {'tm'}, dimensions={0} | all-to-all | bytes 196608 | tf_op jit(solution)/shard_map/blocks_out/all_to_all | solution.py:519
  87.2 0.0 collective-permute-done.10.from_above2.refs_4_
  87.2 0.0 collective-permute-done.9.from_above.refs_3_
  87.2 0.0 collective-permute-done.8.from_below2.refs_2_
  87.2 0.0 collective-permute-done.7.from_below.refs_1_
  87.2 0.6 decayed_sums.1
  87.8 1.6 %collective-permute-start.11 = (f32[144,512]{1,0:T(8,128)S(1)}, f32[144,512]{1,0:T(8,128)S(1)}, u32[]{:S(2)}, u32[]{:S(2)}) collective-permute-start(f32[144,512]{1,0:T(8,128)S(1)} %get-tuple-element.35), channel_id=1, source_target_pairs={{0,192},{32,224},{64,0},{96,32},{128,64},{160,96},{192,128},{224,1... | collective-permute-start | bytes 884744 | tf_op jit(solution)/shard_map/beams_gather/ppermute | solution.py:154
  89.4 1.4 collective-permute-start.12
  90.8 12.1 %all_to_all.22.r_ref = f32[32,5,128]{2,1,0:T(8,128)S(1)} all-to-all(f32[32,5,128]{2,1,0:T(8,128)S(1)} %get-tuple-element.34), channel_id=1, replica_groups=mesh['elem'=8,'tm'=32] {'tm'}, dimensions={0} | all-to-all | bytes 163840 | tf_op jit(solution)/shard_map/blocks_back/all_to_all | solution.py:524
  102.8 1.3 collective-permute-done.11.low_ref.refs_5_
  104.2 2.0 %collective-permute-done.12.high_ref.refs_6_ = f32[144,512]{1,0:T(8,128)S(1)} collective-permute-done((f32[144,512]{1,0:T(8,128)S(1)}, f32[144,512]{1,0:T(8,128)S(1)}, u32[]{:S(2)}, u32[]{:S(2)}) %collective-permute-start.12) | collective-permute-done | bytes 294944 | tf_op jit(solution)/shard_map/beams_gather/ppermute | solution.py:154
  106.2 0.1 replicated.1
  106.3 24.0 %all_to_all.23.p_ref = f32[8,160,128]{2,1,0:T(8,128)S(1)} all-to-all(f32[8,160,128]{2,1,0:T(8,128)S(1)} %replicated.1), channel_id=1, replica_groups=mesh['elem'=8,'tm'=32] {'elem'}, dimensions={0} | all-to-all | bytes 1310720 | tf_op jit(solution)/shard_map/gram_gather/all_to_all | solution.py:526
  130.2 18.7 %whitened_rows.1 = f32[64,768]{1,0:T(8,128)} custom-call(s32[1]{0:T(128)} %bitcast.refs_0_.group_ref, f32[8,160,128]{2,1,0:T(8,128)S(1)} %all_to_all.23.p_ref, f32[96,512]{1,0:T(8,128)S(1)} %get-tuple-element.33.refs_0_, f32[96,512]{1,0:T(8,128)S(1)} %collective-permute-done.7.from_below.refs_1_, f32[96,512]{1,0:T(8,128)S(1)} %collective-permute-done.8.from_below2.refs_2_, ...), custom_call_target="tpu_custom_call" | custom-call | flops 1610612736 | bytes 1048576 | tf_op jit(solution)/shard_map/whitened_rows/pallas_call | solution.py:473
Async XLA Ops:
  0.0 21.2 %copy-start.1 = (bf16[768,256]{1,0:T(8,128)(2,1)S(1)}, bf16[768,256]{1,0:T(8,128)(2,1)}, u32[]{:S(2)}) copy-start(bf16[768,256]{1,0:T(8,128)(2,1)} %refs_2_.3) | copy-start | bytes 1179652
  0.0 21.2 %copy-start.4 = (f32[768]{0:T(1024)S(1)}, f32[768]{0:T(1024)}, u32[]{:S(2)}) copy-start(f32[768]{0:T(1024)} %refs_4_.1) | copy-start | bytes 9220
  0.8 5.0 %collective-permute-start = (bf16[16,256]{1,0:T(8,128)(2,1)S(1)}, bf16[16,256]{1,0:T(8,128)(2,1)S(1)}, u32[]{:S(2)}, u32[]{:S(2)}) collective-permute-start(bf16[16,256]{1,0:T(8,128)(2,1)S(1)} %slice.3), channel_id=1, source_target_pairs={{0,1},{1,2},{2,3},{3,4},{4,5},{5,6},{6,7},{7,8},{8,9},{9,10},{10,1... | collective-permute-start | bytes 24584 | tf_op jit(solution)/shard_map/halo/ppermute | solution.py:18
  5.7 0.6 copy-start.2
  12.3 20.3 %collective-permute-start.1 = (f32[192,512]{1,0:T(8,128)}, f32[192,512]{1,0:T(8,128)S(1)}, u32[]{:S(2)}, u32[]{:S(2)}) collective-permute-start(f32[192,512]{1,0:T(8,128)} %get-tuple-element.23), channel_id=1, source_target_pairs={{0,224},{32,0},{64,32},{96,64},{128,96},{160,128},{192,160},{224,1... | collective-permute-start | bytes 1179656 | tf_op jit(solution)/shard_map/beams_near/ppermute | solution.py:154
  18.3 14.6 %collective-permute-start.2 = (f32[192,512]{1,0:T(8,128)}, f32[192,512]{1,0:T(8,128)S(1)}, u32[]{:S(2)}, u32[]{:S(2)}) collective-permute-start(f32[192,512]{1,0:T(8,128)} %get-tuple-element.24), channel_id=1, source_target_pairs={{0,32},{32,64},{64,96},{96,128},{128,160},{160,192},{192,224},{224... | collective-permute-start | bytes 1179656 | tf_op jit(solution)/shard_map/beams_near/ppermute | solution.py:154
  18.3 12.4 %collective-permute-start.3 = (f32[48,512]{1,0:T(8,128)}, f32[48,512]{1,0:T(8,128)S(1)}, u32[]{:S(2)}, u32[]{:S(2)}) collective-permute-start(f32[48,512]{1,0:T(8,128)} %get-tuple-element.25), channel_id=1, source_target_pairs={{0,192},{32,224},{64,0},{96,32},{128,64},{160,96},{192,128},{224,1... | collective-permute-start | bytes 294920 | tf_op jit(solution)/shard_map/beams_near/ppermute | solution.py:154
  20.7 11.9 %collective-permute-start.4 = (f32[48,512]{1,0:T(8,128)}, f32[48,512]{1,0:T(8,128)S(1)}, u32[]{:S(2)}, u32[]{:S(2)}) collective-permute-start(f32[48,512]{1,0:T(8,128)} %get-tuple-element.26), channel_id=1, source_target_pairs={{0,64},{32,96},{64,128},{96,160},{128,192},{160,224},{192,0},{224,... | collective-permute-start | bytes 294920 | tf_op jit(solution)/shard_map/beams_near/ppermute | solution.py:154
  21.2 2.2 %copy-start = (bf16[16,256,512]{2,1,0:T(8,128)(2,1)S(1)}, bf16[16,256,512]{2,1,0:T(8,128)(2,1)}, u32[]{:S(2)}) copy-start(bf16[16,256,512]{2,1,0:T(8,128)(2,1)} %refs_3_.3) | copy-start | bytes 12582916
  23.4 0.7 copy-start.3
  33.0 8.9 %collective-permute-start.5 = (f32[96,512]{1,0:T(8,128)S(1)}, f32[96,512]{1,0:T(8,128)S(1)}, u32[]{:S(2)}, u32[]{:S(2)}) collective-permute-start(f32[96,512]{1,0:T(8,128)S(1)} %get-tuple-element.27), channel_id=1, source_target_pairs={{0,192},{32,224},{64,0},{96,32},{128,64},{160,96},{192,128},{224,1... | collective-permute-start | bytes 589832 | tf_op jit(solution)/shard_map/beams_far/ppermute | solution.py:154
  35.3 10.5 %collective-permute-start.6 = (f32[96,512]{1,0:T(8,128)S(1)}, f32[96,512]{1,0:T(8,128)S(1)}, u32[]{:S(2)}, u32[]{:S(2)}) collective-permute-start(f32[96,512]{1,0:T(8,128)S(1)} %get-tuple-element.28), channel_id=1, source_target_pairs={{0,64},{32,96},{64,128},{96,160},{128,192},{160,224},{192,0},{224,... | collective-permute-start | bytes 589832 | tf_op jit(solution)/shard_map/beams_far/ppermute | solution.py:154
  68.5 18.7 %collective-permute-start.10 = (f32[96,512]{1,0:T(8,128)S(1)}, f32[96,512]{1,0:T(8,128)S(1)}, u32[]{:S(2)}, u32[]{:S(2)}) collective-permute-start(f32[96,512]{1,0:T(8,128)S(1)} %get-tuple-element.33.refs_0_), channel_id=1, source_target_pairs={{0,192},{32,224},{64,0},{96,32},{128,64},{160,96},{192,128},{224,1... | collective-permute-start | bytes 589832 | tf_op jit(solution)/shard_map/beams_gather/ppermute | solution.py:154
  69.0 18.3 %collective-permute-start.9 = (f32[96,512]{1,0:T(8,128)S(1)}, f32[96,512]{1,0:T(8,128)S(1)}, u32[]{:S(2)}, u32[]{:S(2)}) collective-permute-start(f32[96,512]{1,0:T(8,128)S(1)} %get-tuple-element.33.refs_0_), channel_id=1, source_target_pairs={{0,224},{32,0},{64,32},{96,64},{128,96},{160,128},{192,160},{224,1... | collective-permute-start | bytes 589832 | tf_op jit(solution)/shard_map/beams_gather/ppermute | solution.py:154
  69.7 17.5 %collective-permute-start.8 = (f32[96,512]{1,0:T(8,128)S(1)}, f32[96,512]{1,0:T(8,128)S(1)}, u32[]{:S(2)}, u32[]{:S(2)}) collective-permute-start(f32[96,512]{1,0:T(8,128)S(1)} %get-tuple-element.33.refs_0_), channel_id=1, source_target_pairs={{0,64},{32,96},{64,128},{96,160},{128,192},{160,224},{192,0},{224,... | collective-permute-start | bytes 589832 | tf_op jit(solution)/shard_map/beams_gather/ppermute | solution.py:154
  71.6 15.7 %collective-permute-start.7 = (f32[96,512]{1,0:T(8,128)S(1)}, f32[96,512]{1,0:T(8,128)S(1)}, u32[]{:S(2)}, u32[]{:S(2)}) collective-permute-start(f32[96,512]{1,0:T(8,128)S(1)} %get-tuple-element.33.refs_0_), channel_id=1, source_target_pairs={{0,32},{32,64},{64,96},{96,128},{128,160},{160,192},{192,224},{224... | collective-permute-start | bytes 589832 | tf_op jit(solution)/shard_map/beams_gather/ppermute | solution.py:154
  87.8 16.4 %collective-permute-start.11 = (f32[144,512]{1,0:T(8,128)S(1)}, f32[144,512]{1,0:T(8,128)S(1)}, u32[]{:S(2)}, u32[]{:S(2)}) collective-permute-start(f32[144,512]{1,0:T(8,128)S(1)} %get-tuple-element.35), channel_id=1, source_target_pairs={{0,192},{32,224},{64,0},{96,32},{128,64},{160,96},{192,128},{224,1... | collective-permute-start | bytes 884744 | tf_op jit(solution)/shard_map/beams_gather/ppermute | solution.py:154
  89.4 16.8 %collective-permute-start.12 = (f32[144,512]{1,0:T(8,128)S(1)}, f32[144,512]{1,0:T(8,128)S(1)}, u32[]{:S(2)}, u32[]{:S(2)}) collective-permute-start(f32[144,512]{1,0:T(8,128)S(1)} %get-tuple-element.36), channel_id=1, source_target_pairs={{0,64},{32,96},{64,128},{96,160},{128,192},{160,224},{192,0},{224,... | collective-permute-start | bytes 884744 | tf_op jit(solution)/shard_map/beams_gather/ppermute | solution.py:154

commit v5 on v4

--- a/solution.py
+++ b/solution.py
@@ -106,7 +106,7 @@
     log_total = jnp.sum(logs, axis=1, keepdims=True)
     at = lax.broadcasted_iota(jnp.int32, stats_ref.shape, 1)
     stats_ref[...] = jnp.where(
-        at == 0,
+        at == HALF,
         jnp.broadcast_to(log_total, stats_ref.shape),
         jnp.broadcast_to(mass, stats_ref.shape),
     )
@@ -185,18 +185,45 @@
         + high_ref[...]
     )
     weighted = b_ref[...] * jnp.concatenate([weight_ref[...]] * (beams // TILE), 1)
-    at = 0
-    for r in range(0, beams, TILE):
+    n = beams // TILE
+    places = packing(n)
+    lane = lax.broadcasted_iota(jnp.int32, (HALF, TILE), 1)
+    corner = None
+    for r in range(n):
         part = lax.dot_general(
-            weighted[:, r : r + TILE],
-            b_ref[:, r:],
+            weighted[:, r * TILE : (r + 1) * TILE],
+            b_ref[:, r * TILE :],
             (((0,), (0,)), ((), ())),
             precision=HI,
             preferred_element_type=jnp.float32,
         )
-        for c in range(0, beams - r, TILE):
-            o_ref[at : at + TILE, :] = part[:, c : c + TILE]
+        for c in range(r + 1, n):
+            at = places[r, c]
+            o_ref[at : at + TILE, :] = part[:, (c - r) * TILE : (c - r + 1) * TILE]
+        at, low = places[r, r]
+        o_ref[at : at + HALF, :] = part[:HALF, :TILE]
+        if r % 2 == 0:
+            corner = pltpu.roll(part[HALF:, :TILE], HALF, 1)
+        else:
+            o_ref[low : low + HALF, :] = jnp.where(lane < HALF, corner, part[HALF:, :TILE])
+
+
+HALF = TILE // 2
+
+
+def packing(n):
+    places, at = ({}, 0)
+    for r in range(n):
+        for c in range(r + 1, n):
+            places[r, c] = at
             at += TILE
+    for r in range(n):
+        places[r, r] = (at + r * HALF, at + n * HALF + r // 2 * HALF)
+    return places
+
+
+def packed_rows(n):
+    return (n * (n - 1) // 2) * TILE + n * HALF + n // 2 * HALF
 
 
 def packed_gram(keep, down, up, low, high, weight):
@@ -206,7 +233,7 @@
         gram_body,
         out_shape=(
             jax.ShapeDtypeStruct((share, beams), jnp.float32),
-            jax.ShapeDtypeStruct((n * (n + 1) // 2 * TILE, TILE), jnp.float32),
+            jax.ShapeDtypeStruct((packed_rows(n), TILE), jnp.float32),
         ),
         in_specs=[VMEM] * 6,
         out_specs=(VMEM, VMEM),
@@ -225,7 +252,10 @@
     tiles = rows // ways
     for s in range(tiles):
         o_ref[:, s, :] = total[s * ways : (s + 1) * ways, :]
-    o_ref[:, tiles, :] = jnp.broadcast_to(stats_ref[...], (ways, TILE))
+    rest = total[tiles * ways :, :]
+    lane = lax.broadcasted_iota(jnp.int32, (ways, TILE), 1)
+    rest = jnp.concatenate([rest, pltpu.roll(rest, HALF, 1)], 0)
+    o_ref[:, tiles, :] = jnp.where(lane < HALF, rest, stats_ref[...])
 
 
 def spread_share(parts, stats, my_beams, ways):
@@ -251,16 +281,17 @@
     high_ref[:share, :] = from_below[...]
     high_ref[share:, :] = from_below2[half:, :]
     n, tiles, _ = r_ref.shape
-    tiles -= 1
-    stats = r_ref[:, tiles, :]
-    logs = stats[:, 0:1]
+    stats = r_ref[:, tiles - 1, :]
+    logs = stats[:, HALF : HALF + 1]
     row = lax.broadcasted_iota(jnp.int32, (n, n), 0)
     col = lax.broadcasted_iota(jnp.int32, (n, n), 1)
     upto = jnp.where(col <= row, 1.0, 0.0)
     later = jnp.where(row > col, jnp.broadcast_to(logs, (n, n)), 0.0)
     span = jnp.dot(upto, later, precision=HI, preferred_element_type=jnp.float32)
     factor = jnp.where(col <= row, jnp.exp(jnp.where(col <= row, span, 0.0)), 0.0)
-    count = jnp.dot(factor, stats, precision=HI, preferred_element_type=jnp.float32)[:, 1:2]
+    count = jnp.dot(factor, stats, precision=HI, preferred_element_type=jnp.float32)[
+        :, HALF + 1 : HALF + 2
+    ]
     gram = jnp.dot(
         factor,
         jnp.concatenate([r_ref[:, s, :] for s in range(tiles)], 1),
@@ -278,7 +309,7 @@
     packed = jax.ShapeDtypeStruct((share + share // 2, beams), jnp.float32)
     return pl.pallas_call(
         decay_body,
-        out_shape=(jax.ShapeDtypeStruct((n, tiles - 1, TILE), jnp.float32), packed, packed),
+        out_shape=(jax.ShapeDtypeStruct((n, tiles, TILE), jnp.float32), packed, packed),
         in_specs=[VMEM] * 5,
         out_specs=(VMEM,) * 3,
         compiler_params=pltpu.CompilerParams(vmem_limit_bytes=5 << 20),
@@ -288,17 +319,22 @@
 
 def replicate_body(r_ref, low_ref, high_ref, o_ref):
     ways, tiles, _ = r_ref.shape
-    for s in range(tiles):
-        piece = r_ref[:, s, :]
-        for g in range(o_ref.shape[0]):
-            o_ref[g, s * ways : (s + 1) * ways, :] = piece
+    half = ways // 2
+    tiles -= 1
+    last = r_ref[:, tiles, :]
+    lane = lax.broadcasted_iota(jnp.int32, (half, TILE), 1)
+    last = jnp.where(lane < HALF, last[:half, :], pltpu.roll(last[half:, :], HALF, 1))
+    for g in range(o_ref.shape[0]):
+        for s in range(tiles):
+            o_ref[g, s * ways : (s + 1) * ways, :] = r_ref[:, s, :]
+        o_ref[g, tiles * ways :, :] = last
 
 
 def replicated(returned, groups, low, high):
     ways, tiles, _ = returned.shape
     return pl.pallas_call(
         replicate_body,
-        out_shape=jax.ShapeDtypeStruct((groups, ways * tiles, TILE), jnp.float32),
+        out_shape=jax.ShapeDtypeStruct((groups, ways * tiles - ways // 2, TILE), jnp.float32),
         in_specs=[VMEM] * 3,
         out_specs=VMEM,
         compiler_params=pltpu.CompilerParams(vmem_limit_bytes=4 << 20),
@@ -387,22 +423,33 @@
 def factor_body(group_ref, p_ref, *refs):
     *beam_refs, o_ref, s_ref, d_ref, l_ref, b_ref = refs
     groups, high, _ = p_ref.shape
-    ways = 32
-    tiles = high // ways
     n = s_ref.shape[0]
     count = n // TILE
-    blocks = [(r, c) for r in range(count) for c in range(r, count)]
-    for g in range(groups):
-        for s in range(tiles):
-            first = (g * tiles + s) * ways
-            r, c = blocks[first // TILE]
-            top = r * TILE + first % TILE
-            piece = p_ref[g, s * ways : (s + 1) * ways, :]
-            if r == c:
-                row = lax.broadcasted_iota(jnp.int32, piece.shape, 0) + first % TILE
-                lane = lax.broadcasted_iota(jnp.int32, piece.shape, 1)
-                piece = piece + jnp.where(row == lane, loading_level, 0.0)
-            s_ref[top : top + ways, c * TILE : (c + 1) * TILE] = piece
+    unit = 16
+    lane = lax.broadcasted_iota(jnp.int32, (unit, TILE), 1)
+    row = lax.broadcasted_iota(jnp.int32, (unit, TILE), 0)
+
+    def loaded(r, c, at, piece):
+        if r == c:
+            piece = piece + jnp.where(row + at == lane, loading_level, 0.0)
+        s_ref[r * TILE + at : r * TILE + at + unit, c * TILE : (c + 1) * TILE] = piece
+
+    def pieces(first, tall):
+        for at in range(0, tall, unit):
+            g, at_row = divmod(first + at, high)
+            yield at, p_ref[g, at_row : at_row + unit, :]
+
+    for (r, c), first in packing(count).items():
+        if r != c:
+            for at, piece in pieces(first, TILE):
+                loaded(r, c, at, piece)
+        else:
+            for at, piece in pieces(first[0], HALF):
+                loaded(r, r, at, piece)
+            for at, piece in pieces(first[1], HALF):
+                if r % 2 == 0:
+                    piece = pltpu.roll(piece, HALF, 1)
+                loaded(r, r, HALF + at, jnp.where(lane < HALF, 0.0, piece))
     for r in range(count):
         for c in range(r):
             s_ref[r * TILE : (r + 1) * TILE, c * TILE : (c + 1) * TILE] = jnp.zeros(

time: 149 us -> 146 us (0.980)
  blocking collectives: 71.5 us -> 68.2 us
    all_to_all x1, blocking collectives: 24 us -> 22.2 us  [local(): lax.all_to_all(replicated(returned, groups, low, high), 'elem', 0, 0)]
where the time goes in v5:
time: 146 us
  blocking collectives  68.2 us (47%)
  Pallas kernels  27.8 us (19%)
  waiting for transfers between devices  23.3 us (16%)
  starting transfers between devices  21.8 us (15%)
  local copies, waits for them, and re-layouts  4.25 us (3%)
    all_to_all x1, blocking collectives, local(): lax.all_to_all(replicated(returned, groups, low, high), 'elem', 0, 0)  22.2 us
    all_to_all x1, blocking collectives, local(): lax.all_to_all(packed.reshape(groups, packed.shape[0] // groups, TILE), '...  20.5 us
    ppermute x12, waiting for transfers between devices, ring(): lax.ppermute(array, 'elem', [(i, (i + by) % size) for i in range(size)])  20.3 us
    ppermute x12, starting transfers between devices, ring(): lax.ppermute(array, 'elem', [(i, (i + by) % size) for i in range(size)])  19.9 us
    pallas_call x1, Pallas kernels, whitened_rows(): pl.pallas_call(factor_body, out_shape=jax.ShapeDtypeStruct((n // groups,...  18.7 us
    all_to_all x1, blocking collectives, local(): received = lax.all_to_all(spread, 'tm', 0, 0, tiled=True)  13.6 us
    all_to_all x1, blocking collectives, local(): returned = lax.all_to_all(estimate, 'tm', 0, 0, tiled=True)  11.9 us
    pallas_call x2, Pallas kernels, fir(): pl.pallas_call(lambda *refs: fir_body(offsets, weights, *refs), out_shape...  7.46 us
  transfers between devices with their start and end apart: 13, of which 8 were waited for; matrix products, arithmetic and copies ran while one was open for 0% of the time, Pallas kernels for 1%

profile of v5, /device:TPU:2, one launch (start us, length us, event | category | flops | bytes accessed | tf_op | source)
XLA Modules:
  0.0 145.6 jit_solution(17357041701132882325)
XLA Ops:
  0.0 0.0 copy-start.1
  0.0 0.0 copy-start.4
  0.0 0.8 slice.3
  0.8 1.9 %collective-permute-start = (bf16[16,256]{1,0:T(8,128)(2,1)S(1)}, bf16[16,256]{1,0:T(8,128)(2,1)S(1)}, u32[]{:S(2)}, u32[]{:S(2)}) collective-permute-start(bf16[16,256]{1,0:T(8,128)(2,1)S(1)} %slice.3), channel_id=1, source_target_pairs={{0,1},{1,2},{2,3},{3,4},{4,5},{5,6},{6,7},{7,8},{8,9},{9,10},{10,1... | collective-permute-start | bytes 24584 | tf_op jit(solution)/shard_map/halo/ppermute | solution.py:18
  2.7 3.0 %collective-permute-done.refs_1_ = bf16[16,256]{1,0:T(8,128)(2,1)S(1)} collective-permute-done((bf16[16,256]{1,0:T(8,128)(2,1)S(1)}, bf16[16,256]{1,0:T(8,128)(2,1)S(1)}, u32[]{:S(2)}, u32[]{:S(2)}) %collective-permute-start) | collective-permute-done | bytes 8224 | tf_op jit(solution)/shard_map/halo/ppermute | solution.py:18
  5.7 0.0 copy-start.2
  5.7 0.6 copy-done.2
  6.3 6.0 %fir_sent.1 = (f32[192,512]{1,0:T(8,128)}, f32[192,512]{1,0:T(8,128)}, f32[48,512]{1,0:T(8,128)}, f32[48,512]{1,0:T(8,128)}) custom-call(s32[1]{0:T(128)} %bitcast.refs_0_.group_ref, bf16[16,256]{1,0:T(8,128)(2,1)} %copy-done.2, bf16[768,256]{1,0:T(8,128)(2,1)} %refs_2_.3, bf16[16,256,512]{2,1,0:T(8,128)(2,1)} %refs_3_.3), custom_call_target="tpu_custom_call" | custom-call | flops 2013265920 | bytes 6291456 | tf_op jit(solution)/shard_map/fir_sent/pallas_call | solution.py:136
  12.3 5.9 %collective-permute-start.1 = (f32[192,512]{1,0:T(8,128)}, f32[192,512]{1,0:T(8,128)S(1)}, u32[]{:S(2)}, u32[]{:S(2)}) collective-permute-start(f32[192,512]{1,0:T(8,128)} %get-tuple-element.23), channel_id=1, source_target_pairs={{0,224},{32,0},{64,32},{96,64},{128,96},{160,128},{192,160},{224,1... | collective-permute-start | bytes 1179656 | tf_op jit(solution)/shard_map/beams_near/ppermute | solution.py:154
  18.3 0.0 collective-permute-start.2
  18.3 2.5 %collective-permute-start.3 = (f32[48,512]{1,0:T(8,128)}, f32[48,512]{1,0:T(8,128)S(1)}, u32[]{:S(2)}, u32[]{:S(2)}) collective-permute-start(f32[48,512]{1,0:T(8,128)} %get-tuple-element.25), channel_id=1, source_target_pairs={{0,192},{32,224},{64,0},{96,32},{128,64},{160,96},{192,128},{224,1... | collective-permute-start | bytes 294920 | tf_op jit(solution)/shard_map/beams_near/ppermute | solution.py:154
  20.7 0.5 collective-permute-start.4
  21.2 0.0 copy-done.1
  21.2 0.0 copy-done.4
  21.2 0.0 copy-start
  21.2 2.2 %copy-done = bf16[16,256,512]{2,1,0:T(8,128)(2,1)S(1)} copy-done((bf16[16,256,512]{2,1,0:T(8,128)(2,1)S(1)}, bf16[16,256,512]{2,1,0:T(8,128)(2,1)}, u32[]{:S(2)}) %copy-start) | copy-done | bytes 4194328
  23.4 0.0 copy-start.3
  23.4 0.7 copy-done.3
  24.1 1.5 %fir_rest.1 = (f32[288,512]{1,0:T(8,128)S(1)}, f32[96,128]{1,0:T(8,128)S(1)}, f32[1,128]{1,0:T(1,128)S(1)}) custom-call(s32[1]{0:T(128)} %bitcast.refs_0_.group_ref, bf16[16,256]{1,0:T(8,128)(2,1)S(1)} %copy-done.3, bf16[768,256]{1,0:T(8,128)(2,1)S(1)} %copy-done.1, bf16[16,256,512]{2,1,0:T(8,128)(2,1)S(1)} %copy-done, f32[768]{0:T(1024)S(1)} %copy-done.4), custom_call_target="tpu_custom_call" | custom-call | flops 1207959552 | bytes 6291456 | tf_op jit(solution)/shard_map/fir_rest/pallas_call | solution.py:136
  25.6 5.1 %collective-permute-done.3.far_down_ref = f32[48,512]{1,0:T(8,128)S(1)} collective-permute-done((f32[48,512]{1,0:T(8,128)}, f32[48,512]{1,0:T(8,128)S(1)}, u32[]{:S(2)}, u32[]{:S(2)}) %collective-permute-start.3) | collective-permute-done | bytes 98336 | tf_op jit(solution)/shard_map/beams_near/ppermute | solution.py:154
  30.6 2.0 %collective-permute-done.4.far_up_ref = f32[48,512]{1,0:T(8,128)S(1)} collective-permute-done((f32[48,512]{1,0:T(8,128)}, f32[48,512]{1,0:T(8,128)S(1)}, u32[]{:S(2)}, u32[]{:S(2)}) %collective-permute-start.4) | collective-permute-done | bytes 98336 | tf_op jit(solution)/shard_map/beams_near/ppermute | solution.py:154
  32.6 0.0 collective-permute-done.1.down_ref
  32.6 0.3 collective-permute-done.2.up_ref
  32.9 0.1 relay_sums.1
  33.0 2.3 %collective-permute-start.5 = (f32[96,512]{1,0:T(8,128)S(1)}, f32[96,512]{1,0:T(8,128)S(1)}, u32[]{:S(2)}, u32[]{:S(2)}) collective-permute-start(f32[96,512]{1,0:T(8,128)S(1)} %get-tuple-element.27), channel_id=1, source_target_pairs={{0,192},{32,224},{64,0},{96,32},{128,64},{160,96},{192,128},{224,1... | collective-permute-start | bytes 589832 | tf_op jit(solution)/shard_map/beams_far/ppermute | solution.py:154
  35.3 0.7 collective-permute-start.6
  36.0 5.9 %collective-permute-done.5.low_ref = f32[96,512]{1,0:T(8,128)S(1)} collective-permute-done((f32[96,512]{1,0:T(8,128)S(1)}, f32[96,512]{1,0:T(8,128)S(1)}, u32[]{:S(2)}, u32[]{:S(2)}) %collective-permute-start.5) | collective-permute-done | bytes 196640 | tf_op jit(solution)/shard_map/beams_far/ppermute | solution.py:154
  41.9 3.9 %collective-permute-done.6.high_ref = f32[96,512]{1,0:T(8,128)S(1)} collective-permute-done((f32[96,512]{1,0:T(8,128)S(1)}, f32[96,512]{1,0:T(8,128)S(1)}, u32[]{:S(2)}, u32[]{:S(2)}) %collective-permute-start.6) | collective-permute-done | bytes 196640 | tf_op jit(solution)/shard_map/beams_far/ppermute | solution.py:154
  45.8 0.8 packed_gram.1
  46.6 20.5 %all_to_all.20.p_ref = f32[8,144,128]{2,1,0:T(8,128)S(1)} all-to-all(f32[8,144,128]{2,1,0:T(8,128)S(1)} %bitcast.2), channel_id=1, replica_groups=mesh['elem'=8,'tm'=32] {'elem'}, dimensions={0} | all-to-all | bytes 1179648 | tf_op jit(solution)/shard_map/gram_sum/all_to_all | solution.py:558
  67.1 0.1 spread_share.1
  67.2 0.5 collective-permute-start.10
  67.7 0.7 collective-permute-start.9
  68.4 1.8 %collective-permute-start.8 = (f32[96,512]{1,0:T(8,128)S(1)}, f32[96,512]{1,0:T(8,128)S(1)}, u32[]{:S(2)}, u32[]{:S(2)}) collective-permute-start(f32[96,512]{1,0:T(8,128)S(1)} %get-tuple-element.33.refs_0_), channel_id=1, source_target_pairs={{0,64},{32,96},{64,128},{96,160},{128,192},{160,224},{192,0},{224,... | collective-permute-start | bytes 589832 | tf_op jit(solution)/shard_map/beams_gather/ppermute | solution.py:154
  70.2 2.0 %collective-permute-start.7 = (f32[96,512]{1,0:T(8,128)S(1)}, f32[96,512]{1,0:T(8,128)S(1)}, u32[]{:S(2)}, u32[]{:S(2)}) collective-permute-start(f32[96,512]{1,0:T(8,128)S(1)} %get-tuple-element.33.refs_0_), channel_id=1, source_target_pairs={{0,32},{32,64},{64,96},{96,128},{128,160},{160,192},{192,224},{224... | collective-permute-start | bytes 589832 | tf_op jit(solution)/shard_map/beams_gather/ppermute | solution.py:154
  72.2 13.6 %all_to_all.21.r_ref = f32[32,5,128]{2,1,0:T(8,128)S(1)} all-to-all(f32[32,5,128]{2,1,0:T(8,128)S(1)} %get-tuple-element.32), channel_id=1, replica_groups=mesh['elem'=8,'tm'=32] {'tm'}, dimensions={0} | all-to-all | bytes 163840 | tf_op jit(solution)/shard_map/blocks_out/all_to_all | solution.py:566
  85.8 0.0 collective-permute-done.10.from_above2.refs_4_
  85.8 0.0 collective-permute-done.9.from_above.refs_3_
  85.9 0.0 collective-permute-done.8.from_below2.refs_2_
  85.9 0.0 collective-permute-done.7.from_below.refs_1_
  85.9 0.5 decayed_sums.1
  86.4 1.7 %collective-permute-start.11 = (f32[144,512]{1,0:T(8,128)S(1)}, f32[144,512]{1,0:T(8,128)S(1)}, u32[]{:S(2)}, u32[]{:S(2)}) collective-permute-start(f32[144,512]{1,0:T(8,128)S(1)} %get-tuple-element.35), channel_id=1, source_target_pairs={{0,192},{32,224},{64,0},{96,32},{128,64},{160,96},{192,128},{224,1... | collective-permute-start | bytes 884744 | tf_op jit(solution)/shard_map/beams_gather/ppermute | solution.py:154
  88.1 1.3 collective-permute-start.12
  89.4 11.9 %all_to_all.22.r_ref = f32[32,5,128]{2,1,0:T(8,128)S(1)} all-to-all(f32[32,5,128]{2,1,0:T(8,128)S(1)} %get-tuple-element.34), channel_id=1, replica_groups=mesh['elem'=8,'tm'=32] {'tm'}, dimensions={0} | all-to-all | bytes 163840 | tf_op jit(solution)/shard_map/blocks_back/all_to_all | solution.py:571
  101.4 1.5 %collective-permute-done.11.low_ref.refs_5_ = f32[144,512]{1,0:T(8,128)S(1)} collective-permute-done((f32[144,512]{1,0:T(8,128)S(1)}, f32[144,512]{1,0:T(8,128)S(1)}, u32[]{:S(2)}, u32[]{:S(2)}) %collective-permute-start.11) | collective-permute-done | bytes 294944 | tf_op jit(solution)/shard_map/beams_gather/ppermute | solution.py:154
  102.8 1.7 %collective-permute-done.12.high_ref.refs_6_ = f32[144,512]{1,0:T(8,128)S(1)} collective-permute-done((f32[144,512]{1,0:T(8,128)S(1)}, f32[144,512]{1,0:T(8,128)S(1)}, u32[]{:S(2)}, u32[]{:S(2)}) %collective-permute-start.12) | collective-permute-done | bytes 294944 | tf_op jit(solution)/shard_map/beams_gather/ppermute | solution.py:154
  104.5 0.2 replicated.1
  104.7 22.2 %all_to_all.23.p_ref = f32[8,144,128]{2,1,0:T(8,128)S(1)} all-to-all(f32[8,144,128]{2,1,0:T(8,128)S(1)} %replicated.1), channel_id=1, replica_groups=mesh['elem'=8,'tm'=32] {'elem'}, dimensions={0} | all-to-all | bytes 1179648 | tf_op jit(solution)/shard_map/gram_gather/all_to_all | solution.py:573
  126.9 18.7 %whitened_rows.1 = f32[64,768]{1,0:T(8,128)} custom-call(s32[1]{0:T(128)} %bitcast.refs_0_.group_ref, f32[8,144,128]{2,1,0:T(8,128)S(1)} %all_to_all.23.p_ref, f32[96,512]{1,0:T(8,128)S(1)} %get-tuple-element.33.refs_0_, f32[96,512]{1,0:T(8,128)S(1)} %collective-permute-done.7.from_below.refs_1_, f32[96,512]{1,0:T(8,128)S(1)} %collective-permute-done.8.from_below2.refs_2_, ...), custom_call_target="tpu_custom_call" | custom-call | flops 1610612736 | bytes 1048576 | tf_op jit(solution)/shard_map/whitened_rows/pallas_call | solution.py:520
Async XLA Ops:
  0.0 21.2 %copy-start.1 = (bf16[768,256]{1,0:T(8,128)(2,1)S(1)}, bf16[768,256]{1,0:T(8,128)(2,1)}, u32[]{:S(2)}) copy-start(bf16[768,256]{1,0:T(8,128)(2,1)} %refs_2_.3) | copy-start | bytes 1179652
  0.0 21.2 %copy-start.4 = (f32[768]{0:T(1024)S(1)}, f32[768]{0:T(1024)}, u32[]{:S(2)}) copy-start(f32[768]{0:T(1024)} %refs_4_.1) | copy-start | bytes 9220
  0.8 5.0 %collective-permute-start = (bf16[16,256]{1,0:T(8,128)(2,1)S(1)}, bf16[16,256]{1,0:T(8,128)(2,1)S(1)}, u32[]{:S(2)}, u32[]{:S(2)}) collective-permute-start(bf16[16,256]{1,0:T(8,128)(2,1)S(1)} %slice.3), channel_id=1, source_target_pairs={{0,1},{1,2},{2,3},{3,4},{4,5},{5,6},{6,7},{7,8},{8,9},{9,10},{10,1... | collective-permute-start | bytes 24584 | tf_op jit(solution)/shard_map/halo/ppermute | solution.py:18
  5.7 0.6 copy-start.2
  12.3 20.3 %collective-permute-start.1 = (f32[192,512]{1,0:T(8,128)}, f32[192,512]{1,0:T(8,128)S(1)}, u32[]{:S(2)}, u32[]{:S(2)}) collective-permute-start(f32[192,512]{1,0:T(8,128)} %get-tuple-element.23), channel_id=1, source_target_pairs={{0,224},{32,0},{64,32},{96,64},{128,96},{160,128},{192,160},{224,1... | collective-permute-start | bytes 1179656 | tf_op jit(solution)/shard_map/beams_near/ppermute | solution.py:154
  18.3 14.6 %collective-permute-start.2 = (f32[192,512]{1,0:T(8,128)}, f32[192,512]{1,0:T(8,128)S(1)}, u32[]{:S(2)}, u32[]{:S(2)}) collective-permute-start(f32[192,512]{1,0:T(8,128)} %get-tuple-element.24), channel_id=1, source_target_pairs={{0,32},{32,64},{64,96},{96,128},{128,160},{160,192},{192,224},{224... | collective-permute-start | bytes 1179656 | tf_op jit(solution)/shard_map/beams_near/ppermute | solution.py:154
  18.3 12.4 %collective-permute-start.3 = (f32[48,512]{1,0:T(8,128)}, f32[48,512]{1,0:T(8,128)S(1)}, u32[]{:S(2)}, u32[]{:S(2)}) collective-permute-start(f32[48,512]{1,0:T(8,128)} %get-tuple-element.25), channel_id=1, source_target_pairs={{0,192},{32,224},{64,0},{96,32},{128,64},{160,96},{192,128},{224,1... | collective-permute-start | bytes 294920 | tf_op jit(solution)/shard_map/beams_near/ppermute | solution.py:154
  20.7 11.9 %collective-permute-start.4 = (f32[48,512]{1,0:T(8,128)}, f32[48,512]{1,0:T(8,128)S(1)}, u32[]{:S(2)}, u32[]{:S(2)}) collective-permute-start(f32[48,512]{1,0:T(8,128)} %get-tuple-element.26), channel_id=1, source_target_pairs={{0,64},{32,96},{64,128},{96,160},{128,192},{160,224},{192,0},{224,... | collective-permute-start | bytes 294920 | tf_op jit(solution)/shard_map/beams_near/ppermute | solution.py:154
  21.2 2.2 %copy-start = (bf16[16,256,512]{2,1,0:T(8,128)(2,1)S(1)}, bf16[16,256,512]{2,1,0:T(8,128)(2,1)}, u32[]{:S(2)}) copy-start(bf16[16,256,512]{2,1,0:T(8,128)(2,1)} %refs_3_.3) | copy-start | bytes 12582916
  23.4 0.7 copy-start.3
  33.0 8.9 %collective-permute-start.5 = (f32[96,512]{1,0:T(8,128)S(1)}, f32[96,512]{1,0:T(8,128)S(1)}, u32[]{:S(2)}, u32[]{:S(2)}) collective-permute-start(f32[96,512]{1,0:T(8,128)S(1)} %get-tuple-element.27), channel_id=1, source_target_pairs={{0,192},{32,224},{64,0},{96,32},{128,64},{160,96},{192,128},{224,1... | collective-permute-start | bytes 589832 | tf_op jit(solution)/shard_map/beams_far/ppermute | solution.py:154
  35.3 10.5 %collective-permute-start.6 = (f32[96,512]{1,0:T(8,128)S(1)}, f32[96,512]{1,0:T(8,128)S(1)}, u32[]{:S(2)}, u32[]{:S(2)}) collective-permute-start(f32[96,512]{1,0:T(8,128)S(1)} %get-tuple-element.28), channel_id=1, source_target_pairs={{0,64},{32,96},{64,128},{96,160},{128,192},{160,224},{192,0},{224,... | collective-permute-start | bytes 589832 | tf_op jit(solution)/shard_map/beams_far/ppermute | solution.py:154
  67.2 18.7 %collective-permute-start.10 = (f32[96,512]{1,0:T(8,128)S(1)}, f32[96,512]{1,0:T(8,128)S(1)}, u32[]{:S(2)}, u32[]{:S(2)}) collective-permute-start(f32[96,512]{1,0:T(8,128)S(1)} %get-tuple-element.33.refs_0_), channel_id=1, source_target_pairs={{0,192},{32,224},{64,0},{96,32},{128,64},{160,96},{192,128},{224,1... | collective-permute-start | bytes 589832 | tf_op jit(solution)/shard_map/beams_gather/ppermute | solution.py:154
  67.7 18.2 %collective-permute-start.9 = (f32[96,512]{1,0:T(8,128)S(1)}, f32[96,512]{1,0:T(8,128)S(1)}, u32[]{:S(2)}, u32[]{:S(2)}) collective-permute-start(f32[96,512]{1,0:T(8,128)S(1)} %get-tuple-element.33.refs_0_), channel_id=1, source_target_pairs={{0,224},{32,0},{64,32},{96,64},{128,96},{160,128},{192,160},{224,1... | collective-permute-start | bytes 589832 | tf_op jit(solution)/shard_map/beams_gather/ppermute | solution.py:154
  68.4 17.5 %collective-permute-start.8 = (f32[96,512]{1,0:T(8,128)S(1)}, f32[96,512]{1,0:T(8,128)S(1)}, u32[]{:S(2)}, u32[]{:S(2)}) collective-permute-start(f32[96,512]{1,0:T(8,128)S(1)} %get-tuple-element.33.refs_0_), channel_id=1, source_target_pairs={{0,64},{32,96},{64,128},{96,160},{128,192},{160,224},{192,0},{224,... | collective-permute-start | bytes 589832 | tf_op jit(solution)/shard_map/beams_gather/ppermute | solution.py:154
  70.2 15.7 %collective-permute-start.7 = (f32[96,512]{1,0:T(8,128)S(1)}, f32[96,512]{1,0:T(8,128)S(1)}, u32[]{:S(2)}, u32[]{:S(2)}) collective-permute-start(f32[96,512]{1,0:T(8,128)S(1)} %get-tuple-element.33.refs_0_), channel_id=1, source_target_pairs={{0,32},{32,64},{64,96},{96,128},{128,160},{160,192},{192,224},{224... | collective-permute-start | bytes 589832 | tf_op jit(solution)/shard_map/beams_gather/ppermute | solution.py:154
  86.4 16.4 %collective-permute-start.11 = (f32[144,512]{1,0:T(8,128)S(1)}, f32[144,512]{1,0:T(8,128)S(1)}, u32[]{:S(2)}, u32[]{:S(2)}) collective-permute-start(f32[144,512]{1,0:T(8,128)S(1)} %get-tuple-element.35), channel_id=1, source_target_pairs={{0,192},{32,224},{64,0},{96,32},{128,64},{160,96},{192,128},{224,1... | collective-permute-start | bytes 884744 | tf_op jit(solution)/shard_map/beams_gather/ppermute | solution.py:154
  88.1 16.4 %collective-permute-start.12 = (f32[144,512]{1,0:T(8,128)S(1)}, f32[144,512]{1,0:T(8,128)S(1)}, u32[]{:S(2)}, u32[]{:S(2)}) collective-permute-start(f32[144,512]{1,0:T(8,128)S(1)} %get-tuple-element.36), channel_id=1, source_target_pairs={{0,64},{32,96},{64,128},{96,160},{128,192},{160,224},{192,0},{224,... | collective-permute-start | bytes 884744 | tf_op jit(solution)/shard_map/beams_gather/ppermute | solution.py:154

commit v6 on v5

--- a/solution.py
+++ b/solution.py
@@ -19,72 +19,64 @@
 
 
 LEAD = 16
-SPLIT = 4
-
-
-def fir_body(offsets, weights, group_ref, halo_ref, x_hbm, w_hbm, *refs):
+
+
+def widen_body(x_ref, w_ref, xe_ref):
+    xe_ref[...] = x_ref[...].astype(jnp.float32)
+
+
+def widened(samples, taps_weight):
+    return pl.pallas_call(
+        widen_body,
+        out_shape=jax.ShapeDtypeStruct(samples.shape, jnp.float32),
+        in_specs=[VMEM, VMEM],
+        out_specs=VMEM,
+        compiler_params=pltpu.CompilerParams(vmem_limit_bytes=24 << 20),
+        cost_estimate=pl.CostEstimate(flops=0, bytes_accessed=12 << 20, transcendentals=0),
+        name="widened",
+    )(samples, taps_weight)
+
+
+def fir_body(offsets, weights, group_ref, halo_ref, x_ref, w_ref, *refs):
     if weights:
         retain_ref, refs = (refs[0], refs[1:])
-    held = 2 if weights else 6
-    outs, (xe_ref, part_ref, *own) = (refs[:-held], refs[-held:])
-    taps, width, beams = w_hbm.shape
-    rows = x_hbm.shape[0]
+    outs, (xe_ref, part_ref) = (refs[:-2], refs[-2:])
+    taps, width, beams = w_ref.shape
+    rows = x_ref.shape[0]
     groups = 8
     share = rows // groups
-    each = taps // SPLIT
-    copies = []
-    if weights:
-        xb_ref, wv_ref = (x_hbm, w_hbm)
-    else:
-        xb_ref, wv_ref, x_sem, w_sem = own
-        copy_x = pltpu.make_async_copy(x_hbm, xb_ref, x_sem)
-        copy_x.start()
-        for q in range(SPLIT):
-            span = pl.ds(q * each, each)
-            copies.append(pltpu.make_async_copy(w_hbm.at[span], wv_ref.at[span], w_sem.at[q]))
-            copies[-1].start()
     group = group_ref[0]
     if weights:
         weights_of(group, groups, retain_ref, outs[-2], outs[-1])
         outs = outs[:-2]
     xe_ref[:LEAD, :] = halo_ref[...].astype(jnp.float32)
-    if not weights:
-        copy_x.wait()
-    xe_ref[LEAD:, :] = xb_ref[...].astype(jnp.float32)
+    xe_ref[LEAD:, :] = x_ref[...]
     tall = share + LEAD
     for i, by in enumerate(offsets):
         chunk = lax.rem(group + (by + groups), groups)
         part_ref[i * tall : (i + 1) * tall, :] = xe_ref[
             pl.ds(pl.multiple_of(chunk * share, 8), tall), :
         ]
-    total = None
-    for q in range(SPLIT):
-        if not weights:
-            copies[q].wait()
-        window = jnp.concatenate(
-            [
-                jnp.concatenate(
-                    [
-                        part_ref[i * tall + LEAD - k : (i + 1) * tall - k, :]
-                        for i in range(len(offsets))
-                    ],
-                    0,
-                ).astype(jnp.bfloat16)
-                for k in range(q * each, (q + 1) * each)
-            ],
-            1,
-        )
-        product = jnp.dot(
-            window,
-            wv_ref[q * each : (q + 1) * each].reshape(each * width, beams),
-            preferred_element_type=jnp.float32,
-        )
-        at = 0
-        for o_ref in outs:
-            tall_o = o_ref.shape[0]
-            piece = product[at : at + tall_o]
-            o_ref[...] = piece if q == 0 else o_ref[...] + piece
-            at += tall_o
+    window = jnp.concatenate(
+        [
+            jnp.concatenate(
+                [
+                    part_ref[i * tall + LEAD - k : (i + 1) * tall - k, :]
+                    for i in range(len(offsets))
+                ],
+                0,
+            ).astype(jnp.bfloat16)
+            for k in range(taps)
+        ],
+        1,
+    )
+    product = jnp.dot(
+        window, w_ref[...].reshape(taps * width, beams), preferred_element_type=jnp.float32
+    )
+    at = 0
+    for o_ref in outs:
+        o_ref[...] = product[at : at + o_ref.shape[0]]
+        at += o_ref.shape[0]
 
 
 def weights_of(group, groups, retain_ref, weight_ref, stats_ref):
@@ -112,8 +104,8 @@
     )
 
 
-def fir(offsets, heights, weights, group, halo, samples, taps_weight, retain):
-    rows, width = samples.shape
+def fir(offsets, heights, weights, group, halo, wide, taps_weight, retain):
+    rows, width = wide.shape
     taps, _, beams = taps_weight.shape
     share = rows // 8
     tall = share + LEAD
@@ -121,32 +113,23 @@
     if weights:
         shapes.append(jax.ShapeDtypeStruct((share, TILE), jnp.float32))
         shapes.append(jax.ShapeDtypeStruct((1, TILE), jnp.float32))
-    large = VMEM if weights else pl.BlockSpec(memory_space=pltpu.HBM)
-    scratch = [
-        pltpu.VMEM((rows + LEAD, width), jnp.float32),
-        pltpu.VMEM((tall * len(offsets), width), jnp.float32),
-    ]
-    if not weights:
-        scratch += [
-            pltpu.VMEM((rows, width), samples.dtype),
-            pltpu.VMEM(taps_weight.shape, taps_weight.dtype),
-            pltpu.SemaphoreType.DMA,
-            pltpu.SemaphoreType.DMA((SPLIT,)),
-        ]
     return pl.pallas_call(
         lambda *refs: fir_body(offsets, weights, *refs),
         out_shape=shapes,
-        in_specs=[SMEM, VMEM, large, large] + [VMEM] * weights,
+        in_specs=[SMEM, VMEM, VMEM, VMEM] + [VMEM] * weights,
         out_specs=[VMEM] * len(shapes),
-        scratch_shapes=scratch,
-        compiler_params=pltpu.CompilerParams(vmem_limit_bytes=(16 if weights else 60) << 20),
+        scratch_shapes=[
+            pltpu.VMEM((rows + LEAD, width), jnp.float32),
+            pltpu.VMEM((tall * len(offsets), width), jnp.float32),
+        ],
+        compiler_params=pltpu.CompilerParams(vmem_limit_bytes=24 << 20),
         cost_estimate=pl.CostEstimate(
             flops=2 * share * len(offsets) * taps * width * beams,
             bytes_accessed=6 << 20,
             transcendentals=0,
         ),
         name="fir_rest" if weights else "fir_sent",
-    )(group, halo, samples, taps_weight, *([retain] if weights else []))
+    )(group, halo, wide, taps_weight, *([retain] if weights else []))
 
 
 def ring(array, by):
@@ -457,40 +440,58 @@
             )
     tile_of = lax.broadcasted_iota(jnp.int32, (TILE, n), 1) // TILE
 
-    @pl.loop(0, count)
-    def _(k):
-        first = pl.multiple_of(k * TILE, TILE)
-        d_ref[...] = s_ref[pl.ds(first, TILE), pl.ds(first, TILE)]
-        rows = factor_tile([d_ref[i : i + 8, :] for i in range(0, TILE, 8)])
-        for i in range(TILE // 8):
-            d_ref[8 * i : 8 * i + 8, :] = rows[i]
-        x = d_ref[...]
-        y = jnp.dot(x, s_ref[pl.ds(first, TILE), :], precision=HI, preferred_element_type=jnp.float32)
-        y = jnp.where(tile_of == k, jnp.concatenate([x] * count, 1), y)
-        l_ref[pl.ds(first, TILE), :] = jnp.where(tile_of <= k, y, 0.0)
-        for i in range(1, count):
-
-            @pl.when(i > k)
-            def _():
-                change = lax.dot_general(
-                    y[:, i * TILE : (i + 1) * TILE],
-                    y,
-                    (((0,), (0,)), ((), ())),
-                    precision=HI,
-                    preferred_element_type=jnp.float32,
+    def times_transposed(a, b):
+        return lax.dot_general(
+            a, b, (((0,), (0,)), ((), ())), precision=HI, preferred_element_type=jnp.float32
+        )
+
+    tile = s_ref[:TILE, :TILE]
+    for k in range(count):
+        first = k * TILE
+        after = first + TILE
+        rows = factor_tile([tile[i : i + 8, :] for i in range(0, TILE, 8)])
+        x = jnp.concatenate(rows, 0)
+        l_ref[first:after, first:after] = x
+        pieces = {k: x}
+        for t in [*range(k + 1, count), *range(k)]:
+            pieces[t] = jnp.dot(
+                x,
+                s_ref[first:after, t * TILE : (t + 1) * TILE],
+                precision=HI,
+                preferred_element_type=jnp.float32,
+            )
+            if t == k + 1:
+                tile = s_ref[after : after + TILE, after : after + TILE] - times_transposed(
+                    pieces[t], pieces[t]
                 )
-                old = s_ref[i * TILE : (i + 1) * TILE, :]
-                s_ref[i * TILE : (i + 1) * TILE, :] = jnp.where(tile_of == k, 0.0, old) - change
+            if t < k:
+                l_ref[first:after, t * TILE : (t + 1) * TILE] = pieces[t]
+        for t in range(k + 1, count):
+            l_ref[first:after, t * TILE : (t + 1) * TILE] = jnp.zeros((TILE, TILE), jnp.float32)
+        for i in range(k + 1, count):
+            for t in range(count):
+                if k < t < i or i == t == k + 1:
+                    continue
+                change = times_transposed(pieces[i], pieces[t])
+                span = (slice(i * TILE, (i + 1) * TILE), slice(t * TILE, (t + 1) * TILE))
+                s_ref[span] = -change if t == k else s_ref[span] - change
 
     place_beams(group_ref[0], groups, beam_refs, b_ref)
     mine = o_ref.shape[0]
-    o_ref[...] = lax.dot_general(
-        l_ref[pl.ds(pl.multiple_of(group_ref[0] * mine, 8), mine), :],
-        b_ref[...],
-        (((1,), (1,)), ((), ())),
-        precision=HI,
-        preferred_element_type=jnp.float32,
-    )
+    left_high, left_low = split(l_ref[pl.ds(pl.multiple_of(group_ref[0] * mine, 8), mine), :])
+    right_high, right_low = split(b_ref[...])
+    o_ref[...] = (
+        product_nt(left_high, right_low) + product_nt(left_low, right_high)
+    ) + product_nt(left_high, right_high)
+
+
+def split(x):
+    high = x.astype(jnp.bfloat16)
+    return high, (x - high.astype(jnp.float32)).astype(jnp.bfloat16)
+
+
+def product_nt(a, b):
+    return lax.dot_general(a, b, (((1,), (1,)), ((), ())), preferred_element_type=jnp.float32)
 
 
 def place_beams(group, groups, beam_refs, b_ref):
@@ -542,7 +543,7 @@
     half = share // 2
     with jax.named_scope("halo"):
         halo = shifted(samples[row_count - LEAD :], "tm", 1)
-    args = (group, halo, samples, taps_weight, retain)
+    args = (group, halo, widened(samples, taps_weight), taps_weight, retain)
     down, up, far_down, far_up = fir(
         (-1, -3, 1, 3, 4), (2 * share, 2 * share, half, half), False, *args
     )

time: 146 us -> 146 us (level)
  Pallas kernels: 27.8 us -> 21.3 us
  waiting for transfers between devices: 23.3 us -> 26.3 us
  blocking collectives: 68.2 us -> 70.2 us
  local copies, waits for them, and re-layouts: 4.25 us -> 5.99 us
    ppermute x12, waiting for transfers between devices: 20.3 us -> 26.3 us  [ring(): lax.ppermute(array, 'elem', [(i, (i + by) % size) for i in range(size)])]
    pallas_call x2, Pallas kernels: 7.46 us -> 3.79 us  [fir(): pl.pallas_call(lambda *refs: fir_body(offsets, weights, *refs), out_shape...]
    ppermute x1, waiting for transfers between devices: 3.04 us -> 0.01 us  [shifted(): return lax.ppermute(array, axis, pairs)]
    pallas_call x1, Pallas kernels: 18.7 us -> 15.8 us  [whitened_rows(): pl.pallas_call(factor_body, out_shape=jax.ShapeDtypeStruct((n // groups,...]
    unnamed x10 -> x8, local copies, waits for them, and re-layouts: 3.48 us -> 5.29 us
  transfers between devices with their start and end apart: 13 -> 13, of which waited for: 8 -> 6; matrix products, arithmetic and copies ran while one was open for 0% -> 0% of each run, Pallas kernels for 1% -> 1%
where the time goes in v6:
time: 146 us
  blocking collectives  70.2 us (48%)
  waiting for transfers between devices  26.3 us (18%)
  starting transfers between devices  21.8 us (15%)
  Pallas kernels  21.3 us (15%)
  local copies, waits for them, and re-layouts  5.99 us (4%)
    ppermute x12, waiting for transfers between devices, ring(): lax.ppermute(array, 'elem', [(i, (i + by) % size) for i in range(size)])  26.3 us
    all_to_all x1, blocking collectives, local(): lax.all_to_all(replicated(returned, groups, low, high), 'elem', 0, 0)  22.2 us
    all_to_all x1, blocking collectives, local(): lax.all_to_all(packed.reshape(groups, packed.shape[0] // groups, TILE), '...  21.3 us
    ppermute x12, starting transfers between devices, ring(): lax.ppermute(array, 'elem', [(i, (i + by) % size) for i in range(size)])  19.9 us
    pallas_call x1, Pallas kernels, whitened_rows(): pl.pallas_call(factor_body, out_shape=jax.ShapeDtypeStruct((n // groups,...  15.8 us
    all_to_all x1, blocking collectives, local(): received = lax.all_to_all(spread, 'tm', 0, 0, tiled=True)  14.3 us
    all_to_all x1, blocking collectives, local(): returned = lax.all_to_all(estimate, 'tm', 0, 0, tiled=True)  12.4 us
    unnamed x8, local copies, waits for them, and re-layouts  5.29 us
  transfers between devices with their start and end apart: 13, of which 6 were waited for; matrix products, arithmetic and copies ran while one was open for 0% of the time, Pallas kernels for 1%

profile of v6, /device:TPU:2, one launch (start us, length us, event | category | flops | bytes accessed | tf_op | source)
XLA Modules:
  0.0 145.7 jit_solution(1474214512131949965)
XLA Ops:
  0.0 0.7 slice.3
  0.7 1.9 %collective-permute-start = (bf16[16,256]{1,0:T(8,128)(2,1)S(1)}, bf16[16,256]{1,0:T(8,128)(2,1)S(1)}, u32[]{:S(2)}, u32[]{:S(2)}) collective-permute-start(bf16[16,256]{1,0:T(8,128)(2,1)S(1)} %slice.3), channel_id=1, source_target_pairs={{0,1},{1,2},{2,3},{3,4},{4,5},{5,6},{6,7},{7,8},{8,9},{9,10},{10,1... | collective-permute-start | bytes 24584 | tf_op jit(solution)/shard_map/halo/ppermute | solution.py:18
  2.6 0.0 copy-start
  2.6 2.2 %copy-done = bf16[16,256,512]{2,1,0:T(8,128)(2,1)S(1)} copy-done((bf16[16,256,512]{2,1,0:T(8,128)(2,1)S(1)}, bf16[16,256,512]{2,1,0:T(8,128)(2,1)}, u32[]{:S(2)}) %copy-start) | copy-done | bytes 4194328
  4.8 0.0 copy-start.2
  4.8 1.0 copy-done.2
  5.8 0.0 copy-start.1
  5.8 0.1 widened.1.refs_2_
  5.9 0.0 copy-start.3
  5.9 0.0 collective-permute-done.refs_1_
  5.9 2.1 %copy-done.1 = bf16[16,256,512]{2,1,0:T(8,128)(2,1)S(1)} copy-done((bf16[16,256,512]{2,1,0:T(8,128)(2,1)S(1)}, bf16[16,256,512]{2,1,0:T(8,128)(2,1)}, u32[]{:S(2)}) %copy-start.1) | copy-done | bytes 4194328
  8.0 2.3 %fir_sent.1 = (f32[192,512]{1,0:T(8,128)S(1)}, f32[192,512]{1,0:T(8,128)S(1)}, f32[48,512]{1,0:T(8,128)S(1)}, f32[48,512]{1,0:T(8,128)S(1)}) custom-call(s32[1]{0:T(128)} %bitcast.refs_0_.group_ref, bf16[16,256]{1,0:T(8,128)(2,1)S(1)} %collective-permute-done.refs_1_, f32[768,256]{1,0:T(8,128)S(1)} %widened.1.refs_2_, bf16[16,256,512]{2,1,0:T(8,128)(2,1)S(1)} %copy-done.1), custom_call_target="tpu_custom_call" | custom-call | flops 2013265920 | bytes 6291456 | tf_op jit(solution)/shard_map/fir_sent/pallas_call | solution.py:116
  10.3 5.9 %collective-permute-start.1 = (f32[192,512]{1,0:T(8,128)S(1)}, f32[192,512]{1,0:T(8,128)S(1)}, u32[]{:S(2)}, u32[]{:S(2)}) collective-permute-start(f32[192,512]{1,0:T(8,128)S(1)} %get-tuple-element.23), channel_id=1, source_target_pairs={{0,224},{32,0},{64,32},{96,64},{128,96},{160,128},{192,160},{224,1... | collective-permute-start | bytes 1179656 | tf_op jit(solution)/shard_map/beams_near/ppermute | solution.py:137
  16.2 0.0 collective-permute-start.2
  16.2 2.5 %collective-permute-start.3 = (f32[48,512]{1,0:T(8,128)S(1)}, f32[48,512]{1,0:T(8,128)S(1)}, u32[]{:S(2)}, u32[]{:S(2)}) collective-permute-start(f32[48,512]{1,0:T(8,128)S(1)} %get-tuple-element.25), channel_id=1, source_target_pairs={{0,192},{32,224},{64,0},{96,32},{128,64},{160,96},{192,128},{224,1... | collective-permute-start | bytes 294920 | tf_op jit(solution)/shard_map/beams_near/ppermute | solution.py:137
  18.7 0.5 collective-permute-start.4
  19.2 0.0 copy-done.3
  19.2 1.5 %fir_rest.1 = (f32[288,512]{1,0:T(8,128)S(1)}, f32[96,128]{1,0:T(8,128)S(1)}, f32[1,128]{1,0:T(1,128)S(1)}) custom-call(s32[1]{0:T(128)} %bitcast.refs_0_.group_ref, bf16[16,256]{1,0:T(8,128)(2,1)S(1)} %collective-permute-done.refs_1_, f32[768,256]{1,0:T(8,128)S(1)} %widened.1.refs_2_, bf16[16,256,512]{2,1,0:T(8,128)(2,1)S(1)} %copy-done.1, f32[768]{0:T(1024)S(1)} %copy-done.3), custom_call_target="tpu_custom_call" | custom-call | flops 1207959552 | bytes 6291456 | tf_op jit(solution)/shard_map/fir_rest/pallas_call | solution.py:116
  20.7 8.7 %collective-permute-done.3.far_down_ref = f32[48,512]{1,0:T(8,128)S(1)} collective-permute-done((f32[48,512]{1,0:T(8,128)S(1)}, f32[48,512]{1,0:T(8,128)S(1)}, u32[]{:S(2)}, u32[]{:S(2)}) %collective-permute-start.3) | collective-permute-done | bytes 98336 | tf_op jit(solution)/shard_map/beams_near/ppermute | solution.py:137
  29.4 2.0 %collective-permute-done.4.far_up_ref = f32[48,512]{1,0:T(8,128)S(1)} collective-permute-done((f32[48,512]{1,0:T(8,128)S(1)}, f32[48,512]{1,0:T(8,128)S(1)}, u32[]{:S(2)}, u32[]{:S(2)}) %collective-permute-start.4) | collective-permute-done | bytes 98336 | tf_op jit(solution)/shard_map/beams_near/ppermute | solution.py:137
  31.4 0.0 collective-permute-done.1.down_ref
  31.4 0.0 collective-permute-done.2.up_ref
  31.4 0.1 relay_sums.1
  31.5 2.7 %collective-permute-start.5 = (f32[96,512]{1,0:T(8,128)S(1)}, f32[96,512]{1,0:T(8,128)S(1)}, u32[]{:S(2)}, u32[]{:S(2)}) collective-permute-start(f32[96,512]{1,0:T(8,128)S(1)} %get-tuple-element.27), channel_id=1, source_target_pairs={{0,192},{32,224},{64,0},{96,32},{128,64},{160,96},{192,128},{224,1... | collective-permute-start | bytes 589832 | tf_op jit(solution)/shard_map/beams_far/ppermute | solution.py:137
  34.2 0.3 collective-permute-start.6
  34.5 8.6 %collective-permute-done.5.low_ref = f32[96,512]{1,0:T(8,128)S(1)} collective-permute-done((f32[96,512]{1,0:T(8,128)S(1)}, f32[96,512]{1,0:T(8,128)S(1)}, u32[]{:S(2)}, u32[]{:S(2)}) %collective-permute-start.5) | collective-permute-done | bytes 196640 | tf_op jit(solution)/shard_map/beams_far/ppermute | solution.py:137
  43.1 4.2 %collective-permute-done.6.high_ref = f32[96,512]{1,0:T(8,128)S(1)} collective-permute-done((f32[96,512]{1,0:T(8,128)S(1)}, f32[96,512]{1,0:T(8,128)S(1)}, u32[]{:S(2)}, u32[]{:S(2)}) %collective-permute-start.6) | collective-permute-done | bytes 196640 | tf_op jit(solution)/shard_map/beams_far/ppermute | solution.py:137
  47.3 0.8 packed_gram.1
  48.1 21.3 %all_to_all.20.p_ref = f32[8,144,128]{2,1,0:T(8,128)S(1)} all-to-all(f32[8,144,128]{2,1,0:T(8,128)S(1)} %bitcast.2), channel_id=1, replica_groups=mesh['elem'=8,'tm'=32] {'elem'}, dimensions={0} | all-to-all | bytes 1179648 | tf_op jit(solution)/shard_map/gram_sum/all_to_all | solution.py:559
  69.5 0.1 spread_share.1
  69.6 0.5 collective-permute-start.10
  70.0 0.7 collective-permute-start.9
  70.8 1.8 %collective-permute-start.8 = (f32[96,512]{1,0:T(8,128)S(1)}, f32[96,512]{1,0:T(8,128)S(1)}, u32[]{:S(2)}, u32[]{:S(2)}) collective-permute-start(f32[96,512]{1,0:T(8,128)S(1)} %get-tuple-element.33.refs_0_), channel_id=1, source_target_pairs={{0,64},{32,96},{64,128},{96,160},{128,192},{160,224},{192,0},{224,... | collective-permute-start | bytes 589832 | tf_op jit(solution)/shard_map/beams_gather/ppermute | solution.py:137
  72.6 2.0 %collective-permute-start.7 = (f32[96,512]{1,0:T(8,128)S(1)}, f32[96,512]{1,0:T(8,128)S(1)}, u32[]{:S(2)}, u32[]{:S(2)}) collective-permute-start(f32[96,512]{1,0:T(8,128)S(1)} %get-tuple-element.33.refs_0_), channel_id=1, source_target_pairs={{0,32},{32,64},{64,96},{96,128},{128,160},{160,192},{192,224},{224... | collective-permute-start | bytes 589832 | tf_op jit(solution)/shard_map/beams_gather/ppermute | solution.py:137
  74.6 14.3 %all_to_all.21.r_ref = f32[32,5,128]{2,1,0:T(8,128)S(1)} all-to-all(f32[32,5,128]{2,1,0:T(8,128)S(1)} %get-tuple-element.32), channel_id=1, replica_groups=mesh['elem'=8,'tm'=32] {'tm'}, dimensions={0} | all-to-all | bytes 163840 | tf_op jit(solution)/shard_map/blocks_out/all_to_all | solution.py:567
  88.9 0.0 collective-permute-done.10.from_above2.refs_4_
  88.9 0.0 collective-permute-done.9.from_above.refs_3_
  88.9 0.0 collective-permute-done.8.from_below2.refs_2_
  88.9 0.0 collective-permute-done.7.from_below.refs_1_
  88.9 0.6 decayed_sums.1
  89.4 1.7 %collective-permute-start.11 = (f32[144,512]{1,0:T(8,128)S(1)}, f32[144,512]{1,0:T(8,128)S(1)}, u32[]{:S(2)}, u32[]{:S(2)}) collective-permute-start(f32[144,512]{1,0:T(8,128)S(1)} %get-tuple-element.35), channel_id=1, source_target_pairs={{0,192},{32,224},{64,0},{96,32},{128,64},{160,96},{192,128},{224,1... | collective-permute-start | bytes 884744 | tf_op jit(solution)/shard_map/beams_gather/ppermute | solution.py:137
  91.1 1.3 collective-permute-start.12
  92.4 12.4 %all_to_all.22.r_ref = f32[32,5,128]{2,1,0:T(8,128)S(1)} all-to-all(f32[32,5,128]{2,1,0:T(8,128)S(1)} %get-tuple-element.34), channel_id=1, replica_groups=mesh['elem'=8,'tm'=32] {'tm'}, dimensions={0} | all-to-all | bytes 163840 | tf_op jit(solution)/shard_map/blocks_back/all_to_all | solution.py:572
  104.8 1.0 collective-permute-done.11.low_ref.refs_5_
  105.8 1.7 %collective-permute-done.12.high_ref.refs_6_ = f32[144,512]{1,0:T(8,128)S(1)} collective-permute-done((f32[144,512]{1,0:T(8,128)S(1)}, f32[144,512]{1,0:T(8,128)S(1)}, u32[]{:S(2)}, u32[]{:S(2)}) %collective-permute-start.12) | collective-permute-done | bytes 294944 | tf_op jit(solution)/shard_map/beams_gather/ppermute | solution.py:137
  107.5 0.2 replicated.1
  107.7 22.2 %all_to_all.23.p_ref = f32[8,144,128]{2,1,0:T(8,128)S(1)} all-to-all(f32[8,144,128]{2,1,0:T(8,128)S(1)} %replicated.1), channel_id=1, replica_groups=mesh['elem'=8,'tm'=32] {'elem'}, dimensions={0} | all-to-all | bytes 1179648 | tf_op jit(solution)/shard_map/gram_gather/all_to_all | solution.py:574
  129.9 15.8 %whitened_rows.1 = f32[64,768]{1,0:T(8,128)} custom-call(s32[1]{0:T(128)} %bitcast.refs_0_.group_ref, f32[8,144,128]{2,1,0:T(8,128)S(1)} %all_to_all.23.p_ref, f32[96,512]{1,0:T(8,128)S(1)} %get-tuple-element.33.refs_0_, f32[96,512]{1,0:T(8,128)S(1)} %collective-permute-done.7.from_below.refs_1_, f32[96,512]{1,0:T(8,128)S(1)} %collective-permute-done.8.from_below2.refs_2_, ...), custom_call_target="tpu_custom_call" | custom-call | flops 1610612736 | bytes 1048576 | tf_op jit(solution)/shard_map/whitened_rows/pallas_call | solution.py:521
Async XLA Ops:
  0.7 5.2 %collective-permute-start = (bf16[16,256]{1,0:T(8,128)(2,1)S(1)}, bf16[16,256]{1,0:T(8,128)(2,1)S(1)}, u32[]{:S(2)}, u32[]{:S(2)}) collective-permute-start(bf16[16,256]{1,0:T(8,128)(2,1)S(1)} %slice.3), channel_id=1, source_target_pairs={{0,1},{1,2},{2,3},{3,4},{4,5},{5,6},{6,7},{7,8},{8,9},{9,10},{10,1... | collective-permute-start | bytes 24584 | tf_op jit(solution)/shard_map/halo/ppermute | solution.py:18
  2.6 2.2 %copy-start = (bf16[16,256,512]{2,1,0:T(8,128)(2,1)S(1)}, bf16[16,256,512]{2,1,0:T(8,128)(2,1)}, u32[]{:S(2)}) copy-start(bf16[16,256,512]{2,1,0:T(8,128)(2,1)} %refs_3_.3) | copy-start | bytes 12582916
  4.8 1.0 copy-start.2
  5.8 2.2 %copy-start.1 = (bf16[16,256,512]{2,1,0:T(8,128)(2,1)S(1)}, bf16[16,256,512]{2,1,0:T(8,128)(2,1)}, u32[]{:S(2)}) copy-start(bf16[16,256,512]{2,1,0:T(8,128)(2,1)} %refs_3_.3) | copy-start | bytes 12582916
  5.9 13.3 %copy-start.3 = (f32[768]{0:T(1024)S(1)}, f32[768]{0:T(1024)}, u32[]{:S(2)}) copy-start(f32[768]{0:T(1024)} %refs_4_.1) | copy-start | bytes 9220
  10.3 21.1 %collective-permute-start.1 = (f32[192,512]{1,0:T(8,128)S(1)}, f32[192,512]{1,0:T(8,128)S(1)}, u32[]{:S(2)}, u32[]{:S(2)}) collective-permute-start(f32[192,512]{1,0:T(8,128)S(1)} %get-tuple-element.23), channel_id=1, source_target_pairs={{0,224},{32,0},{64,32},{96,64},{128,96},{160,128},{192,160},{224,1... | collective-permute-start | bytes 1179656 | tf_op jit(solution)/shard_map/beams_near/ppermute | solution.py:137
  16.2 15.2 %collective-permute-start.2 = (f32[192,512]{1,0:T(8,128)S(1)}, f32[192,512]{1,0:T(8,128)S(1)}, u32[]{:S(2)}, u32[]{:S(2)}) collective-permute-start(f32[192,512]{1,0:T(8,128)S(1)} %get-tuple-element.24), channel_id=1, source_target_pairs={{0,32},{32,64},{64,96},{96,128},{128,160},{160,192},{192,224},{224... | collective-permute-start | bytes 1179656 | tf_op jit(solution)/shard_map/beams_near/ppermute | solution.py:137
  16.2 13.1 %collective-permute-start.3 = (f32[48,512]{1,0:T(8,128)S(1)}, f32[48,512]{1,0:T(8,128)S(1)}, u32[]{:S(2)}, u32[]{:S(2)}) collective-permute-start(f32[48,512]{1,0:T(8,128)S(1)} %get-tuple-element.25), channel_id=1, source_target_pairs={{0,192},{32,224},{64,0},{96,32},{128,64},{160,96},{192,128},{224,1... | collective-permute-start | bytes 294920 | tf_op jit(solution)/shard_map/beams_near/ppermute | solution.py:137
  18.7 12.7 %collective-permute-start.4 = (f32[48,512]{1,0:T(8,128)S(1)}, f32[48,512]{1,0:T(8,128)S(1)}, u32[]{:S(2)}, u32[]{:S(2)}) collective-permute-start(f32[48,512]{1,0:T(8,128)S(1)} %get-tuple-element.26), channel_id=1, source_target_pairs={{0,64},{32,96},{64,128},{96,160},{128,192},{160,224},{192,0},{224,... | collective-permute-start | bytes 294920 | tf_op jit(solution)/shard_map/beams_near/ppermute | solution.py:137
  31.5 11.6 %collective-permute-start.5 = (f32[96,512]{1,0:T(8,128)S(1)}, f32[96,512]{1,0:T(8,128)S(1)}, u32[]{:S(2)}, u32[]{:S(2)}) collective-permute-start(f32[96,512]{1,0:T(8,128)S(1)} %get-tuple-element.27), channel_id=1, source_target_pairs={{0,192},{32,224},{64,0},{96,32},{128,64},{160,96},{192,128},{224,1... | collective-permute-start | bytes 589832 | tf_op jit(solution)/shard_map/beams_far/ppermute | solution.py:137
  34.2 13.2 %collective-permute-start.6 = (f32[96,512]{1,0:T(8,128)S(1)}, f32[96,512]{1,0:T(8,128)S(1)}, u32[]{:S(2)}, u32[]{:S(2)}) collective-permute-start(f32[96,512]{1,0:T(8,128)S(1)} %get-tuple-element.28), channel_id=1, source_target_pairs={{0,64},{32,96},{64,128},{96,160},{128,192},{160,224},{192,0},{224,... | collective-permute-start | bytes 589832 | tf_op jit(solution)/shard_map/beams_far/ppermute | solution.py:137
  69.6 19.3 %collective-permute-start.10 = (f32[96,512]{1,0:T(8,128)S(1)}, f32[96,512]{1,0:T(8,128)S(1)}, u32[]{:S(2)}, u32[]{:S(2)}) collective-permute-start(f32[96,512]{1,0:T(8,128)S(1)} %get-tuple-element.33.refs_0_), channel_id=1, source_target_pairs={{0,192},{32,224},{64,0},{96,32},{128,64},{160,96},{192,128},{224,1... | collective-permute-start | bytes 589832 | tf_op jit(solution)/shard_map/beams_gather/ppermute | solution.py:137
  70.0 18.8 %collective-permute-start.9 = (f32[96,512]{1,0:T(8,128)S(1)}, f32[96,512]{1,0:T(8,128)S(1)}, u32[]{:S(2)}, u32[]{:S(2)}) collective-permute-start(f32[96,512]{1,0:T(8,128)S(1)} %get-tuple-element.33.refs_0_), channel_id=1, source_target_pairs={{0,224},{32,0},{64,32},{96,64},{128,96},{160,128},{192,160},{224,1... | collective-permute-start | bytes 589832 | tf_op jit(solution)/shard_map/beams_gather/ppermute | solution.py:137
  70.8 18.1 %collective-permute-start.8 = (f32[96,512]{1,0:T(8,128)S(1)}, f32[96,512]{1,0:T(8,128)S(1)}, u32[]{:S(2)}, u32[]{:S(2)}) collective-permute-start(f32[96,512]{1,0:T(8,128)S(1)} %get-tuple-element.33.refs_0_), channel_id=1, source_target_pairs={{0,64},{32,96},{64,128},{96,160},{128,192},{160,224},{192,0},{224,... | collective-permute-start | bytes 589832 | tf_op jit(solution)/shard_map/beams_gather/ppermute | solution.py:137
  72.6 16.3 %collective-permute-start.7 = (f32[96,512]{1,0:T(8,128)S(1)}, f32[96,512]{1,0:T(8,128)S(1)}, u32[]{:S(2)}, u32[]{:S(2)}) collective-permute-start(f32[96,512]{1,0:T(8,128)S(1)} %get-tuple-element.33.refs_0_), channel_id=1, source_target_pairs={{0,32},{32,64},{64,96},{96,128},{128,160},{160,192},{192,224},{224... | collective-permute-start | bytes 589832 | tf_op jit(solution)/shard_map/beams_gather/ppermute | solution.py:137
  89.4 16.4 %collective-permute-start.11 = (f32[144,512]{1,0:T(8,128)S(1)}, f32[144,512]{1,0:T(8,128)S(1)}, u32[]{:S(2)}, u32[]{:S(2)}) collective-permute-start(f32[144,512]{1,0:T(8,128)S(1)} %get-tuple-element.35), channel_id=1, source_target_pairs={{0,192},{32,224},{64,0},{96,32},{128,64},{160,96},{192,128},{224,1... | collective-permute-start | bytes 884744 | tf_op jit(solution)/shard_map/beams_gather/ppermute | solution.py:137
  91.1 16.4 %collective-permute-start.12 = (f32[144,512]{1,0:T(8,128)S(1)}, f32[144,512]{1,0:T(8,128)S(1)}, u32[]{:S(2)}, u32[]{:S(2)}) collective-permute-start(f32[144,512]{1,0:T(8,128)S(1)} %get-tuple-element.36), channel_id=1, source_target_pairs={{0,64},{32,96},{64,128},{96,160},{128,192},{160,224},{192,0},{224,... | collective-permute-start | bytes 884744 | tf_op jit(solution)/shard_map/beams_gather/ppermute | solution.py:137

commit v7 on v5

--- a/solution.py
+++ b/solution.py
@@ -457,40 +457,58 @@
             )
     tile_of = lax.broadcasted_iota(jnp.int32, (TILE, n), 1) // TILE
 
-    @pl.loop(0, count)
-    def _(k):
-        first = pl.multiple_of(k * TILE, TILE)
-        d_ref[...] = s_ref[pl.ds(first, TILE), pl.ds(first, TILE)]
-        rows = factor_tile([d_ref[i : i + 8, :] for i in range(0, TILE, 8)])
-        for i in range(TILE // 8):
-            d_ref[8 * i : 8 * i + 8, :] = rows[i]
-        x = d_ref[...]
-        y = jnp.dot(x, s_ref[pl.ds(first, TILE), :], precision=HI, preferred_element_type=jnp.float32)
-        y = jnp.where(tile_of == k, jnp.concatenate([x] * count, 1), y)
-        l_ref[pl.ds(first, TILE), :] = jnp.where(tile_of <= k, y, 0.0)
-        for i in range(1, count):
-
-            @pl.when(i > k)
-            def _():
-                change = lax.dot_general(
-                    y[:, i * TILE : (i + 1) * TILE],
-                    y,
-                    (((0,), (0,)), ((), ())),
-                    precision=HI,
-                    preferred_element_type=jnp.float32,
+    def times_transposed(a, b):
+        return lax.dot_general(
+            a, b, (((0,), (0,)), ((), ())), precision=HI, preferred_element_type=jnp.float32
+        )
+
+    tile = s_ref[:TILE, :TILE]
+    for k in range(count):
+        first = k * TILE
+        after = first + TILE
+        rows = factor_tile([tile[i : i + 8, :] for i in range(0, TILE, 8)])
+        x = jnp.concatenate(rows, 0)
+        l_ref[first:after, first:after] = x
+        pieces = {k: x}
+        for t in [*range(k + 1, count), *range(k)]:
+            pieces[t] = jnp.dot(
+                x,
+                s_ref[first:after, t * TILE : (t + 1) * TILE],
+                precision=HI,
+                preferred_element_type=jnp.float32,
+            )
+            if t == k + 1:
+                tile = s_ref[after : after + TILE, after : after + TILE] - times_transposed(
+                    pieces[t], pieces[t]
                 )
-                old = s_ref[i * TILE : (i + 1) * TILE, :]
-                s_ref[i * TILE : (i + 1) * TILE, :] = jnp.where(tile_of == k, 0.0, old) - change
+            if t < k:
+                l_ref[first:after, t * TILE : (t + 1) * TILE] = pieces[t]
+        for t in range(k + 1, count):
+            l_ref[first:after, t * TILE : (t + 1) * TILE] = jnp.zeros((TILE, TILE), jnp.float32)
+        for i in range(k + 1, count):
+            for t in range(count):
+                if k < t < i or i == t == k + 1:
+                    continue
+                change = times_transposed(pieces[i], pieces[t])
+                span = (slice(i * TILE, (i + 1) * TILE), slice(t * TILE, (t + 1) * TILE))
+                s_ref[span] = -change if t == k else s_ref[span] - change
 
     place_beams(group_ref[0], groups, beam_refs, b_ref)
     mine = o_ref.shape[0]
-    o_ref[...] = lax.dot_general(
-        l_ref[pl.ds(pl.multiple_of(group_ref[0] * mine, 8), mine), :],
-        b_ref[...],
-        (((1,), (1,)), ((), ())),
-        precision=HI,
-        preferred_element_type=jnp.float32,
-    )
+    left_high, left_low = split(l_ref[pl.ds(pl.multiple_of(group_ref[0] * mine, 8), mine), :])
+    right_high, right_low = split(b_ref[...])
+    o_ref[...] = (
+        product_nt(left_high, right_low) + product_nt(left_low, right_high)
+    ) + product_nt(left_high, right_high)
+
+
+def split(x):
+    high = x.astype(jnp.bfloat16)
+    return high, (x - high.astype(jnp.float32)).astype(jnp.bfloat16)
+
+
+def product_nt(a, b):
+    return lax.dot_general(a, b, (((1,), (1,)), ((), ())), preferred_element_type=jnp.float32)
 
 
 def place_beams(group, groups, beam_refs, b_ref):

time: 146 us -> 143 us (0.979)
  Pallas kernels: 27.8 us -> 24.9 us
    pallas_call x1, Pallas kernels: 18.7 us -> 15.8 us  [whitened_rows(): pl.pallas_call(factor_body, out_shape=jax.ShapeDtypeStruct((n // groups,...]
where the time goes in v7:
time: 143 us
  blocking collectives  68.2 us (48%)
  Pallas kernels  24.9 us (17%)
  waiting for transfers between devices  23.3 us (16%)
  starting transfers between devices  21.8 us (15%)
  local copies, waits for them, and re-layouts  4.25 us (3%)
    all_to_all x1, blocking collectives, local(): lax.all_to_all(replicated(returned, groups, low, high), 'elem', 0, 0)  22.2 us
    all_to_all x1, blocking collectives, local(): lax.all_to_all(packed.reshape(groups, packed.shape[0] // groups, TILE), '...  20.5 us
    ppermute x12, waiting for transfers between devices, ring(): lax.ppermute(array, 'elem', [(i, (i + by) % size) for i in range(size)])  20.3 us
    ppermute x12, starting transfers between devices, ring(): lax.ppermute(array, 'elem', [(i, (i + by) % size) for i in range(size)])  19.9 us
    pallas_call x1, Pallas kernels, whitened_rows(): pl.pallas_call(factor_body, out_shape=jax.ShapeDtypeStruct((n // groups,...  15.8 us
    all_to_all x1, blocking collectives, local(): received = lax.all_to_all(spread, 'tm', 0, 0, tiled=True)  13.6 us
    all_to_all x1, blocking collectives, local(): returned = lax.all_to_all(estimate, 'tm', 0, 0, tiled=True)  11.9 us
    pallas_call x2, Pallas kernels, fir(): pl.pallas_call(lambda *refs: fir_body(offsets, weights, *refs), out_shape...  7.46 us
  transfers between devices with their start and end apart: 13, of which 8 were waited for; matrix products, arithmetic and copies ran while one was open for 0% of the time, Pallas kernels for 1%

profile of v7, /device:TPU:2, one launch (start us, length us, event | category | flops | bytes accessed | tf_op | source)
XLA Modules:
  0.0 142.7 jit_solution(13866141630218159808)
XLA Ops:
  0.0 0.0 copy-start.1
  0.0 0.0 copy-start.4
  0.0 0.8 slice.3
  0.8 1.9 %collective-permute-start = (bf16[16,256]{1,0:T(8,128)(2,1)S(1)}, bf16[16,256]{1,0:T(8,128)(2,1)S(1)}, u32[]{:S(2)}, u32[]{:S(2)}) collective-permute-start(bf16[16,256]{1,0:T(8,128)(2,1)S(1)} %slice.3), channel_id=1, source_target_pairs={{0,1},{1,2},{2,3},{3,4},{4,5},{5,6},{6,7},{7,8},{8,9},{9,10},{10,1... | collective-permute-start | bytes 24584 | tf_op jit(solution)/shard_map/halo/ppermute | solution.py:18
  2.7 3.0 %collective-permute-done.refs_1_ = bf16[16,256]{1,0:T(8,128)(2,1)S(1)} collective-permute-done((bf16[16,256]{1,0:T(8,128)(2,1)S(1)}, bf16[16,256]{1,0:T(8,128)(2,1)S(1)}, u32[]{:S(2)}, u32[]{:S(2)}) %collective-permute-start) | collective-permute-done | bytes 8224 | tf_op jit(solution)/shard_map/halo/ppermute | solution.py:18
  5.7 0.0 copy-start.2
  5.7 0.6 copy-done.2
  6.3 6.0 %fir_sent.1 = (f32[192,512]{1,0:T(8,128)}, f32[192,512]{1,0:T(8,128)}, f32[48,512]{1,0:T(8,128)}, f32[48,512]{1,0:T(8,128)}) custom-call(s32[1]{0:T(128)} %bitcast.refs_0_.group_ref, bf16[16,256]{1,0:T(8,128)(2,1)} %copy-done.2, bf16[768,256]{1,0:T(8,128)(2,1)} %refs_2_.3, bf16[16,256,512]{2,1,0:T(8,128)(2,1)} %refs_3_.3), custom_call_target="tpu_custom_call" | custom-call | flops 2013265920 | bytes 6291456 | tf_op jit(solution)/shard_map/fir_sent/pallas_call | solution.py:136
  12.3 5.9 %collective-permute-start.1 = (f32[192,512]{1,0:T(8,128)}, f32[192,512]{1,0:T(8,128)S(1)}, u32[]{:S(2)}, u32[]{:S(2)}) collective-permute-start(f32[192,512]{1,0:T(8,128)} %get-tuple-element.23), channel_id=1, source_target_pairs={{0,224},{32,0},{64,32},{96,64},{128,96},{160,128},{192,160},{224,1... | collective-permute-start | bytes 1179656 | tf_op jit(solution)/shard_map/beams_near/ppermute | solution.py:154
  18.3 0.0 collective-permute-start.2
  18.3 2.5 %collective-permute-start.3 = (f32[48,512]{1,0:T(8,128)}, f32[48,512]{1,0:T(8,128)S(1)}, u32[]{:S(2)}, u32[]{:S(2)}) collective-permute-start(f32[48,512]{1,0:T(8,128)} %get-tuple-element.25), channel_id=1, source_target_pairs={{0,192},{32,224},{64,0},{96,32},{128,64},{160,96},{192,128},{224,1... | collective-permute-start | bytes 294920 | tf_op jit(solution)/shard_map/beams_near/ppermute | solution.py:154
  20.7 0.5 collective-permute-start.4
  21.2 0.0 copy-done.1
  21.2 0.0 copy-done.4
  21.2 0.0 copy-start
  21.2 2.2 %copy-done = bf16[16,256,512]{2,1,0:T(8,128)(2,1)S(1)} copy-done((bf16[16,256,512]{2,1,0:T(8,128)(2,1)S(1)}, bf16[16,256,512]{2,1,0:T(8,128)(2,1)}, u32[]{:S(2)}) %copy-start) | copy-done | bytes 4194328
  23.4 0.0 copy-start.3
  23.4 0.7 copy-done.3
  24.1 1.5 %fir_rest.1 = (f32[288,512]{1,0:T(8,128)S(1)}, f32[96,128]{1,0:T(8,128)S(1)}, f32[1,128]{1,0:T(1,128)S(1)}) custom-call(s32[1]{0:T(128)} %bitcast.refs_0_.group_ref, bf16[16,256]{1,0:T(8,128)(2,1)S(1)} %copy-done.3, bf16[768,256]{1,0:T(8,128)(2,1)S(1)} %copy-done.1, bf16[16,256,512]{2,1,0:T(8,128)(2,1)S(1)} %copy-done, f32[768]{0:T(1024)S(1)} %copy-done.4), custom_call_target="tpu_custom_call" | custom-call | flops 1207959552 | bytes 6291456 | tf_op jit(solution)/shard_map/fir_rest/pallas_call | solution.py:136
  25.6 5.1 %collective-permute-done.3.far_down_ref = f32[48,512]{1,0:T(8,128)S(1)} collective-permute-done((f32[48,512]{1,0:T(8,128)}, f32[48,512]{1,0:T(8,128)S(1)}, u32[]{:S(2)}, u32[]{:S(2)}) %collective-permute-start.3) | collective-permute-done | bytes 98336 | tf_op jit(solution)/shard_map/beams_near/ppermute | solution.py:154
  30.6 2.0 %collective-permute-done.4.far_up_ref = f32[48,512]{1,0:T(8,128)S(1)} collective-permute-done((f32[48,512]{1,0:T(8,128)}, f32[48,512]{1,0:T(8,128)S(1)}, u32[]{:S(2)}, u32[]{:S(2)}) %collective-permute-start.4) | collective-permute-done | bytes 98336 | tf_op jit(solution)/shard_map/beams_near/ppermute | solution.py:154
  32.6 0.0 collective-permute-done.1.down_ref
  32.6 0.3 collective-permute-done.2.up_ref
  32.9 0.1 relay_sums.1
  33.0 2.3 %collective-permute-start.5 = (f32[96,512]{1,0:T(8,128)S(1)}, f32[96,512]{1,0:T(8,128)S(1)}, u32[]{:S(2)}, u32[]{:S(2)}) collective-permute-start(f32[96,512]{1,0:T(8,128)S(1)} %get-tuple-element.27), channel_id=1, source_target_pairs={{0,192},{32,224},{64,0},{96,32},{128,64},{160,96},{192,128},{224,1... | collective-permute-start | bytes 589832 | tf_op jit(solution)/shard_map/beams_far/ppermute | solution.py:154
  35.3 0.7 collective-permute-start.6
  36.0 5.9 %collective-permute-done.5.low_ref = f32[96,512]{1,0:T(8,128)S(1)} collective-permute-done((f32[96,512]{1,0:T(8,128)S(1)}, f32[96,512]{1,0:T(8,128)S(1)}, u32[]{:S(2)}, u32[]{:S(2)}) %collective-permute-start.5) | collective-permute-done | bytes 196640 | tf_op jit(solution)/shard_map/beams_far/ppermute | solution.py:154
  41.9 3.9 %collective-permute-done.6.high_ref = f32[96,512]{1,0:T(8,128)S(1)} collective-permute-done((f32[96,512]{1,0:T(8,128)S(1)}, f32[96,512]{1,0:T(8,128)S(1)}, u32[]{:S(2)}, u32[]{:S(2)}) %collective-permute-start.6) | collective-permute-done | bytes 196640 | tf_op jit(solution)/shard_map/beams_far/ppermute | solution.py:154
  45.8 0.8 packed_gram.1
  46.6 20.5 %all_to_all.20.p_ref = f32[8,144,128]{2,1,0:T(8,128)S(1)} all-to-all(f32[8,144,128]{2,1,0:T(8,128)S(1)} %bitcast.2), channel_id=1, replica_groups=mesh['elem'=8,'tm'=32] {'elem'}, dimensions={0} | all-to-all | bytes 1179648 | tf_op jit(solution)/shard_map/gram_sum/all_to_all | solution.py:576
  67.1 0.1 spread_share.1
  67.2 0.5 collective-permute-start.10
  67.7 0.7 collective-permute-start.9
  68.4 1.8 %collective-permute-start.8 = (f32[96,512]{1,0:T(8,128)S(1)}, f32[96,512]{1,0:T(8,128)S(1)}, u32[]{:S(2)}, u32[]{:S(2)}) collective-permute-start(f32[96,512]{1,0:T(8,128)S(1)} %get-tuple-element.33.refs_0_), channel_id=1, source_target_pairs={{0,64},{32,96},{64,128},{96,160},{128,192},{160,224},{192,0},{224,... | collective-permute-start | bytes 589832 | tf_op jit(solution)/shard_map/beams_gather/ppermute | solution.py:154
  70.2 2.0 %collective-permute-start.7 = (f32[96,512]{1,0:T(8,128)S(1)}, f32[96,512]{1,0:T(8,128)S(1)}, u32[]{:S(2)}, u32[]{:S(2)}) collective-permute-start(f32[96,512]{1,0:T(8,128)S(1)} %get-tuple-element.33.refs_0_), channel_id=1, source_target_pairs={{0,32},{32,64},{64,96},{96,128},{128,160},{160,192},{192,224},{224... | collective-permute-start | bytes 589832 | tf_op jit(solution)/shard_map/beams_gather/ppermute | solution.py:154
  72.2 13.6 %all_to_all.21.r_ref = f32[32,5,128]{2,1,0:T(8,128)S(1)} all-to-all(f32[32,5,128]{2,1,0:T(8,128)S(1)} %get-tuple-element.32), channel_id=1, replica_groups=mesh['elem'=8,'tm'=32] {'tm'}, dimensions={0} | all-to-all | bytes 163840 | tf_op jit(solution)/shard_map/blocks_out/all_to_all | solution.py:584
  85.8 0.0 collective-permute-done.10.from_above2.refs_4_
  85.8 0.0 collective-permute-done.9.from_above.refs_3_
  85.9 0.0 collective-permute-done.8.from_below2.refs_2_
  85.9 0.0 collective-permute-done.7.from_below.refs_1_
  85.9 0.5 decayed_sums.1
  86.4 1.7 %collective-permute-start.11 = (f32[144,512]{1,0:T(8,128)S(1)}, f32[144,512]{1,0:T(8,128)S(1)}, u32[]{:S(2)}, u32[]{:S(2)}) collective-permute-start(f32[144,512]{1,0:T(8,128)S(1)} %get-tuple-element.35), channel_id=1, source_target_pairs={{0,192},{32,224},{64,0},{96,32},{128,64},{160,96},{192,128},{224,1... | collective-permute-start | bytes 884744 | tf_op jit(solution)/shard_map/beams_gather/ppermute | solution.py:154
  88.1 1.3 collective-permute-start.12
  89.4 11.9 %all_to_all.22.r_ref = f32[32,5,128]{2,1,0:T(8,128)S(1)} all-to-all(f32[32,5,128]{2,1,0:T(8,128)S(1)} %get-tuple-element.34), channel_id=1, replica_groups=mesh['elem'=8,'tm'=32] {'tm'}, dimensions={0} | all-to-all | bytes 163840 | tf_op jit(solution)/shard_map/blocks_back/all_to_all | solution.py:589
  101.4 1.5 %collective-permute-done.11.low_ref.refs_5_ = f32[144,512]{1,0:T(8,128)S(1)} collective-permute-done((f32[144,512]{1,0:T(8,128)S(1)}, f32[144,512]{1,0:T(8,128)S(1)}, u32[]{:S(2)}, u32[]{:S(2)}) %collective-permute-start.11) | collective-permute-done | bytes 294944 | tf_op jit(solution)/shard_map/beams_gather/ppermute | solution.py:154
  102.8 1.7 %collective-permute-done.12.high_ref.refs_6_ = f32[144,512]{1,0:T(8,128)S(1)} collective-permute-done((f32[144,512]{1,0:T(8,128)S(1)}, f32[144,512]{1,0:T(8,128)S(1)}, u32[]{:S(2)}, u32[]{:S(2)}) %collective-permute-start.12) | collective-permute-done | bytes 294944 | tf_op jit(solution)/shard_map/beams_gather/ppermute | solution.py:154
  104.5 0.2 replicated.1
  104.7 22.2 %all_to_all.23.p_ref = f32[8,144,128]{2,1,0:T(8,128)S(1)} all-to-all(f32[8,144,128]{2,1,0:T(8,128)S(1)} %replicated.1), channel_id=1, replica_groups=mesh['elem'=8,'tm'=32] {'elem'}, dimensions={0} | all-to-all | bytes 1179648 | tf_op jit(solution)/shard_map/gram_gather/all_to_all | solution.py:591
  126.9 15.8 %whitened_rows.1 = f32[64,768]{1,0:T(8,128)} custom-call(s32[1]{0:T(128)} %bitcast.refs_0_.group_ref, f32[8,144,128]{2,1,0:T(8,128)S(1)} %all_to_all.23.p_ref, f32[96,512]{1,0:T(8,128)S(1)} %get-tuple-element.33.refs_0_, f32[96,512]{1,0:T(8,128)S(1)} %collective-permute-done.7.from_below.refs_1_, f32[96,512]{1,0:T(8,128)S(1)} %collective-permute-done.8.from_below2.refs_2_, ...), custom_call_target="tpu_custom_call" | custom-call | flops 1610612736 | bytes 1048576 | tf_op jit(solution)/shard_map/whitened_rows/pallas_call | solution.py:538
Async XLA Ops:
  0.0 21.2 %copy-start.1 = (bf16[768,256]{1,0:T(8,128)(2,1)S(1)}, bf16[768,256]{1,0:T(8,128)(2,1)}, u32[]{:S(2)}) copy-start(bf16[768,256]{1,0:T(8,128)(2,1)} %refs_2_.3) | copy-start | bytes 1179652
  0.0 21.2 %copy-start.4 = (f32[768]{0:T(1024)S(1)}, f32[768]{0:T(1024)}, u32[]{:S(2)}) copy-start(f32[768]{0:T(1024)} %refs_4_.1) | copy-start | bytes 9220
  0.8 5.0 %collective-permute-start = (bf16[16,256]{1,0:T(8,128)(2,1)S(1)}, bf16[16,256]{1,0:T(8,128)(2,1)S(1)}, u32[]{:S(2)}, u32[]{:S(2)}) collective-permute-start(bf16[16,256]{1,0:T(8,128)(2,1)S(1)} %slice.3), channel_id=1, source_target_pairs={{0,1},{1,2},{2,3},{3,4},{4,5},{5,6},{6,7},{7,8},{8,9},{9,10},{10,1... | collective-permute-start | bytes 24584 | tf_op jit(solution)/shard_map/halo/ppermute | solution.py:18
  5.7 0.6 copy-start.2
  12.3 20.3 %collective-permute-start.1 = (f32[192,512]{1,0:T(8,128)}, f32[192,512]{1,0:T(8,128)S(1)}, u32[]{:S(2)}, u32[]{:S(2)}) collective-permute-start(f32[192,512]{1,0:T(8,128)} %get-tuple-element.23), channel_id=1, source_target_pairs={{0,224},{32,0},{64,32},{96,64},{128,96},{160,128},{192,160},{224,1... | collective-permute-start | bytes 1179656 | tf_op jit(solution)/shard_map/beams_near/ppermute | solution.py:154
  18.3 14.6 %collective-permute-start.2 = (f32[192,512]{1,0:T(8,128)}, f32[192,512]{1,0:T(8,128)S(1)}, u32[]{:S(2)}, u32[]{:S(2)}) collective-permute-start(f32[192,512]{1,0:T(8,128)} %get-tuple-element.24), channel_id=1, source_target_pairs={{0,32},{32,64},{64,96},{96,128},{128,160},{160,192},{192,224},{224... | collective-permute-start | bytes 1179656 | tf_op jit(solution)/shard_map/beams_near/ppermute | solution.py:154
  18.3 12.4 %collective-permute-start.3 = (f32[48,512]{1,0:T(8,128)}, f32[48,512]{1,0:T(8,128)S(1)}, u32[]{:S(2)}, u32[]{:S(2)}) collective-permute-start(f32[48,512]{1,0:T(8,128)} %get-tuple-element.25), channel_id=1, source_target_pairs={{0,192},{32,224},{64,0},{96,32},{128,64},{160,96},{192,128},{224,1... | collective-permute-start | bytes 294920 | tf_op jit(solution)/shard_map/beams_near/ppermute | solution.py:154
  20.7 11.9 %collective-permute-start.4 = (f32[48,512]{1,0:T(8,128)}, f32[48,512]{1,0:T(8,128)S(1)}, u32[]{:S(2)}, u32[]{:S(2)}) collective-permute-start(f32[48,512]{1,0:T(8,128)} %get-tuple-element.26), channel_id=1, source_target_pairs={{0,64},{32,96},{64,128},{96,160},{128,192},{160,224},{192,0},{224,... | collective-permute-start | bytes 294920 | tf_op jit(solution)/shard_map/beams_near/ppermute | solution.py:154
  21.2 2.2 %copy-start = (bf16[16,256,512]{2,1,0:T(8,128)(2,1)S(1)}, bf16[16,256,512]{2,1,0:T(8,128)(2,1)}, u32[]{:S(2)}) copy-start(bf16[16,256,512]{2,1,0:T(8,128)(2,1)} %refs_3_.3) | copy-start | bytes 12582916
  23.4 0.7 copy-start.3
  33.0 8.9 %collective-permute-start.5 = (f32[96,512]{1,0:T(8,128)S(1)}, f32[96,512]{1,0:T(8,128)S(1)}, u32[]{:S(2)}, u32[]{:S(2)}) collective-permute-start(f32[96,512]{1,0:T(8,128)S(1)} %get-tuple-element.27), channel_id=1, source_target_pairs={{0,192},{32,224},{64,0},{96,32},{128,64},{160,96},{192,128},{224,1... | collective-permute-start | bytes 589832 | tf_op jit(solution)/shard_map/beams_far/ppermute | solution.py:154
  35.3 10.5 %collective-permute-start.6 = (f32[96,512]{1,0:T(8,128)S(1)}, f32[96,512]{1,0:T(8,128)S(1)}, u32[]{:S(2)}, u32[]{:S(2)}) collective-permute-start(f32[96,512]{1,0:T(8,128)S(1)} %get-tuple-element.28), channel_id=1, source_target_pairs={{0,64},{32,96},{64,128},{96,160},{128,192},{160,224},{192,0},{224,... | collective-permute-start | bytes 589832 | tf_op jit(solution)/shard_map/beams_far/ppermute | solution.py:154
  67.2 18.7 %collective-permute-start.10 = (f32[96,512]{1,0:T(8,128)S(1)}, f32[96,512]{1,0:T(8,128)S(1)}, u32[]{:S(2)}, u32[]{:S(2)}) collective-permute-start(f32[96,512]{1,0:T(8,128)S(1)} %get-tuple-element.33.refs_0_), channel_id=1, source_target_pairs={{0,192},{32,224},{64,0},{96,32},{128,64},{160,96},{192,128},{224,1... | collective-permute-start | bytes 589832 | tf_op jit(solution)/shard_map/beams_gather/ppermute | solution.py:154
  67.7 18.2 %collective-permute-start.9 = (f32[96,512]{1,0:T(8,128)S(1)}, f32[96,512]{1,0:T(8,128)S(1)}, u32[]{:S(2)}, u32[]{:S(2)}) collective-permute-start(f32[96,512]{1,0:T(8,128)S(1)} %get-tuple-element.33.refs_0_), channel_id=1, source_target_pairs={{0,224},{32,0},{64,32},{96,64},{128,96},{160,128},{192,160},{224,1... | collective-permute-start | bytes 589832 | tf_op jit(solution)/shard_map/beams_gather/ppermute | solution.py:154
  68.4 17.5 %collective-permute-start.8 = (f32[96,512]{1,0:T(8,128)S(1)}, f32[96,512]{1,0:T(8,128)S(1)}, u32[]{:S(2)}, u32[]{:S(2)}) collective-permute-start(f32[96,512]{1,0:T(8,128)S(1)} %get-tuple-element.33.refs_0_), channel_id=1, source_target_pairs={{0,64},{32,96},{64,128},{96,160},{128,192},{160,224},{192,0},{224,... | collective-permute-start | bytes 589832 | tf_op jit(solution)/shard_map/beams_gather/ppermute | solution.py:154
  70.2 15.7 %collective-permute-start.7 = (f32[96,512]{1,0:T(8,128)S(1)}, f32[96,512]{1,0:T(8,128)S(1)}, u32[]{:S(2)}, u32[]{:S(2)}) collective-permute-start(f32[96,512]{1,0:T(8,128)S(1)} %get-tuple-element.33.refs_0_), channel_id=1, source_target_pairs={{0,32},{32,64},{64,96},{96,128},{128,160},{160,192},{192,224},{224... | collective-permute-start | bytes 589832 | tf_op jit(solution)/shard_map/beams_gather/ppermute | solution.py:154
  86.4 16.4 %collective-permute-start.11 = (f32[144,512]{1,0:T(8,128)S(1)}, f32[144,512]{1,0:T(8,128)S(1)}, u32[]{:S(2)}, u32[]{:S(2)}) collective-permute-start(f32[144,512]{1,0:T(8,128)S(1)} %get-tuple-element.35), channel_id=1, source_target_pairs={{0,192},{32,224},{64,0},{96,32},{128,64},{160,96},{192,128},{224,1... | collective-permute-start | bytes 884744 | tf_op jit(solution)/shard_map/beams_gather/ppermute | solution.py:154
  88.1 16.4 %collective-permute-start.12 = (f32[144,512]{1,0:T(8,128)S(1)}, f32[144,512]{1,0:T(8,128)S(1)}, u32[]{:S(2)}, u32[]{:S(2)}) collective-permute-start(f32[144,512]{1,0:T(8,128)S(1)} %get-tuple-element.36), channel_id=1, source_target_pairs={{0,64},{32,96},{64,128},{96,160},{128,192},{160,224},{192,0},{224,... | collective-permute-start | bytes 884744 | tf_op jit(solution)/shard_map/beams_gather/ppermute | solution.py:154

commit v8 on v6

--- a/solution.py
+++ b/solution.py
@@ -109,7 +109,8 @@
     taps, _, beams = taps_weight.shape
     share = rows // 8
     tall = share + LEAD
-    shapes = [jax.ShapeDtypeStruct((h, beams), jnp.float32) for h in heights]
+    place = jax.ShapeDtypeStruct if weights else pltpu.HBM
+    shapes = [place((h, beams), jnp.float32) for h in heights]
     if weights:
         shapes.append(jax.ShapeDtypeStruct((share, TILE), jnp.float32))
         shapes.append(jax.ShapeDtypeStruct((1, TILE), jnp.float32))
@@ -149,7 +150,7 @@
 
 
 def relay_sums(keep, down, up, far_down, far_up):
-    shape = jax.ShapeDtypeStruct((keep.shape[0] // 3, keep.shape[1]), jnp.float32)
+    shape = pltpu.HBM((keep.shape[0] // 3, keep.shape[1]), jnp.float32)
     return pl.pallas_call(
         relay_body,
         out_shape=(shape, shape),
@@ -216,7 +217,7 @@
         gram_body,
         out_shape=(
             jax.ShapeDtypeStruct((share, beams), jnp.float32),
-            jax.ShapeDtypeStruct((packed_rows(n), TILE), jnp.float32),
+            pltpu.HBM((packed_rows(n), TILE), jnp.float32),
         ),
         in_specs=[VMEM] * 6,
         out_specs=(VMEM, VMEM),
@@ -317,7 +318,7 @@
     ways, tiles, _ = returned.shape
     return pl.pallas_call(
         replicate_body,
-        out_shape=jax.ShapeDtypeStruct((groups, ways * tiles - ways // 2, TILE), jnp.float32),
+        out_shape=pltpu.HBM((groups, ways * tiles - ways // 2, TILE), jnp.float32),
         in_specs=[VMEM] * 3,
         out_specs=VMEM,
         compiler_params=pltpu.CompilerParams(vmem_limit_bytes=4 << 20),

time: 146 us -> 150 us (1.027)
  Pallas kernels: 21.3 us -> 24.5 us
where the time goes in v8:
time: 150 us
  blocking collectives  70.2 us (47%)
  waiting for transfers between devices  27.1 us (18%)
  Pallas kernels  24.5 us (16%)
  starting transfers between devices  21.6 us (14%)
  local copies, waits for them, and re-layouts  5.99 us (4%)
    ppermute x12, waiting for transfers between devices, ring(): lax.ppermute(array, 'elem', [(i, (i + by) % size) for i in range(size)])  27.1 us
    all_to_all x1, blocking collectives, local(): lax.all_to_all(replicated(returned, groups, low, high), 'elem', 0, 0)  22.4 us
    all_to_all x1, blocking collectives, local(): lax.all_to_all(packed.reshape(groups, packed.shape[0] // groups, TILE), '...  22.1 us
    ppermute x12, starting transfers between devices, ring(): lax.ppermute(array, 'elem', [(i, (i + by) % size) for i in range(size)])  19.7 us
    pallas_call x1, Pallas kernels, whitened_rows(): pl.pallas_call(factor_body, out_shape=jax.ShapeDtypeStruct((n // groups,...  15.8 us
    all_to_all x1, blocking collectives, local(): received = lax.all_to_all(spread, 'tm', 0, 0, tiled=True)  13.8 us
    all_to_all x1, blocking collectives, local(): returned = lax.all_to_all(estimate, 'tm', 0, 0, tiled=True)  12 us
    unnamed x8, local copies, waits for them, and re-layouts  5.29 us
  transfers between devices with their start and end apart: 13, of which 6 were waited for; matrix products, arithmetic and copies ran while one was open for 0% of the time, Pallas kernels for 1%

profile of v8, /device:TPU:2, one launch (start us, length us, event | category | flops | bytes accessed | tf_op | source)
XLA Modules:
  0.0 149.6 jit_solution(15449241881668471527)
XLA Ops:
  0.0 0.7 slice.3
  0.7 1.9 %collective-permute-start = (bf16[16,256]{1,0:T(8,128)(2,1)S(1)}, bf16[16,256]{1,0:T(8,128)(2,1)S(1)}, u32[]{:S(2)}, u32[]{:S(2)}) collective-permute-start(bf16[16,256]{1,0:T(8,128)(2,1)S(1)} %slice.3), channel_id=1, source_target_pairs={{0,1},{1,2},{2,3},{3,4},{4,5},{5,6},{6,7},{7,8},{8,9},{9,10},{10,1... | collective-permute-start | bytes 24584 | tf_op jit(solution)/shard_map/halo/ppermute | solution.py:18
  2.6 0.0 copy-start
  2.6 2.2 %copy-done = bf16[16,256,512]{2,1,0:T(8,128)(2,1)S(1)} copy-done((bf16[16,256,512]{2,1,0:T(8,128)(2,1)S(1)}, bf16[16,256,512]{2,1,0:T(8,128)(2,1)}, u32[]{:S(2)}) %copy-start) | copy-done | bytes 4194328
  4.8 0.0 copy-start.2
  4.8 1.0 copy-done.2
  5.8 0.0 copy-start.1
  5.8 0.1 widened.1.refs_2_
  5.9 0.0 copy-start.3
  5.9 0.0 collective-permute-done.refs_1_
  5.9 2.1 %copy-done.1 = bf16[16,256,512]{2,1,0:T(8,128)(2,1)S(1)} copy-done((bf16[16,256,512]{2,1,0:T(8,128)(2,1)S(1)}, bf16[16,256,512]{2,1,0:T(8,128)(2,1)}, u32[]{:S(2)}) %copy-start.1) | copy-done | bytes 4194328
  8.0 3.2 %fir_sent.1 = (f32[192,512]{1,0:T(8,128)}, f32[192,512]{1,0:T(8,128)}, f32[48,512]{1,0:T(8,128)}, f32[48,512]{1,0:T(8,128)}) custom-call(s32[1]{0:T(128)} %bitcast.refs_0_.group_ref, bf16[16,256]{1,0:T(8,128)(2,1)S(1)} %collective-permute-done.refs_1_, f32[768,256]{1,0:T(8,128)S(1)} %widened.1.refs_2_, bf16[16,256,512]{2,1,0:T(8,128)(2,1)S(1)} %copy-done.1), custom_call_target="tpu_custom_call" | custom-call | flops 2013265920 | bytes 6291456 | tf_op jit(solution)/shard_map/fir_sent/pallas_call | solution.py:117
  11.2 5.9 %collective-permute-start.1 = (f32[192,512]{1,0:T(8,128)}, f32[192,512]{1,0:T(8,128)S(1)}, u32[]{:S(2)}, u32[]{:S(2)}) collective-permute-start(f32[192,512]{1,0:T(8,128)} %get-tuple-element.23), channel_id=1, source_target_pairs={{0,224},{32,0},{64,32},{96,64},{128,96},{160,128},{192,160},{224,1... | collective-permute-start | bytes 1179656 | tf_op jit(solution)/shard_map/beams_near/ppermute | solution.py:138
  17.0 0.0 collective-permute-start.2
  17.0 2.5 %collective-permute-start.3 = (f32[48,512]{1,0:T(8,128)}, f32[48,512]{1,0:T(8,128)S(1)}, u32[]{:S(2)}, u32[]{:S(2)}) collective-permute-start(f32[48,512]{1,0:T(8,128)} %get-tuple-element.25), channel_id=1, source_target_pairs={{0,192},{32,224},{64,0},{96,32},{128,64},{160,96},{192,128},{224,1... | collective-permute-start | bytes 294920 | tf_op jit(solution)/shard_map/beams_near/ppermute | solution.py:138
  19.5 0.5 collective-permute-start.4
  19.9 0.0 copy-done.3
  19.9 1.5 fir_rest.1
  21.4 9.0 %collective-permute-done.3.far_down_ref = f32[48,512]{1,0:T(8,128)S(1)} collective-permute-done((f32[48,512]{1,0:T(8,128)}, f32[48,512]{1,0:T(8,128)S(1)}, u32[]{:S(2)}, u32[]{:S(2)}) %collective-permute-start.3) | collective-permute-done | bytes 98336 | tf_op jit(solution)/shard_map/beams_near/ppermute | solution.py:138
  30.5 1.9 %collective-permute-done.4.far_up_ref = f32[48,512]{1,0:T(8,128)S(1)} collective-permute-done((f32[48,512]{1,0:T(8,128)}, f32[48,512]{1,0:T(8,128)S(1)}, u32[]{:S(2)}, u32[]{:S(2)}) %collective-permute-start.4) | collective-permute-done | bytes 98336 | tf_op jit(solution)/shard_map/beams_near/ppermute | solution.py:138
  32.4 0.0 collective-permute-done.1.down_ref
  32.4 0.0 collective-permute-done.2.up_ref
  32.4 0.8 relay_sums.1
  33.2 2.6 %collective-permute-start.5 = (f32[96,512]{1,0:T(8,128)}, f32[96,512]{1,0:T(8,128)S(1)}, u32[]{:S(2)}, u32[]{:S(2)}) collective-permute-start(f32[96,512]{1,0:T(8,128)} %get-tuple-element.27), channel_id=1, source_target_pairs={{0,192},{32,224},{64,0},{96,32},{128,64},{160,96},{192,128},{224,1... | collective-permute-start | bytes 589832 | tf_op jit(solution)/shard_map/beams_far/ppermute | solution.py:138
  35.8 0.3 collective-permute-start.6
  36.1 8.9 %collective-permute-done.5.low_ref = f32[96,512]{1,0:T(8,128)S(1)} collective-permute-done((f32[96,512]{1,0:T(8,128)}, f32[96,512]{1,0:T(8,128)S(1)}, u32[]{:S(2)}, u32[]{:S(2)}) %collective-permute-start.5) | collective-permute-done | bytes 196640 | tf_op jit(solution)/shard_map/beams_far/ppermute | solution.py:138
  45.0 4.1 %collective-permute-done.6.high_ref = f32[96,512]{1,0:T(8,128)S(1)} collective-permute-done((f32[96,512]{1,0:T(8,128)}, f32[96,512]{1,0:T(8,128)S(1)}, u32[]{:S(2)}, u32[]{:S(2)}) %collective-permute-start.6) | collective-permute-done | bytes 196640 | tf_op jit(solution)/shard_map/beams_far/ppermute | solution.py:138
  49.2 1.7 %packed_gram.1 = (f32[96,512]{1,0:T(8,128)S(1)}, f32[1152,128]{1,0:T(8,128)}) custom-call(f32[288,512]{1,0:T(8,128)S(1)} %get-tuple-element.22.keep_ref, f32[192,512]{1,0:T(8,128)S(1)} %collective-permute-done.1.down_ref, f32[192,512]{1,0:T(8,128)S(1)} %collective-permute-done.2.up_ref, f32[96,512]{1,0:T(8,128)S(1)} %collective-permute-done.5.low_ref, ...), custom_call_target="tpu_custom_call" | custom-call | tf_op jit(solution)/shard_map/packed_gram/pallas_call | solution.py:216
  50.8 22.1 %all_to_all.20.p_ref = f32[8,144,128]{2,1,0:T(8,128)S(1)} all-to-all(f32[8,144,128]{2,1,0:T(8,128)} %bitcast.2), channel_id=1, replica_groups=mesh['elem'=8,'tm'=32] {'elem'}, dimensions={0} | all-to-all | bytes 1179648 | tf_op jit(solution)/shard_map/gram_sum/all_to_all | solution.py:560
  72.9 0.1 spread_share.1
  73.0 0.5 collective-permute-start.10
  73.4 0.7 collective-permute-start.9
  74.2 1.8 %collective-permute-start.8 = (f32[96,512]{1,0:T(8,128)S(1)}, f32[96,512]{1,0:T(8,128)S(1)}, u32[]{:S(2)}, u32[]{:S(2)}) collective-permute-start(f32[96,512]{1,0:T(8,128)S(1)} %get-tuple-element.33.refs_0_), channel_id=1, source_target_pairs={{0,64},{32,96},{64,128},{96,160},{128,192},{160,224},{192,0},{224,... | collective-permute-start | bytes 589832 | tf_op jit(solution)/shard_map/beams_gather/ppermute | solution.py:138
  76.0 2.0 %collective-permute-start.7 = (f32[96,512]{1,0:T(8,128)S(1)}, f32[96,512]{1,0:T(8,128)S(1)}, u32[]{:S(2)}, u32[]{:S(2)}) collective-permute-start(f32[96,512]{1,0:T(8,128)S(1)} %get-tuple-element.33.refs_0_), channel_id=1, source_target_pairs={{0,32},{32,64},{64,96},{96,128},{128,160},{160,192},{192,224},{224... | collective-permute-start | bytes 589832 | tf_op jit(solution)/shard_map/beams_gather/ppermute | solution.py:138
  78.0 13.8 %all_to_all.21.r_ref = f32[32,5,128]{2,1,0:T(8,128)S(1)} all-to-all(f32[32,5,128]{2,1,0:T(8,128)S(1)} %get-tuple-element.32), channel_id=1, replica_groups=mesh['elem'=8,'tm'=32] {'tm'}, dimensions={0} | all-to-all | bytes 163840 | tf_op jit(solution)/shard_map/blocks_out/all_to_all | solution.py:568
  91.8 0.0 collective-permute-done.10.from_above2.refs_4_
  91.8 0.0 collective-permute-done.9.from_above.refs_3_
  91.8 0.0 collective-permute-done.8.from_below2.refs_2_
  91.8 0.0 collective-permute-done.7.from_below.refs_1_
  91.8 0.5 decayed_sums.1
  92.4 1.7 %collective-permute-start.11 = (f32[144,512]{1,0:T(8,128)S(1)}, f32[144,512]{1,0:T(8,128)S(1)}, u32[]{:S(2)}, u32[]{:S(2)}) collective-permute-start(f32[144,512]{1,0:T(8,128)S(1)} %get-tuple-element.35), channel_id=1, source_target_pairs={{0,192},{32,224},{64,0},{96,32},{128,64},{160,96},{192,128},{224,1... | collective-permute-start | bytes 884744 | tf_op jit(solution)/shard_map/beams_gather/ppermute | solution.py:138
  94.1 1.3 collective-permute-start.12
  95.4 12.0 %all_to_all.22.r_ref = f32[32,5,128]{2,1,0:T(8,128)S(1)} all-to-all(f32[32,5,128]{2,1,0:T(8,128)S(1)} %get-tuple-element.34), channel_id=1, replica_groups=mesh['elem'=8,'tm'=32] {'tm'}, dimensions={0} | all-to-all | bytes 163840 | tf_op jit(solution)/shard_map/blocks_back/all_to_all | solution.py:573
  107.4 1.4 collective-permute-done.11.low_ref.refs_5_
  108.8 1.7 %collective-permute-done.12.high_ref.refs_6_ = f32[144,512]{1,0:T(8,128)S(1)} collective-permute-done((f32[144,512]{1,0:T(8,128)S(1)}, f32[144,512]{1,0:T(8,128)S(1)}, u32[]{:S(2)}, u32[]{:S(2)}) %collective-permute-start.12) | collective-permute-done | bytes 294944 | tf_op jit(solution)/shard_map/beams_gather/ppermute | solution.py:138
  110.5 1.0 replicated.1
  111.4 22.4 %all_to_all.23.p_ref = f32[8,144,128]{2,1,0:T(8,128)S(1)} all-to-all(f32[8,144,128]{2,1,0:T(8,128)} %replicated.1), channel_id=1, replica_groups=mesh['elem'=8,'tm'=32] {'elem'}, dimensions={0} | all-to-all | bytes 1179648 | tf_op jit(solution)/shard_map/gram_gather/all_to_all | solution.py:575
  133.9 15.8 %whitened_rows.1 = f32[64,768]{1,0:T(8,128)} custom-call(s32[1]{0:T(128)} %bitcast.refs_0_.group_ref, f32[8,144,128]{2,1,0:T(8,128)S(1)} %all_to_all.23.p_ref, f32[96,512]{1,0:T(8,128)S(1)} %get-tuple-element.33.refs_0_, f32[96,512]{1,0:T(8,128)S(1)} %collective-permute-done.7.from_below.refs_1_, f32[96,512]{1,0:T(8,128)S(1)} %collective-permute-done.8.from_below2.refs_2_, ...), custom_call_target="tpu_custom_call" | custom-call | flops 1610612736 | bytes 1048576 | tf_op jit(solution)/shard_map/whitened_rows/pallas_call | solution.py:522
Async XLA Ops:
  0.7 5.2 %collective-permute-start = (bf16[16,256]{1,0:T(8,128)(2,1)S(1)}, bf16[16,256]{1,0:T(8,128)(2,1)S(1)}, u32[]{:S(2)}, u32[]{:S(2)}) collective-permute-start(bf16[16,256]{1,0:T(8,128)(2,1)S(1)} %slice.3), channel_id=1, source_target_pairs={{0,1},{1,2},{2,3},{3,4},{4,5},{5,6},{6,7},{7,8},{8,9},{9,10},{10,1... | collective-permute-start | bytes 24584 | tf_op jit(solution)/shard_map/halo/ppermute | solution.py:18
  2.6 2.2 %copy-start = (bf16[16,256,512]{2,1,0:T(8,128)(2,1)S(1)}, bf16[16,256,512]{2,1,0:T(8,128)(2,1)}, u32[]{:S(2)}) copy-start(bf16[16,256,512]{2,1,0:T(8,128)(2,1)} %refs_3_.3) | copy-start | bytes 12582916
  4.8 1.0 copy-start.2
  5.8 2.2 %copy-start.1 = (bf16[16,256,512]{2,1,0:T(8,128)(2,1)S(1)}, bf16[16,256,512]{2,1,0:T(8,128)(2,1)}, u32[]{:S(2)}) copy-start(bf16[16,256,512]{2,1,0:T(8,128)(2,1)} %refs_3_.3) | copy-start | bytes 12582916
  5.9 14.1 %copy-start.3 = (f32[768]{0:T(1024)S(1)}, f32[768]{0:T(1024)}, u32[]{:S(2)}) copy-start(f32[768]{0:T(1024)} %refs_4_.1) | copy-start | bytes 9220
  11.2 21.3 %collective-permute-start.1 = (f32[192,512]{1,0:T(8,128)}, f32[192,512]{1,0:T(8,128)S(1)}, u32[]{:S(2)}, u32[]{:S(2)}) collective-permute-start(f32[192,512]{1,0:T(8,128)} %get-tuple-element.23), channel_id=1, source_target_pairs={{0,224},{32,0},{64,32},{96,64},{128,96},{160,128},{192,160},{224,1... | collective-permute-start | bytes 1179656 | tf_op jit(solution)/shard_map/beams_near/ppermute | solution.py:138
  17.0 15.4 %collective-permute-start.2 = (f32[192,512]{1,0:T(8,128)}, f32[192,512]{1,0:T(8,128)S(1)}, u32[]{:S(2)}, u32[]{:S(2)}) collective-permute-start(f32[192,512]{1,0:T(8,128)} %get-tuple-element.24), channel_id=1, source_target_pairs={{0,32},{32,64},{64,96},{96,128},{128,160},{160,192},{192,224},{224... | collective-permute-start | bytes 1179656 | tf_op jit(solution)/shard_map/beams_near/ppermute | solution.py:138
  17.0 13.5 %collective-permute-start.3 = (f32[48,512]{1,0:T(8,128)}, f32[48,512]{1,0:T(8,128)S(1)}, u32[]{:S(2)}, u32[]{:S(2)}) collective-permute-start(f32[48,512]{1,0:T(8,128)} %get-tuple-element.25), channel_id=1, source_target_pairs={{0,192},{32,224},{64,0},{96,32},{128,64},{160,96},{192,128},{224,1... | collective-permute-start | bytes 294920 | tf_op jit(solution)/shard_map/beams_near/ppermute | solution.py:138
  19.5 12.9 %collective-permute-start.4 = (f32[48,512]{1,0:T(8,128)}, f32[48,512]{1,0:T(8,128)S(1)}, u32[]{:S(2)}, u32[]{:S(2)}) collective-permute-start(f32[48,512]{1,0:T(8,128)} %get-tuple-element.26), channel_id=1, source_target_pairs={{0,64},{32,96},{64,128},{96,160},{128,192},{160,224},{192,0},{224,... | collective-permute-start | bytes 294920 | tf_op jit(solution)/shard_map/beams_near/ppermute | solution.py:138
  33.2 11.8 %collective-permute-start.5 = (f32[96,512]{1,0:T(8,128)}, f32[96,512]{1,0:T(8,128)S(1)}, u32[]{:S(2)}, u32[]{:S(2)}) collective-permute-start(f32[96,512]{1,0:T(8,128)} %get-tuple-element.27), channel_id=1, source_target_pairs={{0,192},{32,224},{64,0},{96,32},{128,64},{160,96},{192,128},{224,1... | collective-permute-start | bytes 589832 | tf_op jit(solution)/shard_map/beams_far/ppermute | solution.py:138
  35.8 13.4 %collective-permute-start.6 = (f32[96,512]{1,0:T(8,128)}, f32[96,512]{1,0:T(8,128)S(1)}, u32[]{:S(2)}, u32[]{:S(2)}) collective-permute-start(f32[96,512]{1,0:T(8,128)} %get-tuple-element.28), channel_id=1, source_target_pairs={{0,64},{32,96},{64,128},{96,160},{128,192},{160,224},{192,0},{224,... | collective-permute-start | bytes 589832 | tf_op jit(solution)/shard_map/beams_far/ppermute | solution.py:138
  73.0 18.8 %collective-permute-start.10 = (f32[96,512]{1,0:T(8,128)S(1)}, f32[96,512]{1,0:T(8,128)S(1)}, u32[]{:S(2)}, u32[]{:S(2)}) collective-permute-start(f32[96,512]{1,0:T(8,128)S(1)} %get-tuple-element.33.refs_0_), channel_id=1, source_target_pairs={{0,192},{32,224},{64,0},{96,32},{128,64},{160,96},{192,128},{224,1... | collective-permute-start | bytes 589832 | tf_op jit(solution)/shard_map/beams_gather/ppermute | solution.py:138
  73.4 18.4 %collective-permute-start.9 = (f32[96,512]{1,0:T(8,128)S(1)}, f32[96,512]{1,0:T(8,128)S(1)}, u32[]{:S(2)}, u32[]{:S(2)}) collective-permute-start(f32[96,512]{1,0:T(8,128)S(1)} %get-tuple-element.33.refs_0_), channel_id=1, source_target_pairs={{0,224},{32,0},{64,32},{96,64},{128,96},{160,128},{192,160},{224,1... | collective-permute-start | bytes 589832 | tf_op jit(solution)/shard_map/beams_gather/ppermute | solution.py:138
  74.2 17.6 %collective-permute-start.8 = (f32[96,512]{1,0:T(8,128)S(1)}, f32[96,512]{1,0:T(8,128)S(1)}, u32[]{:S(2)}, u32[]{:S(2)}) collective-permute-start(f32[96,512]{1,0:T(8,128)S(1)} %get-tuple-element.33.refs_0_), channel_id=1, source_target_pairs={{0,64},{32,96},{64,128},{96,160},{128,192},{160,224},{192,0},{224,... | collective-permute-start | bytes 589832 | tf_op jit(solution)/shard_map/beams_gather/ppermute | solution.py:138
  76.0 15.8 %collective-permute-start.7 = (f32[96,512]{1,0:T(8,128)S(1)}, f32[96,512]{1,0:T(8,128)S(1)}, u32[]{:S(2)}, u32[]{:S(2)}) collective-permute-start(f32[96,512]{1,0:T(8,128)S(1)} %get-tuple-element.33.refs_0_), channel_id=1, source_target_pairs={{0,32},{32,64},{64,96},{96,128},{128,160},{160,192},{192,224},{224... | collective-permute-start | bytes 589832 | tf_op jit(solution)/shard_map/beams_gather/ppermute | solution.py:138
  92.4 16.4 %collective-permute-start.11 = (f32[144,512]{1,0:T(8,128)S(1)}, f32[144,512]{1,0:T(8,128)S(1)}, u32[]{:S(2)}, u32[]{:S(2)}) collective-permute-start(f32[144,512]{1,0:T(8,128)S(1)} %get-tuple-element.35), channel_id=1, source_target_pairs={{0,192},{32,224},{64,0},{96,32},{128,64},{160,96},{192,128},{224,1... | collective-permute-start | bytes 884744 | tf_op jit(solution)/shard_map/beams_gather/ppermute | solution.py:138
  94.1 16.4 %collective-permute-start.12 = (f32[144,512]{1,0:T(8,128)S(1)}, f32[144,512]{1,0:T(8,128)S(1)}, u32[]{:S(2)}, u32[]{:S(2)}) collective-permute-start(f32[144,512]{1,0:T(8,128)S(1)} %get-tuple-element.36), channel_id=1, source_target_pairs={{0,64},{32,96},{64,128},{96,160},{128,192},{160,224},{192,0},{224,... | collective-permute-start | bytes 884744 | tf_op jit(solution)/shard_map/beams_gather/ppermute | solution.py:138

commit v9 on v7

--- a/solution.py
+++ b/solution.py
@@ -19,7 +19,7 @@
 
 
 LEAD = 16
-SPLIT = 4
+SPLIT = 2
 
 
 def fir_body(offsets, weights, group_ref, halo_ref, x_hbm, w_hbm, *refs):
@@ -117,7 +117,8 @@
     taps, _, beams = taps_weight.shape
     share = rows // 8
     tall = share + LEAD
-    shapes = [jax.ShapeDtypeStruct((h, beams), jnp.float32) for h in heights]
+    place = jax.ShapeDtypeStruct if weights else pltpu.HBM
+    shapes = [place((h, beams), jnp.float32) for h in heights]
     if weights:
         shapes.append(jax.ShapeDtypeStruct((share, TILE), jnp.float32))
         shapes.append(jax.ShapeDtypeStruct((1, TILE), jnp.float32))
@@ -133,13 +134,17 @@
             pltpu.SemaphoreType.DMA,
             pltpu.SemaphoreType.DMA((SPLIT,)),
         ]
+    if not weights:
+        samples, taps_weight = (
+            pltpu.with_memory_space_constraint(a, pltpu.HBM) for a in (samples, taps_weight)
+        )
     return pl.pallas_call(
         lambda *refs: fir_body(offsets, weights, *refs),
         out_shape=shapes,
         in_specs=[SMEM, VMEM, large, large] + [VMEM] * weights,
         out_specs=[VMEM] * len(shapes),
         scratch_shapes=scratch,
-        compiler_params=pltpu.CompilerParams(vmem_limit_bytes=(16 if weights else 60) << 20),
+        compiler_params=pltpu.CompilerParams(vmem_limit_bytes=(16 if weights else 40) << 20),
         cost_estimate=pl.CostEstimate(
             flops=2 * share * len(offsets) * taps * width * beams,
             bytes_accessed=6 << 20,

time: 143 us -> 142 us (level)
  waiting for transfers between devices: 23.3 us -> 28.1 us
  local copies, waits for them, and re-layouts: 4.25 us -> 0.78 us
    ppermute x12, waiting for transfers between devices: 20.3 us -> 25 us  [ring(): lax.ppermute(array, 'elem', [(i, (i + by) % size) for i in range(size)])]
    unnamed x10 -> x6, local copies, waits for them, and re-layouts: 3.48 us -> 0.01 us
where the time goes in v9:
time: 142 us; the launch traced here: 141 us
  blocking collectives  66.8 us (47%)
  waiting for transfers between devices  28.1 us (20%)
  Pallas kernels  23.8 us (17%)
  starting transfers between devices  21.8 us (15%)
    ppermute x12, waiting for transfers between devices, ring(): lax.ppermute(array, 'elem', [(i, (i + by) % size) for i in range(size)])  25 us
    all_to_all x1, blocking collectives, local(): lax.all_to_all(replicated(returned, groups, low, high), 'elem', 0, 0)  22.2 us
    ppermute x12, starting transfers between devices, ring(): lax.ppermute(array, 'elem', [(i, (i + by) % size) for i in range(size)])  19.9 us
    all_to_all x1, blocking collectives, local(): lax.all_to_all(packed.reshape(groups, packed.shape[0] // groups, TILE), '...  19.7 us
    pallas_call x1, Pallas kernels, whitened_rows(): pl.pallas_call(factor_body, out_shape=jax.ShapeDtypeStruct((n // groups,...  15.8 us
    all_to_all x1, blocking collectives, local(): received = lax.all_to_all(spread, 'tm', 0, 0, tiled=True)  13.6 us
    all_to_all x1, blocking collectives, local(): returned = lax.all_to_all(estimate, 'tm', 0, 0, tiled=True)  11.3 us
    pallas_call x2, Pallas kernels, fir(): pl.pallas_call(lambda *refs: fir_body(offsets, weights, *refs), out_shape...  6.33 us
  transfers between devices with their start and end apart: 13, of which 8 were waited for; matrix products, arithmetic and copies ran while one was open for 0% of the time, Pallas kernels for 1%

profile of v9, /device:TPU:2, one launch (start us, length us, event | category | flops | bytes accessed | tf_op | source)
XLA Modules:
  0.0 141.3 jit_solution(14761974282628954287)
XLA Ops:
  0.0 0.0 copy-start.1
  0.0 0.0 copy-start.2
  0.0 0.8 slice.3
  0.8 1.9 %collective-permute-start = (bf16[16,256]{1,0:T(8,128)(2,1)S(1)}, bf16[16,256]{1,0:T(8,128)(2,1)S(1)}, u32[]{:S(2)}, u32[]{:S(2)}) collective-permute-start(bf16[16,256]{1,0:T(8,128)(2,1)S(1)} %slice.3), channel_id=1, source_target_pairs={{0,1},{1,2},{2,3},{3,4},{4,5},{5,6},{6,7},{7,8},{8,9},{9,10},{10,1... | collective-permute-start | bytes 24584 | tf_op jit(solution)/shard_map/halo/ppermute | solution.py:18
  2.7 0.0 copy-start
  2.7 3.0 %collective-permute-done.refs_1_ = bf16[16,256]{1,0:T(8,128)(2,1)S(1)} collective-permute-done((bf16[16,256]{1,0:T(8,128)(2,1)S(1)}, bf16[16,256]{1,0:T(8,128)(2,1)S(1)}, u32[]{:S(2)}, u32[]{:S(2)}) %collective-permute-start) | collective-permute-done | bytes 8224 | tf_op jit(solution)/shard_map/halo/ppermute | solution.py:18
  5.7 4.9 %fir_sent.1 = (f32[192,512]{1,0:T(8,128)}, f32[192,512]{1,0:T(8,128)}, f32[48,512]{1,0:T(8,128)}, f32[48,512]{1,0:T(8,128)}) custom-call(s32[1]{0:T(128)} %bitcast.refs_0_.group_ref, bf16[16,256]{1,0:T(8,128)(2,1)S(1)} %collective-permute-done.refs_1_, bf16[768,256]{1,0:T(8,128)(2,1)} %refs_2_.3, bf16[16,256,512]{2,1,0:T(8,128)(2,1)} %refs_3_.3), custom_call_target="tpu_custom_call" | custom-call | flops 2013265920 | bytes 6291456 | tf_op jit(solution)/shard_map/fir_sent/pallas_call | solution.py:141
  10.6 5.9 %collective-permute-start.1 = (f32[192,512]{1,0:T(8,128)}, f32[192,512]{1,0:T(8,128)S(1)}, u32[]{:S(2)}, u32[]{:S(2)}) collective-permute-start(f32[192,512]{1,0:T(8,128)} %get-tuple-element.23), channel_id=1, source_target_pairs={{0,224},{32,0},{64,32},{96,64},{128,96},{160,128},{192,160},{224,1... | collective-permute-start | bytes 1179656 | tf_op jit(solution)/shard_map/beams_near/ppermute | solution.py:159
  16.5 0.0 collective-permute-start.2
  16.5 2.5 %collective-permute-start.3 = (f32[48,512]{1,0:T(8,128)}, f32[48,512]{1,0:T(8,128)S(1)}, u32[]{:S(2)}, u32[]{:S(2)}) collective-permute-start(f32[48,512]{1,0:T(8,128)} %get-tuple-element.25), channel_id=1, source_target_pairs={{0,192},{32,224},{64,0},{96,32},{128,64},{160,96},{192,128},{224,1... | collective-permute-start | bytes 294920 | tf_op jit(solution)/shard_map/beams_near/ppermute | solution.py:159
  19.0 0.5 collective-permute-start.4
  19.4 0.0 copy-done.1
  19.4 0.0 copy-done.2
  19.5 0.0 copy-done
  19.5 1.5 %fir_rest.1 = (f32[288,512]{1,0:T(8,128)S(1)}, f32[96,128]{1,0:T(8,128)S(1)}, f32[1,128]{1,0:T(1,128)S(1)}) custom-call(s32[1]{0:T(128)} %bitcast.refs_0_.group_ref, bf16[16,256]{1,0:T(8,128)(2,1)S(1)} %collective-permute-done.refs_1_, bf16[768,256]{1,0:T(8,128)(2,1)S(1)} %copy-done.1, bf16[16,256,512]{2,1,0:T(8,128)(2,1)S(1)} %copy-done, f32[768]{0:T(1024)S(1)} %copy-done.2), custom_call_target="tpu_custom_call" | custom-call | flops 1207959552 | bytes 6291456 | tf_op jit(solution)/shard_map/fir_rest/pallas_call | solution.py:141
  20.9 8.3 %collective-permute-done.3.far_down_ref = f32[48,512]{1,0:T(8,128)S(1)} collective-permute-done((f32[48,512]{1,0:T(8,128)}, f32[48,512]{1,0:T(8,128)S(1)}, u32[]{:S(2)}, u32[]{:S(2)}) %collective-permute-start.3) | collective-permute-done | bytes 98336 | tf_op jit(solution)/shard_map/beams_near/ppermute | solution.py:159
  29.3 1.8 %collective-permute-done.4.far_up_ref = f32[48,512]{1,0:T(8,128)S(1)} collective-permute-done((f32[48,512]{1,0:T(8,128)}, f32[48,512]{1,0:T(8,128)S(1)}, u32[]{:S(2)}, u32[]{:S(2)}) %collective-permute-start.4) | collective-permute-done | bytes 98336 | tf_op jit(solution)/shard_map/beams_near/ppermute | solution.py:159
  31.1 0.0 collective-permute-done.1.down_ref
  31.1 0.5 collective-permute-done.2.up_ref
  31.5 0.1 relay_sums.1
  31.6 2.3 %collective-permute-start.5 = (f32[96,512]{1,0:T(8,128)S(1)}, f32[96,512]{1,0:T(8,128)S(1)}, u32[]{:S(2)}, u32[]{:S(2)}) collective-permute-start(f32[96,512]{1,0:T(8,128)S(1)} %get-tuple-element.27), channel_id=1, source_target_pairs={{0,192},{32,224},{64,0},{96,32},{128,64},{160,96},{192,128},{224,1... | collective-permute-start | bytes 589832 | tf_op jit(solution)/shard_map/beams_far/ppermute | solution.py:159
  33.9 0.7 collective-permute-start.6
  34.6 6.9 %collective-permute-done.5.low_ref = f32[96,512]{1,0:T(8,128)S(1)} collective-permute-done((f32[96,512]{1,0:T(8,128)S(1)}, f32[96,512]{1,0:T(8,128)S(1)}, u32[]{:S(2)}, u32[]{:S(2)}) %collective-permute-start.5) | collective-permute-done | bytes 196640 | tf_op jit(solution)/shard_map/beams_far/ppermute | solution.py:159
  41.4 3.8 %collective-permute-done.6.high_ref = f32[96,512]{1,0:T(8,128)S(1)} collective-permute-done((f32[96,512]{1,0:T(8,128)S(1)}, f32[96,512]{1,0:T(8,128)S(1)}, u32[]{:S(2)}, u32[]{:S(2)}) %collective-permute-start.6) | collective-permute-done | bytes 196640 | tf_op jit(solution)/shard_map/beams_far/ppermute | solution.py:159
  45.2 0.8 packed_gram.1
  46.0 19.7 %all_to_all.20.p_ref = f32[8,144,128]{2,1,0:T(8,128)S(1)} all-to-all(f32[8,144,128]{2,1,0:T(8,128)S(1)} %bitcast.2), channel_id=1, replica_groups=mesh['elem'=8,'tm'=32] {'elem'}, dimensions={0} | all-to-all | bytes 1179648 | tf_op jit(solution)/shard_map/gram_sum/all_to_all | solution.py:581
  65.7 0.1 spread_share.1
  65.8 0.5 collective-permute-start.10
  66.3 0.7 collective-permute-start.9
  67.0 1.8 %collective-permute-start.8 = (f32[96,512]{1,0:T(8,128)S(1)}, f32[96,512]{1,0:T(8,128)S(1)}, u32[]{:S(2)}, u32[]{:S(2)}) collective-permute-start(f32[96,512]{1,0:T(8,128)S(1)} %get-tuple-element.33.refs_0_), channel_id=1, source_target_pairs={{0,64},{32,96},{64,128},{96,160},{128,192},{160,224},{192,0},{224,... | collective-permute-start | bytes 589832 | tf_op jit(solution)/shard_map/beams_gather/ppermute | solution.py:159
  68.8 2.0 %collective-permute-start.7 = (f32[96,512]{1,0:T(8,128)S(1)}, f32[96,512]{1,0:T(8,128)S(1)}, u32[]{:S(2)}, u32[]{:S(2)}) collective-permute-start(f32[96,512]{1,0:T(8,128)S(1)} %get-tuple-element.33.refs_0_), channel_id=1, source_target_pairs={{0,32},{32,64},{64,96},{96,128},{128,160},{160,192},{192,224},{224... | collective-permute-start | bytes 589832 | tf_op jit(solution)/shard_map/beams_gather/ppermute | solution.py:159
  70.9 13.6 %all_to_all.21.r_ref = f32[32,5,128]{2,1,0:T(8,128)S(1)} all-to-all(f32[32,5,128]{2,1,0:T(8,128)S(1)} %get-tuple-element.32), channel_id=1, replica_groups=mesh['elem'=8,'tm'=32] {'tm'}, dimensions={0} | all-to-all | bytes 163840 | tf_op jit(solution)/shard_map/blocks_out/all_to_all | solution.py:589
  84.5 0.0 collective-permute-done.10.from_above2.refs_4_
  84.5 0.0 collective-permute-done.9.from_above.refs_3_
  84.5 0.0 collective-permute-done.8.from_below2.refs_2_
  84.5 0.0 collective-permute-done.7.from_below.refs_1_
  84.5 0.6 decayed_sums.1
  85.1 1.7 %collective-permute-start.11 = (f32[144,512]{1,0:T(8,128)S(1)}, f32[144,512]{1,0:T(8,128)S(1)}, u32[]{:S(2)}, u32[]{:S(2)}) collective-permute-start(f32[144,512]{1,0:T(8,128)S(1)} %get-tuple-element.35), channel_id=1, source_target_pairs={{0,192},{32,224},{64,0},{96,32},{128,64},{160,96},{192,128},{224,1... | collective-permute-start | bytes 884744 | tf_op jit(solution)/shard_map/beams_gather/ppermute | solution.py:159
  86.7 1.3 collective-permute-start.12
  88.1 11.3 %all_to_all.22.r_ref = f32[32,5,128]{2,1,0:T(8,128)S(1)} all-to-all(f32[32,5,128]{2,1,0:T(8,128)S(1)} %get-tuple-element.34), channel_id=1, replica_groups=mesh['elem'=8,'tm'=32] {'tm'}, dimensions={0} | all-to-all | bytes 163840 | tf_op jit(solution)/shard_map/blocks_back/all_to_all | solution.py:594
  99.3 2.1 %collective-permute-done.11.low_ref.refs_5_ = f32[144,512]{1,0:T(8,128)S(1)} collective-permute-done((f32[144,512]{1,0:T(8,128)S(1)}, f32[144,512]{1,0:T(8,128)S(1)}, u32[]{:S(2)}, u32[]{:S(2)}) %collective-permute-start.11) | collective-permute-done | bytes 294944 | tf_op jit(solution)/shard_map/beams_gather/ppermute | solution.py:159
  101.5 1.7 %collective-permute-done.12.high_ref.refs_6_ = f32[144,512]{1,0:T(8,128)S(1)} collective-permute-done((f32[144,512]{1,0:T(8,128)S(1)}, f32[144,512]{1,0:T(8,128)S(1)}, u32[]{:S(2)}, u32[]{:S(2)}) %collective-permute-start.12) | collective-permute-done | bytes 294944 | tf_op jit(solution)/shard_map/beams_gather/ppermute | solution.py:159
  103.1 0.2 replicated.1
  103.3 22.2 %all_to_all.23.p_ref = f32[8,144,128]{2,1,0:T(8,128)S(1)} all-to-all(f32[8,144,128]{2,1,0:T(8,128)S(1)} %replicated.1), channel_id=1, replica_groups=mesh['elem'=8,'tm'=32] {'elem'}, dimensions={0} | all-to-all | bytes 1179648 | tf_op jit(solution)/shard_map/gram_gather/all_to_all | solution.py:596
  125.5 15.8 %whitened_rows.1 = f32[64,768]{1,0:T(8,128)} custom-call(s32[1]{0:T(128)} %bitcast.refs_0_.group_ref, f32[8,144,128]{2,1,0:T(8,128)S(1)} %all_to_all.23.p_ref, f32[96,512]{1,0:T(8,128)S(1)} %get-tuple-element.33.refs_0_, f32[96,512]{1,0:T(8,128)S(1)} %collective-permute-done.7.from_below.refs_1_, f32[96,512]{1,0:T(8,128)S(1)} %collective-permute-done.8.from_below2.refs_2_, ...), custom_call_target="tpu_custom_call" | custom-call | flops 1610612736 | bytes 1048576 | tf_op jit(solution)/shard_map/whitened_rows/pallas_call | solution.py:543
Async XLA Ops:
  0.0 19.4 %copy-start.1 = (bf16[768,256]{1,0:T(8,128)(2,1)S(1)}, bf16[768,256]{1,0:T(8,128)(2,1)}, u32[]{:S(2)}) copy-start(bf16[768,256]{1,0:T(8,128)(2,1)} %refs_2_.3) | copy-start | bytes 1179652
  0.0 19.4 %copy-start.2 = (f32[768]{0:T(1024)S(1)}, f32[768]{0:T(1024)}, u32[]{:S(2)}) copy-start(f32[768]{0:T(1024)} %refs_4_.1) | copy-start | bytes 9220
  0.8 5.0 %collective-permute-start = (bf16[16,256]{1,0:T(8,128)(2,1)S(1)}, bf16[16,256]{1,0:T(8,128)(2,1)S(1)}, u32[]{:S(2)}, u32[]{:S(2)}) collective-permute-start(bf16[16,256]{1,0:T(8,128)(2,1)S(1)} %slice.3), channel_id=1, source_target_pairs={{0,1},{1,2},{2,3},{3,4},{4,5},{5,6},{6,7},{7,8},{8,9},{9,10},{10,1... | collective-permute-start | bytes 24584 | tf_op jit(solution)/shard_map/halo/ppermute | solution.py:18
  2.7 16.8 %copy-start = (bf16[16,256,512]{2,1,0:T(8,128)(2,1)S(1)}, bf16[16,256,512]{2,1,0:T(8,128)(2,1)}, u32[]{:S(2)}) copy-start(bf16[16,256,512]{2,1,0:T(8,128)(2,1)} %refs_3_.3) | copy-start | bytes 12582916
  10.6 20.5 %collective-permute-start.1 = (f32[192,512]{1,0:T(8,128)}, f32[192,512]{1,0:T(8,128)S(1)}, u32[]{:S(2)}, u32[]{:S(2)}) collective-permute-start(f32[192,512]{1,0:T(8,128)} %get-tuple-element.23), channel_id=1, source_target_pairs={{0,224},{32,0},{64,32},{96,64},{128,96},{160,128},{192,160},{224,1... | collective-permute-start | bytes 1179656 | tf_op jit(solution)/shard_map/beams_near/ppermute | solution.py:159
  16.5 15.0 %collective-permute-start.2 = (f32[192,512]{1,0:T(8,128)}, f32[192,512]{1,0:T(8,128)S(1)}, u32[]{:S(2)}, u32[]{:S(2)}) collective-permute-start(f32[192,512]{1,0:T(8,128)} %get-tuple-element.24), channel_id=1, source_target_pairs={{0,32},{32,64},{64,96},{96,128},{128,160},{160,192},{192,224},{224... | collective-permute-start | bytes 1179656 | tf_op jit(solution)/shard_map/beams_near/ppermute | solution.py:159
  16.5 12.8 %collective-permute-start.3 = (f32[48,512]{1,0:T(8,128)}, f32[48,512]{1,0:T(8,128)S(1)}, u32[]{:S(2)}, u32[]{:S(2)}) collective-permute-start(f32[48,512]{1,0:T(8,128)} %get-tuple-element.25), channel_id=1, source_target_pairs={{0,192},{32,224},{64,0},{96,32},{128,64},{160,96},{192,128},{224,1... | collective-permute-start | bytes 294920 | tf_op jit(solution)/shard_map/beams_near/ppermute | solution.py:159
  19.0 12.1 %collective-permute-start.4 = (f32[48,512]{1,0:T(8,128)}, f32[48,512]{1,0:T(8,128)S(1)}, u32[]{:S(2)}, u32[]{:S(2)}) collective-permute-start(f32[48,512]{1,0:T(8,128)} %get-tuple-element.26), channel_id=1, source_target_pairs={{0,64},{32,96},{64,128},{96,160},{128,192},{160,224},{192,0},{224,... | collective-permute-start | bytes 294920 | tf_op jit(solution)/shard_map/beams_near/ppermute | solution.py:159
  31.6 9.9 %collective-permute-start.5 = (f32[96,512]{1,0:T(8,128)S(1)}, f32[96,512]{1,0:T(8,128)S(1)}, u32[]{:S(2)}, u32[]{:S(2)}) collective-permute-start(f32[96,512]{1,0:T(8,128)S(1)} %get-tuple-element.27), channel_id=1, source_target_pairs={{0,192},{32,224},{64,0},{96,32},{128,64},{160,96},{192,128},{224,1... | collective-permute-start | bytes 589832 | tf_op jit(solution)/shard_map/beams_far/ppermute | solution.py:159
  33.9 11.3 %collective-permute-start.6 = (f32[96,512]{1,0:T(8,128)S(1)}, f32[96,512]{1,0:T(8,128)S(1)}, u32[]{:S(2)}, u32[]{:S(2)}) collective-permute-start(f32[96,512]{1,0:T(8,128)S(1)} %get-tuple-element.28), channel_id=1, source_target_pairs={{0,64},{32,96},{64,128},{96,160},{128,192},{160,224},{192,0},{224,... | collective-permute-start | bytes 589832 | tf_op jit(solution)/shard_map/beams_far/ppermute | solution.py:159
  65.8 18.6 %collective-permute-start.10 = (f32[96,512]{1,0:T(8,128)S(1)}, f32[96,512]{1,0:T(8,128)S(1)}, u32[]{:S(2)}, u32[]{:S(2)}) collective-permute-start(f32[96,512]{1,0:T(8,128)S(1)} %get-tuple-element.33.refs_0_), channel_id=1, source_target_pairs={{0,192},{32,224},{64,0},{96,32},{128,64},{160,96},{192,128},{224,1... | collective-permute-start | bytes 589832 | tf_op jit(solution)/shard_map/beams_gather/ppermute | solution.py:159
  66.3 18.2 %collective-permute-start.9 = (f32[96,512]{1,0:T(8,128)S(1)}, f32[96,512]{1,0:T(8,128)S(1)}, u32[]{:S(2)}, u32[]{:S(2)}) collective-permute-start(f32[96,512]{1,0:T(8,128)S(1)} %get-tuple-element.33.refs_0_), channel_id=1, source_target_pairs={{0,224},{32,0},{64,32},{96,64},{128,96},{160,128},{192,160},{224,1... | collective-permute-start | bytes 589832 | tf_op jit(solution)/shard_map/beams_gather/ppermute | solution.py:159
  67.0 17.4 %collective-permute-start.8 = (f32[96,512]{1,0:T(8,128)S(1)}, f32[96,512]{1,0:T(8,128)S(1)}, u32[]{:S(2)}, u32[]{:S(2)}) collective-permute-start(f32[96,512]{1,0:T(8,128)S(1)} %get-tuple-element.33.refs_0_), channel_id=1, source_target_pairs={{0,64},{32,96},{64,128},{96,160},{128,192},{160,224},{192,0},{224,... | collective-permute-start | bytes 589832 | tf_op jit(solution)/shard_map/beams_gather/ppermute | solution.py:159
  68.8 15.6 %collective-permute-start.7 = (f32[96,512]{1,0:T(8,128)S(1)}, f32[96,512]{1,0:T(8,128)S(1)}, u32[]{:S(2)}, u32[]{:S(2)}) collective-permute-start(f32[96,512]{1,0:T(8,128)S(1)} %get-tuple-element.33.refs_0_), channel_id=1, source_target_pairs={{0,32},{32,64},{64,96},{96,128},{128,160},{160,192},{192,224},{224... | collective-permute-start | bytes 589832 | tf_op jit(solution)/shard_map/beams_gather/ppermute | solution.py:159
  85.1 16.4 %collective-permute-start.11 = (f32[144,512]{1,0:T(8,128)S(1)}, f32[144,512]{1,0:T(8,128)S(1)}, u32[]{:S(2)}, u32[]{:S(2)}) collective-permute-start(f32[144,512]{1,0:T(8,128)S(1)} %get-tuple-element.35), channel_id=1, source_target_pairs={{0,192},{32,224},{64,0},{96,32},{128,64},{160,96},{192,128},{224,1... | collective-permute-start | bytes 884744 | tf_op jit(solution)/shard_map/beams_gather/ppermute | solution.py:159
  86.7 16.4 %collective-permute-start.12 = (f32[144,512]{1,0:T(8,128)S(1)}, f32[144,512]{1,0:T(8,128)S(1)}, u32[]{:S(2)}, u32[]{:S(2)}) collective-permute-start(f32[144,512]{1,0:T(8,128)S(1)} %get-tuple-element.36), channel_id=1, source_target_pairs={{0,64},{32,96},{64,128},{96,160},{128,192},{160,224},{192,0},{224,... | collective-permute-start | bytes 884744 | tf_op jit(solution)/shard_map/beams_gather/ppermute | solution.py:159

commit v10 on v9

--- a/solution.py
+++ b/solution.py
@@ -117,8 +117,7 @@
     taps, _, beams = taps_weight.shape
     share = rows // 8
     tall = share + LEAD
-    place = jax.ShapeDtypeStruct if weights else pltpu.HBM
-    shapes = [place((h, beams), jnp.float32) for h in heights]
+    shapes = [jax.ShapeDtypeStruct((h, beams), jnp.float32) for h in heights]
     if weights:
         shapes.append(jax.ShapeDtypeStruct((share, TILE), jnp.float32))
         shapes.append(jax.ShapeDtypeStruct((1, TILE), jnp.float32))

time: 142 us -> 141 us (level)
  no operation moved by 1% of the time
where the time goes in v10:
time: 141 us; the launch traced here: 140 us
  blocking collectives  66.8 us (47%)
  waiting for transfers between devices  27.8 us (20%)
  Pallas kernels  22.9 us (16%)
  starting transfers between devices  21.8 us (15%)
    ppermute x12, waiting for transfers between devices, ring(): lax.ppermute(array, 'elem', [(i, (i + by) % size) for i in range(size)])  24.8 us
    all_to_all x1, blocking collectives, local(): lax.all_to_all(replicated(returned, groups, low, high), 'elem', 0, 0)  22.2 us
    ppermute x12, starting transfers between devices, ring(): lax.ppermute(array, 'elem', [(i, (i + by) % size) for i in range(size)])  19.9 us
    all_to_all x1, blocking collectives, local(): lax.all_to_all(packed.reshape(groups, packed.shape[0] // groups, TILE), '...  19.7 us
    pallas_call x1, Pallas kernels, whitened_rows(): pl.pallas_call(factor_body, out_shape=jax.ShapeDtypeStruct((n // groups,...  15.8 us
    all_to_all x1, blocking collectives, local(): received = lax.all_to_all(spread, 'tm', 0, 0, tiled=True)  13.6 us
    all_to_all x1, blocking collectives, local(): returned = lax.all_to_all(estimate, 'tm', 0, 0, tiled=True)  11.3 us
    pallas_call x2, Pallas kernels, fir(): pl.pallas_call(lambda *refs: fir_body(offsets, weights, *refs), out_shape...  5.47 us
  transfers between devices with their start and end apart: 13, of which 8 were waited for; matrix products, arithmetic and copies ran while one was open for 0% of the time, Pallas kernels for 1%

profile of v10, /device:TPU:2, one launch (start us, length us, event | category | flops | bytes accessed | tf_op | source)
XLA Modules:
  0.0 140.3 jit_solution(11310116977405072510)
XLA Ops:
  0.0 0.0 copy-start.1
  0.0 0.0 copy-start.2
  0.0 0.8 slice.3
  0.8 1.9 %collective-permute-start = (bf16[16,256]{1,0:T(8,128)(2,1)S(1)}, bf16[16,256]{1,0:T(8,128)(2,1)S(1)}, u32[]{:S(2)}, u32[]{:S(2)}) collective-permute-start(bf16[16,256]{1,0:T(8,128)(2,1)S(1)} %slice.3), channel_id=1, source_target_pairs={{0,1},{1,2},{2,3},{3,4},{4,5},{5,6},{6,7},{7,8},{8,9},{9,10},{10,1... | collective-permute-start | bytes 24584 | tf_op jit(solution)/shard_map/halo/ppermute | solution.py:18
  2.7 0.0 copy-start
  2.7 3.0 %collective-permute-done.refs_1_ = bf16[16,256]{1,0:T(8,128)(2,1)S(1)} collective-permute-done((bf16[16,256]{1,0:T(8,128)(2,1)S(1)}, bf16[16,256]{1,0:T(8,128)(2,1)S(1)}, u32[]{:S(2)}, u32[]{:S(2)}) %collective-permute-start) | collective-permute-done | bytes 8224 | tf_op jit(solution)/shard_map/halo/ppermute | solution.py:18
  5.7 4.0 %fir_sent.1 = (f32[192,512]{1,0:T(8,128)S(1)}, f32[192,512]{1,0:T(8,128)S(1)}, f32[48,512]{1,0:T(8,128)S(1)}, f32[48,512]{1,0:T(8,128)S(1)}) custom-call(s32[1]{0:T(128)} %bitcast.refs_0_.group_ref, bf16[16,256]{1,0:T(8,128)(2,1)S(1)} %collective-permute-done.refs_1_, bf16[768,256]{1,0:T(8,128)(2,1)} %refs_2_.3, bf16[16,256,512]{2,1,0:T(8,128)(2,1)} %refs_3_.3), custom_call_target="tpu_custom_call" | custom-call | flops 2013265920 | bytes 6291456 | tf_op jit(solution)/shard_map/fir_sent/pallas_call | solution.py:140
  9.7 5.9 %collective-permute-start.1 = (f32[192,512]{1,0:T(8,128)S(1)}, f32[192,512]{1,0:T(8,128)S(1)}, u32[]{:S(2)}, u32[]{:S(2)}) collective-permute-start(f32[192,512]{1,0:T(8,128)S(1)} %get-tuple-element.23), channel_id=1, source_target_pairs={{0,224},{32,0},{64,32},{96,64},{128,96},{160,128},{192,160},{224,1... | collective-permute-start | bytes 1179656 | tf_op jit(solution)/shard_map/beams_near/ppermute | solution.py:158
  15.7 0.0 collective-permute-start.2
  15.7 2.5 %collective-permute-start.3 = (f32[48,512]{1,0:T(8,128)S(1)}, f32[48,512]{1,0:T(8,128)S(1)}, u32[]{:S(2)}, u32[]{:S(2)}) collective-permute-start(f32[48,512]{1,0:T(8,128)S(1)} %get-tuple-element.25), channel_id=1, source_target_pairs={{0,192},{32,224},{64,0},{96,32},{128,64},{160,96},{192,128},{224,1... | collective-permute-start | bytes 294920 | tf_op jit(solution)/shard_map/beams_near/ppermute | solution.py:158
  18.1 0.5 collective-permute-start.4
  18.6 0.0 copy-done.1
  18.6 0.0 copy-done.2
  18.6 0.0 copy-done
  18.6 1.5 %fir_rest.1 = (f32[288,512]{1,0:T(8,128)S(1)}, f32[96,128]{1,0:T(8,128)S(1)}, f32[1,128]{1,0:T(1,128)S(1)}) custom-call(s32[1]{0:T(128)} %bitcast.refs_0_.group_ref, bf16[16,256]{1,0:T(8,128)(2,1)S(1)} %collective-permute-done.refs_1_, bf16[768,256]{1,0:T(8,128)(2,1)S(1)} %copy-done.1, bf16[16,256,512]{2,1,0:T(8,128)(2,1)S(1)} %copy-done, f32[768]{0:T(1024)S(1)} %copy-done.2), custom_call_target="tpu_custom_call" | custom-call | flops 1207959552 | bytes 6291456 | tf_op jit(solution)/shard_map/fir_rest/pallas_call | solution.py:140
  20.1 8.0 %collective-permute-done.3.far_down_ref = f32[48,512]{1,0:T(8,128)S(1)} collective-permute-done((f32[48,512]{1,0:T(8,128)S(1)}, f32[48,512]{1,0:T(8,128)S(1)}, u32[]{:S(2)}, u32[]{:S(2)}) %collective-permute-start.3) | collective-permute-done | bytes 98336 | tf_op jit(solution)/shard_map/beams_near/ppermute | solution.py:158
  28.1 1.9 %collective-permute-done.4.far_up_ref = f32[48,512]{1,0:T(8,128)S(1)} collective-permute-done((f32[48,512]{1,0:T(8,128)S(1)}, f32[48,512]{1,0:T(8,128)S(1)}, u32[]{:S(2)}, u32[]{:S(2)}) %collective-permute-start.4) | collective-permute-done | bytes 98336 | tf_op jit(solution)/shard_map/beams_near/ppermute | solution.py:158
  30.0 0.0 collective-permute-done.1.down_ref
  30.0 0.4 collective-permute-done.2.up_ref
  30.5 0.1 relay_sums.1
  30.5 2.3 %collective-permute-start.5 = (f32[96,512]{1,0:T(8,128)S(1)}, f32[96,512]{1,0:T(8,128)S(1)}, u32[]{:S(2)}, u32[]{:S(2)}) collective-permute-start(f32[96,512]{1,0:T(8,128)S(1)} %get-tuple-element.27), channel_id=1, source_target_pairs={{0,192},{32,224},{64,0},{96,32},{128,64},{160,96},{192,128},{224,1... | collective-permute-start | bytes 589832 | tf_op jit(solution)/shard_map/beams_far/ppermute | solution.py:158
  32.9 0.7 collective-permute-start.6
  33.5 6.9 %collective-permute-done.5.low_ref = f32[96,512]{1,0:T(8,128)S(1)} collective-permute-done((f32[96,512]{1,0:T(8,128)S(1)}, f32[96,512]{1,0:T(8,128)S(1)}, u32[]{:S(2)}, u32[]{:S(2)}) %collective-permute-start.5) | collective-permute-done | bytes 196640 | tf_op jit(solution)/shard_map/beams_far/ppermute | solution.py:158
  40.4 3.8 %collective-permute-done.6.high_ref = f32[96,512]{1,0:T(8,128)S(1)} collective-permute-done((f32[96,512]{1,0:T(8,128)S(1)}, f32[96,512]{1,0:T(8,128)S(1)}, u32[]{:S(2)}, u32[]{:S(2)}) %collective-permute-start.6) | collective-permute-done | bytes 196640 | tf_op jit(solution)/shard_map/beams_far/ppermute | solution.py:158
  44.2 0.8 packed_gram.1
  45.0 19.7 %all_to_all.20.p_ref = f32[8,144,128]{2,1,0:T(8,128)S(1)} all-to-all(f32[8,144,128]{2,1,0:T(8,128)S(1)} %bitcast.2), channel_id=1, replica_groups=mesh['elem'=8,'tm'=32] {'elem'}, dimensions={0} | all-to-all | bytes 1179648 | tf_op jit(solution)/shard_map/gram_sum/all_to_all | solution.py:580
  64.7 0.1 spread_share.1
  64.8 0.5 collective-permute-start.10
  65.2 0.7 collective-permute-start.9
  66.0 1.8 %collective-permute-start.8 = (f32[96,512]{1,0:T(8,128)S(1)}, f32[96,512]{1,0:T(8,128)S(1)}, u32[]{:S(2)}, u32[]{:S(2)}) collective-permute-start(f32[96,512]{1,0:T(8,128)S(1)} %get-tuple-element.33.refs_0_), channel_id=1, source_target_pairs={{0,64},{32,96},{64,128},{96,160},{128,192},{160,224},{192,0},{224,... | collective-permute-start | bytes 589832 | tf_op jit(solution)/shard_map/beams_gather/ppermute | solution.py:158
  67.8 2.0 %collective-permute-start.7 = (f32[96,512]{1,0:T(8,128)S(1)}, f32[96,512]{1,0:T(8,128)S(1)}, u32[]{:S(2)}, u32[]{:S(2)}) collective-permute-start(f32[96,512]{1,0:T(8,128)S(1)} %get-tuple-element.33.refs_0_), channel_id=1, source_target_pairs={{0,32},{32,64},{64,96},{96,128},{128,160},{160,192},{192,224},{224... | collective-permute-start | bytes 589832 | tf_op jit(solution)/shard_map/beams_gather/ppermute | solution.py:158
  69.8 13.6 %all_to_all.21.r_ref = f32[32,5,128]{2,1,0:T(8,128)S(1)} all-to-all(f32[32,5,128]{2,1,0:T(8,128)S(1)} %get-tuple-element.32), channel_id=1, replica_groups=mesh['elem'=8,'tm'=32] {'tm'}, dimensions={0} | all-to-all | bytes 163840 | tf_op jit(solution)/shard_map/blocks_out/all_to_all | solution.py:588
  83.4 0.0 collective-permute-done.10.from_above2.refs_4_
  83.4 0.0 collective-permute-done.9.from_above.refs_3_
  83.4 0.0 collective-permute-done.8.from_below2.refs_2_
  83.4 0.0 collective-permute-done.7.from_below.refs_1_
  83.5 0.5 decayed_sums.1
  84.0 1.7 %collective-permute-start.11 = (f32[144,512]{1,0:T(8,128)S(1)}, f32[144,512]{1,0:T(8,128)S(1)}, u32[]{:S(2)}, u32[]{:S(2)}) collective-permute-start(f32[144,512]{1,0:T(8,128)S(1)} %get-tuple-element.35), channel_id=1, source_target_pairs={{0,192},{32,224},{64,0},{96,32},{128,64},{160,96},{192,128},{224,1... | collective-permute-start | bytes 884744 | tf_op jit(solution)/shard_map/beams_gather/ppermute | solution.py:158
  85.7 1.3 collective-permute-start.12
  87.0 11.3 %all_to_all.22.r_ref = f32[32,5,128]{2,1,0:T(8,128)S(1)} all-to-all(f32[32,5,128]{2,1,0:T(8,128)S(1)} %get-tuple-element.34), channel_id=1, replica_groups=mesh['elem'=8,'tm'=32] {'tm'}, dimensions={0} | all-to-all | bytes 163840 | tf_op jit(solution)/shard_map/blocks_back/all_to_all | solution.py:593
  98.3 2.1 %collective-permute-done.11.low_ref.refs_5_ = f32[144,512]{1,0:T(8,128)S(1)} collective-permute-done((f32[144,512]{1,0:T(8,128)S(1)}, f32[144,512]{1,0:T(8,128)S(1)}, u32[]{:S(2)}, u32[]{:S(2)}) %collective-permute-start.11) | collective-permute-done | bytes 294944 | tf_op jit(solution)/shard_map/beams_gather/ppermute | solution.py:158
  100.4 1.7 %collective-permute-done.12.high_ref.refs_6_ = f32[144,512]{1,0:T(8,128)S(1)} collective-permute-done((f32[144,512]{1,0:T(8,128)S(1)}, f32[144,512]{1,0:T(8,128)S(1)}, u32[]{:S(2)}, u32[]{:S(2)}) %collective-permute-start.12) | collective-permute-done | bytes 294944 | tf_op jit(solution)/shard_map/beams_gather/ppermute | solution.py:158
  102.1 0.2 replicated.1
  102.3 22.2 %all_to_all.23.p_ref = f32[8,144,128]{2,1,0:T(8,128)S(1)} all-to-all(f32[8,144,128]{2,1,0:T(8,128)S(1)} %replicated.1), channel_id=1, replica_groups=mesh['elem'=8,'tm'=32] {'elem'}, dimensions={0} | all-to-all | bytes 1179648 | tf_op jit(solution)/shard_map/gram_gather/all_to_all | solution.py:595
  124.5 15.8 %whitened_rows.1 = f32[64,768]{1,0:T(8,128)} custom-call(s32[1]{0:T(128)} %bitcast.refs_0_.group_ref, f32[8,144,128]{2,1,0:T(8,128)S(1)} %all_to_all.23.p_ref, f32[96,512]{1,0:T(8,128)S(1)} %get-tuple-element.33.refs_0_, f32[96,512]{1,0:T(8,128)S(1)} %collective-permute-done.7.from_below.refs_1_, f32[96,512]{1,0:T(8,128)S(1)} %collective-permute-done.8.from_below2.refs_2_, ...), custom_call_target="tpu_custom_call" | custom-call | flops 1610612736 | bytes 1048576 | tf_op jit(solution)/shard_map/whitened_rows/pallas_call | solution.py:542
Async XLA Ops:
  0.0 18.6 %copy-start.1 = (bf16[768,256]{1,0:T(8,128)(2,1)S(1)}, bf16[768,256]{1,0:T(8,128)(2,1)}, u32[]{:S(2)}) copy-start(bf16[768,256]{1,0:T(8,128)(2,1)} %refs_2_.3) | copy-start | bytes 1179652
  0.0 18.6 %copy-start.2 = (f32[768]{0:T(1024)S(1)}, f32[768]{0:T(1024)}, u32[]{:S(2)}) copy-start(f32[768]{0:T(1024)} %refs_4_.1) | copy-start | bytes 9220
  0.8 5.0 %collective-permute-start = (bf16[16,256]{1,0:T(8,128)(2,1)S(1)}, bf16[16,256]{1,0:T(8,128)(2,1)S(1)}, u32[]{:S(2)}, u32[]{:S(2)}) collective-permute-start(bf16[16,256]{1,0:T(8,128)(2,1)S(1)} %slice.3), channel_id=1, source_target_pairs={{0,1},{1,2},{2,3},{3,4},{4,5},{5,6},{6,7},{7,8},{8,9},{9,10},{10,1... | collective-permute-start | bytes 24584 | tf_op jit(solution)/shard_map/halo/ppermute | solution.py:18
  2.7 15.9 %copy-start = (bf16[16,256,512]{2,1,0:T(8,128)(2,1)S(1)}, bf16[16,256,512]{2,1,0:T(8,128)(2,1)}, u32[]{:S(2)}) copy-start(bf16[16,256,512]{2,1,0:T(8,128)(2,1)} %refs_3_.3) | copy-start | bytes 12582916
  9.7 20.3 %collective-permute-start.1 = (f32[192,512]{1,0:T(8,128)S(1)}, f32[192,512]{1,0:T(8,128)S(1)}, u32[]{:S(2)}, u32[]{:S(2)}) collective-permute-start(f32[192,512]{1,0:T(8,128)S(1)} %get-tuple-element.23), channel_id=1, source_target_pairs={{0,224},{32,0},{64,32},{96,64},{128,96},{160,128},{192,160},{224,1... | collective-permute-start | bytes 1179656 | tf_op jit(solution)/shard_map/beams_near/ppermute | solution.py:158
  15.7 14.8 %collective-permute-start.2 = (f32[192,512]{1,0:T(8,128)S(1)}, f32[192,512]{1,0:T(8,128)S(1)}, u32[]{:S(2)}, u32[]{:S(2)}) collective-permute-start(f32[192,512]{1,0:T(8,128)S(1)} %get-tuple-element.24), channel_id=1, source_target_pairs={{0,32},{32,64},{64,96},{96,128},{128,160},{160,192},{192,224},{224... | collective-permute-start | bytes 1179656 | tf_op jit(solution)/shard_map/beams_near/ppermute | solution.py:158
  15.7 12.4 %collective-permute-start.3 = (f32[48,512]{1,0:T(8,128)S(1)}, f32[48,512]{1,0:T(8,128)S(1)}, u32[]{:S(2)}, u32[]{:S(2)}) collective-permute-start(f32[48,512]{1,0:T(8,128)S(1)} %get-tuple-element.25), channel_id=1, source_target_pairs={{0,192},{32,224},{64,0},{96,32},{128,64},{160,96},{192,128},{224,1... | collective-permute-start | bytes 294920 | tf_op jit(solution)/shard_map/beams_near/ppermute | solution.py:158
  18.1 11.9 %collective-permute-start.4 = (f32[48,512]{1,0:T(8,128)S(1)}, f32[48,512]{1,0:T(8,128)S(1)}, u32[]{:S(2)}, u32[]{:S(2)}) collective-permute-start(f32[48,512]{1,0:T(8,128)S(1)} %get-tuple-element.26), channel_id=1, source_target_pairs={{0,64},{32,96},{64,128},{96,160},{128,192},{160,224},{192,0},{224,... | collective-permute-start | bytes 294920 | tf_op jit(solution)/shard_map/beams_near/ppermute | solution.py:158
  30.5 9.9 %collective-permute-start.5 = (f32[96,512]{1,0:T(8,128)S(1)}, f32[96,512]{1,0:T(8,128)S(1)}, u32[]{:S(2)}, u32[]{:S(2)}) collective-permute-start(f32[96,512]{1,0:T(8,128)S(1)} %get-tuple-element.27), channel_id=1, source_target_pairs={{0,192},{32,224},{64,0},{96,32},{128,64},{160,96},{192,128},{224,1... | collective-permute-start | bytes 589832 | tf_op jit(solution)/shard_map/beams_far/ppermute | solution.py:158
  32.9 11.3 %collective-permute-start.6 = (f32[96,512]{1,0:T(8,128)S(1)}, f32[96,512]{1,0:T(8,128)S(1)}, u32[]{:S(2)}, u32[]{:S(2)}) collective-permute-start(f32[96,512]{1,0:T(8,128)S(1)} %get-tuple-element.28), channel_id=1, source_target_pairs={{0,64},{32,96},{64,128},{96,160},{128,192},{160,224},{192,0},{224,... | collective-permute-start | bytes 589832 | tf_op jit(solution)/shard_map/beams_far/ppermute | solution.py:158
  64.8 18.7 %collective-permute-start.10 = (f32[96,512]{1,0:T(8,128)S(1)}, f32[96,512]{1,0:T(8,128)S(1)}, u32[]{:S(2)}, u32[]{:S(2)}) collective-permute-start(f32[96,512]{1,0:T(8,128)S(1)} %get-tuple-element.33.refs_0_), channel_id=1, source_target_pairs={{0,192},{32,224},{64,0},{96,32},{128,64},{160,96},{192,128},{224,1... | collective-permute-start | bytes 589832 | tf_op jit(solution)/shard_map/beams_gather/ppermute | solution.py:158
  65.2 18.2 %collective-permute-start.9 = (f32[96,512]{1,0:T(8,128)S(1)}, f32[96,512]{1,0:T(8,128)S(1)}, u32[]{:S(2)}, u32[]{:S(2)}) collective-permute-start(f32[96,512]{1,0:T(8,128)S(1)} %get-tuple-element.33.refs_0_), channel_id=1, source_target_pairs={{0,224},{32,0},{64,32},{96,64},{128,96},{160,128},{192,160},{224,1... | collective-permute-start | bytes 589832 | tf_op jit(solution)/shard_map/beams_gather/ppermute | solution.py:158
  66.0 17.5 %collective-permute-start.8 = (f32[96,512]{1,0:T(8,128)S(1)}, f32[96,512]{1,0:T(8,128)S(1)}, u32[]{:S(2)}, u32[]{:S(2)}) collective-permute-start(f32[96,512]{1,0:T(8,128)S(1)} %get-tuple-element.33.refs_0_), channel_id=1, source_target_pairs={{0,64},{32,96},{64,128},{96,160},{128,192},{160,224},{192,0},{224,... | collective-permute-start | bytes 589832 | tf_op jit(solution)/shard_map/beams_gather/ppermute | solution.py:158
  67.8 15.7 %collective-permute-start.7 = (f32[96,512]{1,0:T(8,128)S(1)}, f32[96,512]{1,0:T(8,128)S(1)}, u32[]{:S(2)}, u32[]{:S(2)}) collective-permute-start(f32[96,512]{1,0:T(8,128)S(1)} %get-tuple-element.33.refs_0_), channel_id=1, source_target_pairs={{0,32},{32,64},{64,96},{96,128},{128,160},{160,192},{192,224},{224... | collective-permute-start | bytes 589832 | tf_op jit(solution)/shard_map/beams_gather/ppermute | solution.py:158
  84.0 16.4 %collective-permute-start.11 = (f32[144,512]{1,0:T(8,128)S(1)}, f32[144,512]{1,0:T(8,128)S(1)}, u32[]{:S(2)}, u32[]{:S(2)}) collective-permute-start(f32[144,512]{1,0:T(8,128)S(1)} %get-tuple-element.35), channel_id=1, source_target_pairs={{0,192},{32,224},{64,0},{96,32},{128,64},{160,96},{192,128},{224,1... | collective-permute-start | bytes 884744 | tf_op jit(solution)/shard_map/beams_gather/ppermute | solution.py:158
  85.7 16.4 %collective-permute-start.12 = (f32[144,512]{1,0:T(8,128)S(1)}, f32[144,512]{1,0:T(8,128)S(1)}, u32[]{:S(2)}, u32[]{:S(2)}) collective-permute-start(f32[144,512]{1,0:T(8,128)S(1)} %get-tuple-element.36), channel_id=1, source_target_pairs={{0,64},{32,96},{64,128},{96,160},{128,192},{160,224},{192,0},{224,... | collective-permute-start | bytes 884744 | tf_op jit(solution)/shard_map/beams_gather/ppermute | solution.py:158
